TPU v7x, 32 devices: a whole 2x2x4 slice. The times are simulated.
32 devices in a mesh: batch: 4 (over y, x), proto: 8 (over z, core).
Axes of the slice: x: 2, y: 2, z: 4, core: 2. Of those that a mesh axis runs over, the one named last changes fastest.
Arguments:
- teacher_emb: bfloat16 [256, 2048], P('proto', 'batch'), may hold values from -22 to 22
- student_emb: bfloat16 [256, 2048], P('proto', 'batch'), may hold values from -6 to 6
- prototypes: bfloat16 [256, 65536], P('batch', 'proto'), may hold values from -16 to 16
Outputs:
- grad_proto: float32 [256, 65536], P('batch', 'proto')
- grad_student: float32 [256, 2048], P('proto', 'batch')
- loss: float32 [], replicated
All inputs are finite; a program needn't handle non-finite values.
Results may differ from a plain program's by a relative error of at most 0.00055.
The roundings to bfloat16 on the way count: a program that leaves them out, or rounds other values in their place, can miss the bound.
Values may be sent and summed in bfloat16 or wider, within the bound.
No kernel may reach another device: no remote copies, remote signals or barrier semaphores. Data moves between devices by JAX's collectives and lax.ppermute only.
A program may use at most 128 MiB of HBM per device.

v0:
```python
import jax
import jax.numpy as jnp
from jax import lax
from jax.sharding import PartitionSpec as P

ITERS = 3


teacher_temp = 0.07
student_temp = 0.1
epsilon = 1e-06


def unit(matrix):
    values = matrix.astype(jnp.float32)
    factor = lax.rsqrt(jnp.sum(values * values, axis=0, keepdims=True) + epsilon)
    return ((values * factor).astype(jnp.bfloat16), factor)


def cosine(left, right):
    return lax.dot_general(
        left, right, (((0,), (0,)), ((), ())), preferred_element_type=jnp.float32
    )


def shards(teacher_emb, student_emb, prototypes):
    teacher_full, student_full = (
        lax.all_gather(teacher_emb, "proto", axis=0, tiled=True),
        lax.all_gather(student_emb, "proto", axis=0, tiled=True),
    )
    proto_full = lax.all_gather(prototypes, "batch", axis=0, tiled=True)
    proto_unit, proto_scale = unit(proto_full)
    teacher_unit, unused = unit(teacher_full)
    student_unit, student_scale = unit(student_full)
    width = proto_full.shape[0]
    local_rows = teacher_full.shape[1]
    total_rows = local_rows * lax.axis_size("batch")
    expo = jnp.exp(cosine(teacher_unit, proto_unit) / teacher_temp)
    targets = expo
    for iteration in range(ITERS):
        column_total = lax.psum(jnp.sum(targets, axis=0), "batch")
        targets = targets / column_total[None, :]
        row_total = lax.psum(jnp.sum(targets, axis=1), "proto")
        targets = targets / row_total[:, None]
    cos_student = cosine(student_unit, proto_unit)
    logits = cos_student / student_temp
    partial_total = jnp.sum(jnp.exp(logits), axis=1)
    softmax_total = lax.psum(partial_total, "proto")
    logp = logits - jnp.log(softmax_total)[:, None]
    loss_part = -jnp.sum(targets * logp)
    loss = lax.psum(loss_part, ("batch", "proto")) / total_rows
    grad_logit = ((jnp.exp(logp) - targets) / (total_rows * student_temp)).astype(jnp.bfloat16)
    proto_rows = width // lax.axis_size("batch")
    crop_rows = width // lax.axis_size("proto")
    proto_start = lax.axis_index("batch") * proto_rows
    crop_start = lax.axis_index("proto") * crop_rows
    proto_own = lax.dynamic_slice_in_dim(proto_unit, proto_start, proto_rows, 0).astype(jnp.float32)
    student_own = lax.dynamic_slice_in_dim(student_unit, crop_start, crop_rows, 0).astype(
        jnp.float32
    )
    rows = student_unit
    proto_part = lax.psum_scatter(
        jnp.dot(rows, grad_logit, preferred_element_type=jnp.float32),
        "batch",
        scatter_dimension=0,
        tiled=True,
    )
    rows = proto_unit
    crop_part = lax.psum_scatter(
        lax.dot_general(
            rows, grad_logit, (((1,), (1,)), ((), ())), preferred_element_type=jnp.float32
        ),
        "proto",
        scatter_dimension=0,
        tiled=True,
    )
    proto_dot = lax.psum(jnp.sum(proto_own * proto_part, axis=0), "batch")
    crop_dot = lax.psum(jnp.sum(student_own * crop_part, axis=0), "proto")
    grad_proto = (proto_part - proto_own * proto_dot[None, :]) * proto_scale
    grad_student = (crop_part - student_own * crop_dot[None, :]) * student_scale
    return (grad_proto, grad_student, loss)


def solution(mesh):
    in_specs = (P("proto", "batch"), P("proto", "batch"), P("batch", "proto"))
    out_specs = (P("batch", "proto"), P("proto", "batch"), P())
    return jax.shard_map(shards, mesh=mesh, in_specs=in_specs, out_specs=out_specs, check_vma=False)
```

profile of v0, /device:TPU:0, one launch (start us, length us, event | category | flops | bytes accessed | tf_op | source)
XLA Modules:
  0.0 381.8 jit_solution(16406410473220215280)
XLA Ops:
  7.9 16.1 %all_gather.11 = bf16[256,512]{1,0:T(8,128)(2,1)S(1)} all-gather(bf16[32,512]{1,0:T(8,128)(2,1)} %param.3), channel_id=1, replica_groups=mesh['batch'=4,'proto'=8] {'proto'}, dimensions={0}, use_global_device_ids=true | all-gather | bytes 294912 | tf_op jit(solution)/shard_map/all_gather | solution.py:28
  24.1 14.4 %all_gather.9 = bf16[256,512]{1,0:T(8,128)(2,1)S(1)} all-gather(bf16[32,512]{1,0:T(8,128)(2,1)} %param.4), channel_id=1, replica_groups=mesh['batch'=4,'proto'=8] {'proto'}, dimensions={0}, use_global_device_ids=true | all-gather | bytes 294912 | tf_op jit(solution)/shard_map/all_gather | solution.py:29
  38.7 26.5 %all-gather.2.cloned.1.call-done = bf16[256,8192]{1,0:T(8,128)(2,1)} async-done(((bf16[64,8192]{1,0:T(8,128)(2,1)}), bf16[256,8192]{1,0:T(8,128)(2,1)}) %all-gather.2.cloned.1.call-update) | async-done | bytes 4194320 | tf_op jit(solution)/shard_map/all_gather | solution.py:31
  68.2 3.3 fusion.12
  73.6 7.2 %fusion.25 = (f32[8192]{0:T(1024)S(1)}, f32[512,8192]{1,0:T(8,128)}) fusion(bf16[256,8192]{1,0:T(8,128)(2,1)S(1)} %fusion.12, bf16[256,512]{1,0:T(8,128)(2,1)S(1)} %all_gather.11, f32[512]{0:T(512)S(1)} %add_rsqrt_fusion.1), kind=kOutput, calls=%fused_computation.44 | convolution fusion | flops 2156257280 | bytes 21268480 | tf_op jit(solution)/shard_map/dot_general | solution.py:21
  80.9 15.4 %psum.71 = f32[8192]{0:T(1024)S(1)} all-reduce(f32[8192]{0:T(1024)S(1)} %get-tuple-element.9), channel_id=1, replica_groups=mesh['batch'=4,'proto'=8] {'batch'}, use_global_device_ids=true, to_apply=%region_6.0 | all-reduce | flops 8192 | bytes 65536 | tf_op jit(solution)/shard_map/psum | solution.py:41
  96.3 7.0 %divide_reduce_fusion = f32[512]{0:T(512)S(1)} fusion(f32[512,8192]{1,0:T(8,128)} %get-tuple-element.10, f32[8192]{0:T(1024)S(1)} %psum.71), kind=kLoop, calls=%fused_computation.13 | loop fusion | flops 8388096 | bytes 16812032 | tf_op jit(solution)/shard_map/reduce_sum | solution.py:43
  103.3 13.6 %psum.72 = f32[512]{0:T(512)S(1)} all-reduce(f32[512]{0:T(512)S(1)} %divide_reduce_fusion), channel_id=1, replica_groups=mesh['batch'=4,'proto'=8] {'proto'}, use_global_device_ids=true, to_apply=%region_8.0 | all-reduce | flops 512 | bytes 4096 | tf_op jit(solution)/shard_map/psum | solution.py:43
  116.9 8.4 %fusion.7 = f32[8192]{0:T(1024)S(1)} fusion(f32[512,8192]{1,0:T(8,128)} %get-tuple-element.10, f32[512]{0:T(512)S(1)} %psum.72, f32[8192]{0:T(1024)S(1)} %psum.71), kind=kLoop, calls=%fused_computation.14 | loop fusion | flops 12574720 | bytes 16844800 | tf_op jit(solution)/shard_map/reduce_sum | solution.py:41
  125.3 15.1 %psum.73 = f32[8192]{0:T(1024)S(1)} all-reduce(f32[8192]{0:T(1024)S(1)} %fusion.7), channel_id=1, replica_groups=mesh['batch'=4,'proto'=8] {'batch'}, use_global_device_ids=true, to_apply=%region_10.0 | all-reduce | flops 8192 | bytes 65536 | tf_op jit(solution)/shard_map/psum | solution.py:41
  140.4 8.7 %fusion.8 = f32[512]{0:T(512)S(1)} fusion(f32[512,8192]{1,0:T(8,128)} %get-tuple-element.10, f32[8192]{0:T(1024)S(1)} %psum.73, f32[512]{0:T(512)S(1)} %psum.72, f32[8192]{0:T(1024)S(1)} %psum.71), kind=kLoop, calls=%fused_computation.15 | loop fusion | flops 16776704 | bytes 16846848 | tf_op jit(solution)/shard_map/reduce_sum | solution.py:43
  149.1 13.6 %psum.74 = f32[512]{0:T(512)S(1)} all-reduce(f32[512]{0:T(512)S(1)} %fusion.8), channel_id=1, replica_groups=mesh['batch'=4,'proto'=8] {'proto'}, use_global_device_ids=true, to_apply=%region_12.0 | all-reduce | flops 512 | bytes 4096 | tf_op jit(solution)/shard_map/psum | solution.py:43
  162.7 7.8 %fusion.9 = f32[8192]{0:T(1024)S(1)} fusion(f32[512,8192]{1,0:T(8,128)} %get-tuple-element.10, f32[512]{0:T(512)S(1)} %psum.74, f32[8192]{0:T(1024)S(1)} %psum.73, f32[512]{0:T(512)S(1)} %psum.72, f32[8192]{0:T(1024)S(1)} %psum.71), kind=kLoop, calls=%fused_computation.16 | loop fusion | flops 20963328 | bytes 16879616 | tf_op jit(solution)/shard_map/reduce_sum | solution.py:41
  170.5 15.3 %psum.75 = f32[8192]{0:T(1024)S(1)} all-reduce(f32[8192]{0:T(1024)S(1)} %fusion.9), channel_id=1, replica_groups=mesh['batch'=4,'proto'=8] {'batch'}, use_global_device_ids=true, to_apply=%region_14.0 | all-reduce | flops 8192 | bytes 65536 | tf_op jit(solution)/shard_map/psum | solution.py:41
  185.9 8.4 %fusion.10 = f32[512]{0:T(512)S(1)} fusion(f32[512,8192]{1,0:T(8,128)} %get-tuple-element.10, f32[8192]{0:T(1024)S(1)} %psum.75, f32[512]{0:T(512)S(1)} %psum.74, f32[8192]{0:T(1024)S(1)} %psum.73, f32[512]{0:T(512)S(1)} %psum.72, f32[8192]{0:T(1024)S(1)} %psum.71), kind=kLoop, calls=%fused_computation.17 | loop fusion | flops 25165312 | bytes 16881664 | tf_op jit(solution)/shard_map/reduce_sum | solution.py:43
  194.3 7.2 %exponential_reduce_fusion = (f32[512]{0:T(512)S(1)}, f32[512,8192]{1,0:T(8,128)}) fusion(bf16[256,512]{1,0:T(8,128)(2,1)S(1)} %fusion.17, bf16[256,8192]{1,0:T(8,128)(2,1)S(1)} %copy-done.1), kind=kOutput, calls=%fused_computation.12 | convolution fusion | flops 2155871744 | bytes 21235712 | tf_op jit(solution)/shard_map/dot_general | solution.py:21
  201.5 13.8 %all-reduce = (f32[512]{0:T(512)S(1)}, f32[512]{0:T(512)S(1)}) all-reduce(f32[512]{0:T(512)S(1)} %get-tuple-element.7, f32[512]{0:T(512)S(1)} %fusion.10), channel_id=1, replica_groups=mesh['batch'=4,'proto'=8] {'proto'}, use_global_device_ids=true, to_apply=%region_3.0 | all-reduce | flops 1024 | bytes 8192 | tf_op jit(solution)/shard_map/psum | solution.py:48
  215.3 15.3 %multiply_reduce_fusion = (f32[]{:T(128)}, bf16[512,8192]{1,0:T(8,128)(2,1)S(1)}) fusion(f32[512,8192]{1,0:T(8,128)} %get-tuple-element.8, f32[512]{0:T(512)S(1)} %log.3, f32[512,8192]{1,0:T(8,128)} %get-tuple-element.10, f32[512]{0:T(512)S(1)} %get-tuple-element.4, f32[8192]{0:T(1024)S(1)} %psum.75, f32[512]{0:T(512)S(1)} %psum.74, f32[8192]{0:T(1024)S(1)} %psum.73, ...), kind=kLoop, calls=%fused_computation.9 | loop fusion | flops 54525952 | bytes 42049540 | tf_op jit(solution)/shard_map/reduce_sum | solution.py:50
  237.0 9.0 %fusion.26 = f32[256,8192]{1,0:T(8,128)} fusion(bf16[256,512]{1,0:T(8,128)(2,1)S(1)} %fusion.17, bf16[512,8192]{1,0:T(8,128)(2,1)} %copy-done.3), kind=kOutput, calls=%fused_computation.45 | convolution fusion | flops 2147483648 | bytes 17039360 | tf_op jit(solution)/shard_map/dot_general | solution.py:63
  246.7 37.5 %psum.79 = f32[]{:T(128)} all-reduce(f32[]{:T(128)S(6)} %neg.3), channel_id=1, replica_groups=mesh['batch'=4,'proto'=8] {'batch','proto'}, use_global_device_ids=true, to_apply=%region_24.0 | all-reduce | flops 1 | bytes 8 | tf_op jit(solution)/shard_map/psum | solution.py:51
  285.8 15.5 %psum.78 = f32[512]{0:T(512)S(1)} all-reduce(f32[512]{0:T(512)S(1)} %fusion.22), channel_id=1, replica_groups=mesh['batch'=4,'proto'=8] {'proto'}, use_global_device_ids=true, to_apply=%region_22.0 | all-reduce | flops 512 | bytes 4096 | tf_op jit(solution)/shard_map/psum | solution.py:78
  302.7 50.4 %reduce-scatter.3.cloned.1.call-done = f32[64,8192]{1,0:T(8,128)} async-done(((f32[256,8192]{1,0:T(8,128)}), f32[64,8192]{1,0:T(8,128)}) %reduce-scatter.3.cloned.1.call-update) | async-done | bytes 2097168 | tf_op jit(solution)/shard_map/reduce_scatter | solution.py:62
  355.2 15.4 %psum.77 = f32[8192]{0:T(1024)S(1)} all-reduce(f32[8192]{0:T(1024)S(1)} %fusion.13), channel_id=1, replica_groups=mesh['batch'=4,'proto'=8] {'batch'}, use_global_device_ids=true, to_apply=%region_19.0 | all-reduce | flops 8192 | bytes 65536 | tf_op jit(solution)/shard_map/psum | solution.py:77
  370.6 3.5 fusion.15
  (27 shorter events, 17.1 us)
Async XLA Ops:
  7.2 58.0 %all-gather.2.cloned.1.call-start = ((), (), s32[]{:S(2)}) async-start(), calls=%async_computation.2 | async-start | bytes 5242880 | tf_op jit(solution)/shard_map/all_gather | solution.py:31
  7.9 277.0 %reduce-scatter.5.cloned.1.call-start = ((), (), s32[]{:S(2)}) async-start(), calls=%async_computation.4 | async-start | bytes 589824 | tf_op jit(solution)/shard_map/reduce_scatter | solution.py:69
  71.6 2.0 copy-start
  185.8 8.4 %copy-start.1 = (bf16[256,8192]{1,0:T(8,128)(2,1)S(1)}, bf16[256,8192]{1,0:T(8,128)(2,1)}, u32[]{:S(2)}) copy-start(bf16[256,8192]{1,0:T(8,128)(2,1)} %copy-done) | copy-start | bytes 12582916
  215.3 18.5 %copy-start.2 = (bf16[256,8192]{1,0:T(8,128)(2,1)S(1)}, bf16[256,8192]{1,0:T(8,128)(2,1)}, u32[]{:S(2)}) copy-start(bf16[256,8192]{1,0:T(8,128)(2,1)} %copy-done) | copy-start | bytes 12582916
  230.5 3.2 copy-start.3
  236.9 116.2 %reduce-scatter.3.cloned.1.call-start = ((), (), s32[]{:S(2)}) async-start(), calls=%async_computation.3 | async-start | bytes 10485760 | tf_op jit(solution)/shard_map/reduce_scatter | solution.py:62
Sparse Core Ops, SparseCore 0:
  9.8 55.2 all-gather.1
  237.0 27.9 reduce-scatter.4
  268.1 84.9 reduce-scatter.2
where the time goes:
time: 382 us
  blocking collectives  186 us (49%)
  waiting for transfers between devices  77.5 us (20%)
  other arithmetic  70.2 us (18%)
  matrix products  26.6 us (7%)
  between operations  16.3 us (4%)
  local copies, waits for them, and re-layouts  5.26 us (1%)
    reduce_scatter x1, waiting for transfers between devices, shards(): lax.psum_scatter(jnp.dot(rows, grad_logit, preferred_element_type=jnp.flo...  50.4 us
    psum x3, blocking collectives, shards(): column_total = lax.psum(jnp.sum(targets, axis=0), 'batch')  45.8 us
    psum x1, blocking collectives, shards(): loss = lax.psum(loss_part, ('batch', 'proto')) / total_rows  37.5 us
    psum x2, blocking collectives, shards(): row_total = lax.psum(jnp.sum(targets, axis=1), 'proto')  27.2 us
    all_gather x1, waiting for transfers between devices, shards(): proto_full = lax.all_gather(prototypes, 'batch', axis=0, tiled=True)  26.5 us
    reduce_sum x3, other arithmetic, shards(): row_total = lax.psum(jnp.sum(targets, axis=1), 'proto')  24.2 us
    reduce_sum x2, other arithmetic, shards(): column_total = lax.psum(jnp.sum(targets, axis=0), 'batch')  16.2 us
    all_gather x1, blocking collectives, shards(): lax.all_gather(teacher_emb, 'proto', axis=0, tiled=True)  16.1 us
  transfers between devices with their start and end apart: 3, of which 2 were waited for; matrix products, arithmetic and copies ran while one was open for 3% of the time, Pallas kernels for 0%

commit v1 on v0

v1 whole, which is shorter than its diff:
```python
import functools
import math

import jax
import jax.numpy as jnp
from jax import lax
from jax.experimental import pallas as pl
from jax.experimental.pallas import tpu as pltpu
from jax.sharding import PartitionSpec as P

ITERS = 3
CORES = 2
AXES = ("batch", "proto")

teacher_temp = 0.07
student_temp = 0.1
epsilon = 1e-06
LOG2E = 1.0 / math.log(2.0)
T_GAIN = LOG2E / teacher_temp
S_GAIN = LOG2E / student_temp

SMEM = pl.BlockSpec(memory_space=pltpu.SMEM)
VMEM = pl.BlockSpec(memory_space=pltpu.VMEM)


def whole(shape):
    return pl.BlockSpec(shape, lambda *grid: (0,) * len(shape))


def params(megabytes=48):
    return pltpu.CompilerParams(vmem_limit_bytes=megabytes << 20)


def swap(x, over_batch, over_z, over_core):
    batch, proto = lax.axis_size("batch"), lax.axis_size("proto")
    pairs = []
    for b in range(batch):
        for p in range(proto):
            other = p ^ (over_z * CORES + over_core)
            pairs.append((b * proto + p, (b ^ over_batch) * proto + other))
    return lax.ppermute(x, AXES, pairs)


def z_masks(nz):
    return [(2 << i) - 1 for i in range(nz.bit_length() - 1)]


def gather_crops(x):
    batch = lax.axis_size("batch")
    nz = lax.axis_size("proto") // CORES
    pieces = jnp.stack([x] + [swap(x, o, 0, 0) for o in range(1, batch)])
    found = []
    masks = z_masks(nz)
    for first, order in ((0, masks), (batch // 2, masks[::-1])):
        held = pieces[None, first : first + batch // 2]
        offsets = [0]
        for mask in order:
            held = jnp.concatenate([held, swap(held, 0, mask, 0)], axis=0)
            offsets = offsets + [o ^ mask for o in offsets]
        found.append((held, offsets, first, 0))
        found.append((swap(held, 0, 0, 1), offsets, first, 1))
    return found


def unit_crops_body(plan, at_ref, *refs):
    pieces, (unit_ref, scale_ref, raw) = refs[: len(plan)], refs[len(plan) :]
    j, z, c = at_ref[0], at_ref[1], at_ref[2]
    for ref, (offsets, first, core) in zip(pieces, plan):
        rows, cols = ref.shape[2:]
        for i, oz in enumerate(offsets):
            top = pl.multiple_of(((z ^ oz) * CORES + (c ^ core)) * rows, rows)
            for k in range(ref.shape[1]):
                left = pl.multiple_of((j ^ (first + k)) * cols, cols)
                raw[pl.ds(top, rows), pl.ds(left, cols)] = ref[i, k]
    step = ref.shape[3]
    for left in range(0, raw.shape[1], step):
        values = raw[:, left : left + step].astype(jnp.float32)
        factor = lax.rsqrt(jnp.sum(values * values, axis=0, keepdims=True) + epsilon)
        unit_ref[:, left : left + step] = (values * factor).astype(jnp.bfloat16)
        scale_ref[:, left : left + step] = factor


def unit_crops(at, found, width, crops):
    plan = [(offsets, first, core) for _, offsets, first, core in found]
    return pl.pallas_call(
        functools.partial(unit_crops_body, plan),
        out_shape=(
            jax.ShapeDtypeStruct((width, crops), jnp.bfloat16),
            jax.ShapeDtypeStruct((1, crops), jnp.float32),
        ),
        in_specs=[SMEM] + [VMEM] * len(found),
        out_specs=(VMEM, VMEM),
        scratch_shapes=[pltpu.VMEM((width, crops), jnp.bfloat16)],
        compiler_params=params(),
        name="unit_crops",
    )(at, *[piece for piece, *_ in found])


def unit_protos_body(at_ref, *refs):
    blocks, (unit_ref, turned_ref, scale_ref, raw) = refs[:-4], refs[-4:]
    j = at_ref[0]
    rows = blocks[0].shape[0]
    for o, ref in enumerate(blocks):
        top = pl.multiple_of((j ^ o) * rows, rows)
        raw[pl.ds(top, rows), :] = ref[...]
    values = raw[...].astype(jnp.float32)
    factor = lax.rsqrt(jnp.sum(values * values, axis=0, keepdims=True) + epsilon)
    unit = (values * factor).astype(jnp.bfloat16)
    unit_ref[...] = unit
    turned_ref[...] = unit.T
    scale_ref[...] = factor


def unit_protos(at, blocks):
    rows, protos = blocks[0].shape
    width = rows * len(blocks)
    step = min(512, protos)
    return pl.pallas_call(
        unit_protos_body,
        grid=(protos // step,),
        out_shape=(
            jax.ShapeDtypeStruct((width, protos), jnp.bfloat16),
            jax.ShapeDtypeStruct((protos, width), jnp.bfloat16),
            jax.ShapeDtypeStruct((1, protos), jnp.float32),
        ),
        in_specs=[SMEM] + [pl.BlockSpec((rows, step), lambda i: (0, i))] * len(blocks),
        out_specs=(
            pl.BlockSpec((width, step), lambda i: (0, i)),
            pl.BlockSpec((step, width), lambda i: (i, 0)),
            pl.BlockSpec((1, step), lambda i: (0, i)),
        ),
        scratch_shapes=[pltpu.VMEM((width, step), jnp.bfloat16)],
        compiler_params=params(),
        name="unit_protos",
    )(at, *blocks)


def scores(turned_ref, unit_ref):
    return jnp.dot(turned_ref[...], unit_ref[...], preferred_element_type=jnp.float32)


def add_rows(row_ref, values):
    total = jnp.sum(values, axis=0, keepdims=True)

    @pl.when(pl.program_id(0) == 0)
    def _():
        row_ref[...] = total

    @pl.when(pl.program_id(0) > 0)
    def _():
        row_ref[...] += total


def sinkhorn_body(turned_ref, teacher_ref, crop_ref, row_ref, inv_ref):
    mass = jnp.exp2(scores(turned_ref, teacher_ref) * T_GAIN) * crop_ref[...]
    inv = 1.0 / jnp.sum(mass, axis=1, keepdims=True)
    inv_ref[...] = inv
    add_rows(row_ref, mass * inv)


def first_body(turned_ref, teacher_ref, row_ref):
    mass = jnp.exp2(scores(turned_ref, teacher_ref) * T_GAIN)
    add_rows(row_ref, mass * (1.0 / jnp.sum(mass, axis=1, keepdims=True)))


def softmax_body(turned_ref, student_ref, row_ref):
    add_rows(row_ref, jnp.exp2(scores(turned_ref, student_ref) * S_GAIN))


def sweep(body, name, turned, *rest, inverse=False):
    protos, width = turned.shape
    step = min(256, protos)
    crops = rest[0].shape[1]
    row = jax.ShapeDtypeStruct((1, crops), jnp.float32)
    inv = jax.ShapeDtypeStruct((protos, 1), jnp.float32)
    return pl.pallas_call(
        body,
        grid=(protos // step,),
        out_shape=(row, inv) if inverse else row,
        in_specs=[pl.BlockSpec((step, width), lambda i: (i, 0))] + [whole(x.shape) for x in rest],
        out_specs=(whole((1, crops)), pl.BlockSpec((step, 1), lambda i: (i, 0)))
        if inverse
        else whole((1, crops)),
        compiler_params=params(),
        name=name,
    )(turned, *rest)


def grads_body(
    plan,
    grain,
    at_ref,
    turned_ref,
    protos_ref,
    inv_ref,
    proto_scale_ref,
    teacher_ref,
    student_ref,
    crop_ref,
    total_ref,
    crop_scale_ref,
    proto_out,
    crop_out,
    loss_ref,
    crop_sum,
    loss_sum,
):
    nb, nz, rows, cols = plan
    j, z, c = at_ref[0], at_ref[1], at_ref[2]
    first = pl.program_id(0) == 0
    log_total = jnp.log(total_ref[...])
    targets = jnp.exp2(scores(turned_ref, teacher_ref) * T_GAIN) * crop_ref[...] * inv_ref[...]
    logp = scores(turned_ref, student_ref) * (1.0 / student_temp) - log_total
    grad = ((jnp.exp(logp) - targets) * (1.0 / grain)).astype(jnp.bfloat16)
    add_rows(loss_sum, targets * logp)
    protos = protos_ref[...]
    by_proto = lax.dot_general(
        student_ref[...], grad, (((1,), (1,)), ((), ())), preferred_element_type=jnp.float32
    )
    values = protos.astype(jnp.float32)
    radial = jnp.sum(values * by_proto, axis=0, keepdims=True)
    result = (by_proto - values * radial) * proto_scale_ref[...]
    wide = result.shape[0] // nb
    for o in range(nb):
        for source in range(nb):
            @pl.when((j ^ o) == source)
            def _(o=o, source=source):
                proto_out[o] = result[source * wide : (source + 1) * wide, :]
    part = jnp.dot(protos, grad, preferred_element_type=jnp.float32)

    @pl.when(first)
    def _():
        crop_sum[...] = part

    @pl.when(jnp.logical_not(first))
    def _():
        crop_sum[...] += part

    @pl.when(pl.program_id(0) == pl.num_programs(0) - 1)
    def _():
        loss_ref[...] = jnp.sum(loss_sum[...], axis=1, keepdims=True)
        student = student_ref[...].astype(jnp.float32)
        total = crop_sum[...]
        dot = jnp.sum(student * total, axis=0, keepdims=True)
        crop_sum[...] = (total - student * dot) * crop_scale_ref[...]
        for oc in range(CORES):
            for oz in range(nz):
                top = pl.multiple_of(((z ^ oz) * CORES + (c ^ oc)) * rows, rows)
                for ob in range(nb):
                    left = pl.multiple_of((j ^ ob) * cols, cols)
                    crop_out[oc, oz, ob] = crop_sum[pl.ds(top, rows), pl.ds(left, cols)]


def gradients(at, grain, sizes, turned, protos, inv, proto_scale, teacher, student, crop, total, crop_scale):
    nb, nz = sizes
    width, count = protos.shape
    crops = teacher.shape[1]
    step = min(256, count)
    rows, cols = width // (nz * CORES), crops // nb
    wide = width // nb
    return pl.pallas_call(
        functools.partial(grads_body, (nb, nz, rows, cols), grain),
        grid=(count // step,),
        out_shape=(
            jax.ShapeDtypeStruct((nb, wide, count), jnp.float32),
            jax.ShapeDtypeStruct((CORES, nz, nb, rows, cols), jnp.float32),
            jax.ShapeDtypeStruct((1, 1), jnp.float32),
        ),
        in_specs=[
            SMEM,
            pl.BlockSpec((step, width), lambda i: (i, 0)),
            pl.BlockSpec((width, step), lambda i: (0, i)),
            pl.BlockSpec((step, 1), lambda i: (i, 0)),
            pl.BlockSpec((1, step), lambda i: (0, i)),
        ]
        + [whole(x.shape) for x in (teacher, student, crop, total, crop_scale)],
        out_specs=(
            pl.BlockSpec((nb, wide, step), lambda i: (0, 0, i)),
            whole((CORES, nz, nb, rows, cols)),
            whole((1, 1)),
        ),
        scratch_shapes=[
            pltpu.VMEM((width, crops), jnp.float32),
            pltpu.VMEM((1, crops), jnp.float32),
        ],
        compiler_params=params(56),
        name="gradients",
    )(at, turned, protos, inv, proto_scale, teacher, student, crop, total, crop_scale)


def sum_everywhere(rows):
    n, crops = rows.shape
    devices = lax.axis_size("batch") * lax.axis_size("proto")
    core = lax.axis_index("proto") % CORES
    rows = rows + swap(rows, 0, 0, 1)
    half = lax.dynamic_index_in_dim(rows.reshape(n, CORES, crops // CORES), core, 1, keepdims=False)
    sent = jnp.broadcast_to(half[None], (devices, n, crops // CORES))
    got = lax.all_to_all(sent, AXES, 0, 0)
    got = got.reshape(devices // CORES, CORES, n, crops // CORES).sum(axis=0)
    return got.transpose(1, 0, 2).reshape(n, crops)


def scatter_crops(parts, nz, nb):
    kept = parts[0] + swap(parts[1], 0, 0, 1)
    masks = z_masks(nz)
    halves = []
    for first, order in ((0, masks), (nb // 2, masks[::-1])):
        held = {o: kept[o, first : first + nb // 2] for o in range(nz)}
        for i, mask in enumerate(order):
            span = [0]
            for later in order[i + 1 :]:
                span = span + [o ^ later for o in span]
            sent = jnp.stack([held[o ^ mask] for o in span])
            got = swap(sent, 0, mask, 0)
            held = {o: held[o] + got[n] for n, o in enumerate(span)}
        halves.append(held[0])
    mine = jnp.concatenate(halves, axis=0)
    return sum([swap(mine[o], o, 0, 0) for o in range(1, nb)], mine[0])


def shards(teacher_emb, student_emb, prototypes):
    nb, nproto = lax.axis_size("batch"), lax.axis_size("proto")
    nz = nproto // CORES
    j, p = lax.axis_index("batch"), lax.axis_index("proto")
    at = jnp.stack([j, p // CORES, p % CORES]).astype(jnp.int32)
    width = teacher_emb.shape[0] * nproto
    crops = teacher_emb.shape[1] * nb
    rows, local = prototypes.shape
    count = local // nb

    def columns(o):
        return lax.dynamic_slice_in_dim(prototypes, (j ^ o) * count, count, 1)

    blocks = [columns(0)] + [swap(columns(o), o, 0, 0) for o in range(1, nb)]
    protos, turned, proto_scale = unit_protos(at, blocks)
    teacher, unused = unit_crops(at, gather_crops(teacher_emb), width, crops)
    student, crop_unit_scale = unit_crops(at, gather_crops(student_emb), width, crops)

    crop_scale = 1.0 / sum_everywhere(sweep(first_body, "first", turned, teacher))
    softmax_part = sweep(softmax_body, "softmax", turned, student)
    for iteration in range(1, ITERS):
        total, inv = sweep(sinkhorn_body, "sinkhorn", turned, teacher, crop_scale, inverse=True)
        if iteration == 1:
            both = sum_everywhere(jnp.concatenate([total, softmax_part], axis=0))
            total, softmax_total = both[:1], both[1:]
        else:
            total = sum_everywhere(total)
        crop_scale = crop_scale / total
    grain = crops * student_temp
    proto_parts, crop_parts, loss_part = gradients(
        at, grain, (nb, nz), turned, protos, inv, proto_scale, teacher, student, crop_scale,
        softmax_total, crop_unit_scale,
    )
    grad_proto = jnp.zeros((rows, local), jnp.float32)
    for o in range(nb):
        got = swap(proto_parts[o], o, 0, 0) if o else proto_parts[0]
        grad_proto = lax.dynamic_update_slice_in_dim(grad_proto, got, (j ^ o) * count, 1)
    grad_student = scatter_crops(crop_parts, nz, nb)
    loss = jnp.broadcast_to(loss_part, (1, 128))
    loss = loss + swap(loss, 0, 0, 1)
    for mask in z_masks(nz):
        loss = loss + swap(loss, 0, mask, 0)
    for i in range(nb.bit_length() - 1):
        loss = loss + swap(loss, 1 << i, 0, 0)
    return (grad_proto, grad_student, -loss[0, 0] / crops)


def solution(mesh):
    in_specs = (P("proto", "batch"), P("proto", "batch"), P("batch", "proto"))
    out_specs = (P("batch", "proto"), P("proto", "batch"), P())
    return jax.shard_map(shards, mesh=mesh, in_specs=in_specs, out_specs=out_specs, check_vma=False)
```

time: 382 us -> 215 us (0.56)
  blocking collectives: 186 us -> 26.1 us
  other arithmetic: 70.2 us -> 6.59 us
  Pallas kernels: 0 us -> 52.2 us
  starting transfers between devices: 0.12 us -> 49.8 us
  matrix products: 26.6 us -> 0 us
  waiting for transfers between devices: 77.5 us -> 62.2 us
  between operations: 16.3 us -> 2.43 us
  local copies, waits for them, and re-layouts: 5.26 us -> 14.8 us
    psum x9 -> x0, blocking collectives: 155 us -> none  [the longest x3 45.8 us: shards(): column_total = lax.psum(jnp.sum(targets, axis=0), 'batch')]
    ppermute x0 -> x40, waiting for transfers between devices: none -> 62.2 us  [swap(): return lax.ppermute(x, AXES, pairs)]
    reduce_sum x11 -> x3, other arithmetic: 61.9 us -> 0.21 us  [sum_everywhere(): got = got.reshape(devices // CORES, CORES, n, crops // CORES).sum(axis=0)]
    pallas_call x0 -> x8, Pallas kernels: none -> 52.2 us  [the longest x1 27.8 us: gradients(): pl.pallas_call(functools.partial(grads_body, (nb, nz, rows, cols), grain)...]
    reduce_scatter x2 -> x0, waiting for transfers between devices: 50.4 us -> none  [the longest x1 50.4 us: shards(): lax.psum_scatter(jnp.dot(rows, grad_logit, preferred_element_type=jnp.flo...]
    ppermute x0 -> x40, starting transfers between devices: none -> 45.7 us  [swap(): return lax.ppermute(x, AXES, pairs)]
    all_gather x2 -> x0, blocking collectives: 30.5 us -> none  [the longest x1 16.1 us: shards(): lax.all_gather(teacher_emb, 'proto', axis=0, tiled=True)]
    dot_general x4 -> x0, matrix products: 26.6 us -> none  [the longest x2 14.4 us: cosine(): lax.dot_general(left, right, (((0,), (0,)), ((), ())), preferred_element_...]
  transfers between devices with their start and end apart: 3 -> 41, of which waited for: 2 -> 15; matrix products, arithmetic and copies ran while one was open for 3% -> 4% of each run, Pallas kernels for 0% -> 6%
where the time goes in v1:
time: 215 us; the launch traced here: 214 us
  waiting for transfers between devices  62.2 us (29%)
  Pallas kernels  52.2 us (24%)
  starting transfers between devices  49.8 us (23%)
  blocking collectives  26.1 us (12%)
  local copies, waits for them, and re-layouts  14.8 us (7%)
  other arithmetic  6.59 us (3%)
  between operations  2.43 us (1%)
    ppermute x40, waiting for transfers between devices, swap(): return lax.ppermute(x, AXES, pairs)  62.2 us
    ppermute x40, starting transfers between devices, swap(): return lax.ppermute(x, AXES, pairs)  45.7 us
    pallas_call x1, Pallas kernels, gradients(): pl.pallas_call(functools.partial(grads_body, (nb, nz, rows, cols), grain)...  27.8 us
    all_to_all x2, blocking collectives, sum_everywhere(): got = lax.all_to_all(sent, AXES, 0, 0)  26.1 us
    pallas_call x4, Pallas kernels, sweep(): pl.pallas_call(body, grid=(protos // step,), out_shape=(row, inv) if inve...  19.9 us
    unnamed x45, local copies, waits for them, and re-layouts  9.11 us
  transfers between devices with their start and end apart: 41, of which 15 were waited for; matrix products, arithmetic and copies ran while one was open for 4% of the time, Pallas kernels for 6%

profile of v1, /device:TPU:0, one launch (start us, length us, event | category | flops | bytes accessed | tf_op | source)
XLA Modules:
  0.0 214.2 jit_solution(10310221487772110985)
XLA Ops:
  0.7 3.0 %collective-permute-start.3 = (bf16[32,512]{1,0:T(8,128)(2,1)}, bf16[32,512]{1,0:T(8,128)(2,1)S(1)}, u32[]{:S(2)}, u32[]{:S(2)}) collective-permute-start(bf16[32,512]{1,0:T(8,128)(2,1)} %param.3), channel_id=1, source_target_pairs={{0,8},{1,9},{2,10},{3,11},{4,12},{5,13},{6,14},{7,15},{8,0},{9,1},... | collective-permute-start | bytes 98312 | tf_op jit(solution)/shard_map/ppermute | solution.py:41
  10.1 3.0 %collective-permute-start.2 = (bf16[64,2048]{1,0:T(8,128)(2,1)S(1)}, bf16[64,2048]{1,0:T(8,128)(2,1)S(1)}, u32[]{:S(2)}, u32[]{:S(2)}) collective-permute-start(bf16[64,2048]{1,0:T(8,128)(2,1)S(1)} %get-tuple-element.37), channel_id=1, source_target_pairs={{0,24},{1,25},{2,26},{3,27},{4,28},{5,29},{6,30},{7,31},{8,16},{9,... | collective-permute-start | bytes 786440 | tf_op jit(solution)/shard_map/ppermute | solution.py:41
  16.7 3.3 %collective-permute-start.9 = (bf16[1,2,32,512]{3,2,1,0:T(8,128)(2,1)S(1)}, bf16[1,2,32,512]{3,2,1,0:T(8,128)(2,1)S(1)}, u32[]{:S(2)}, u32[]{:S(2)}) collective-permute-start(bf16[1,2,32,512]{3,2,1,0:T(8,128)(2,1)S(1)} %maximum_bitcast_fusion.1), channel_id=1, source_target_pairs={{0,6},{1,7},{2,4},{3,5},{4,2},{5,3},{6,0},{7,1},{8,14},{9,15},{10,... | collective-permute-start | bytes 196616 | tf_op jit(solution)/shard_map/ppermute | solution.py:41
  20.0 2.7 %collective-permute-done.9 = bf16[1,2,32,512]{3,2,1,0:T(8,128)(2,1)S(1)} collective-permute-done((bf16[1,2,32,512]{3,2,1,0:T(8,128)(2,1)S(1)}, bf16[1,2,32,512]{3,2,1,0:T(8,128)(2,1)S(1)}, u32[]{:S(2)}, u32[]{:S(2)}) %collective-permute-start.9) | collective-permute-done | bytes 65568 | tf_op jit(solution)/shard_map/ppermute | solution.py:41
  22.8 5.4 %collective-permute-done.4 = bf16[1,2,32,512]{3,2,1,0:T(8,128)(2,1)S(1)} collective-permute-done((bf16[1,2,32,512]{3,2,1,0:T(8,128)(2,1)S(1)}, bf16[1,2,32,512]{3,2,1,0:T(8,128)(2,1)S(1)}, u32[]{:S(2)}, u32[]{:S(2)}) %collective-permute-start.4) | collective-permute-done | bytes 65568 | tf_op jit(solution)/shard_map/ppermute | solution.py:41
  28.2 2.9 %collective-permute-start.5 = (bf16[2,2,32,512]{3,2,1,0:T(8,128)(2,1)S(1)}, bf16[2,2,32,512]{3,2,1,0:T(8,128)(2,1)S(1)}, u32[]{:S(2)}, u32[]{:S(2)}) collective-permute-start(bf16[2,2,32,512]{3,2,1,0:T(8,128)(2,1)S(1)} %pad_maximum_fusion.5), channel_id=1, source_target_pairs={{0,6},{1,7},{2,4},{3,5},{4,2},{5,3},{6,0},{7,1},{8,14},{9,15},{10,... | collective-permute-start | bytes 393224 | tf_op jit(solution)/shard_map/ppermute | solution.py:41
  31.1 2.7 %collective-permute-done.10 = bf16[2,2,32,512]{3,2,1,0:T(8,128)(2,1)S(1)} collective-permute-done((bf16[2,2,32,512]{3,2,1,0:T(8,128)(2,1)S(1)}, bf16[2,2,32,512]{3,2,1,0:T(8,128)(2,1)S(1)}, u32[]{:S(2)}, u32[]{:S(2)}) %collective-permute-start.10) | collective-permute-done | bytes 131104 | tf_op jit(solution)/shard_map/ppermute | solution.py:41
  33.8 4.3 %collective-permute-start.15 = (bf16[2,2,32,512]{3,2,1,0:T(8,128)(2,1)S(1)}, bf16[2,2,32,512]{3,2,1,0:T(8,128)(2,1)}, u32[]{:S(2)}, u32[]{:S(2)}) collective-permute-start(bf16[2,2,32,512]{3,2,1,0:T(8,128)(2,1)S(1)} %pad_maximum_fusion.7), channel_id=1, source_target_pairs={{0,6},{1,7},{2,4},{3,5},{4,2},{5,3},{6,0},{7,1},{8,14},{9,15},{10,... | collective-permute-start | bytes 393224 | tf_op jit(solution)/shard_map/ppermute | solution.py:41
  38.3 6.0 %collective-permute-done.19 = bf16[1,2,32,512]{3,2,1,0:T(8,128)(2,1)S(1)} collective-permute-done((bf16[1,2,32,512]{3,2,1,0:T(8,128)(2,1)S(1)}, bf16[1,2,32,512]{3,2,1,0:T(8,128)(2,1)S(1)}, u32[]{:S(2)}, u32[]{:S(2)}) %collective-permute-start.19) | collective-permute-done | bytes 65568 | tf_op jit(solution)/shard_map/ppermute | solution.py:41
  54.6 5.1 %first.1 = f32[1,2048]{1,0:T(1,128)S(1)} custom-call(bf16[2048,256]{1,0:T(8,128)(2,1)S(1)} %get-tuple-element.15.turned_ref, bf16[256,2048]{1,0:T(8,128)(2,1)S(1)} %get-tuple-element.17.teacher_ref), custom_call_target="tpu_custom_call" | custom-call | tf_op jit(solution)/shard_map/first/pallas_call | solution.py:176
  62.1 4.1 %all-to-all-start = ((f32[32,1,1024]{2,1,0:T(1,128)}), f32[32,1,1024]{2,1,0:T(1,128)S(1)}, u32[]{:S(2)}, u32[]{:S(2)}) async-start(f32[32,1,1024]{2,1,0:T(1,128)} %broadcast_in_dim.50), calls=%async_computation | async-start | bytes 262144 | tf_op jit(solution)/shard_map/all_to_all | solution.py:298
  70.8 3.8 %softmax.1 = f32[1,2048]{1,0:T(1,128)S(1)} custom-call(bf16[2048,256]{1,0:T(8,128)(2,1)S(1)} %get-tuple-element.15.turned_ref, bf16[256,2048]{1,0:T(8,128)(2,1)S(1)} %get-tuple-element.19.student_ref), custom_call_target="tpu_custom_call" | custom-call | tf_op jit(solution)/shard_map/softmax/pallas_call | solution.py:176
  75.1 5.9 %sinkhorn.2 = (f32[1,2048]{1,0:T(1,128)S(1)}, f32[2048,1]{1,0:T(8,128)}) custom-call(bf16[2048,256]{1,0:T(8,128)(2,1)S(1)} %get-tuple-element.15.turned_ref, bf16[256,2048]{1,0:T(8,128)(2,1)S(1)} %get-tuple-element.17.teacher_ref, f32[1,2048]{1,0:T(1,128)S(1)} %broadcast_divide_fusion.1.crop_ref), custom_call_target="tpu_custom_call" | custom-call | tf_op jit(solution)/shard_map/sinkhorn/pallas_call | solution.py:176
  82.5 15.6 %all_to_all.15 = f32[32,2,1024]{2,1,0:T(2,128)S(1)} all-to-all(f32[32,2,1024]{2,1,0:T(2,128)S(1)} %broadcast_in_dim.54), channel_id=1, replica_groups=mesh['batch'=4,'proto'=8] {'batch','proto'}, dimensions={0} | all-to-all | bytes 524288 | tf_op jit(solution)/shard_map/all_to_all | solution.py:298
  98.8 5.2 %sinkhorn.3 = (f32[1,2048]{1,0:T(1,128)S(1)}, f32[2048,1]{1,0:T(8,128)S(1)}) custom-call(bf16[2048,256]{1,0:T(8,128)(2,1)S(1)} %get-tuple-element.15.turned_ref, bf16[256,2048]{1,0:T(8,128)(2,1)S(1)} %get-tuple-element.17.teacher_ref, f32[1,2048]{1,0:T(1,128)S(1)} %get-tuple-element.27.crop_ref), custom_call_target="tpu_custom_call" | custom-call | tf_op jit(solution)/shard_map/sinkhorn/pallas_call | solution.py:176
  106.7 10.4 %all_to_all.16 = f32[32,1,1024]{2,1,0:T(1,128)S(1)} all-to-all(f32[32,1,1024]{2,1,0:T(1,128)S(1)} %broadcast_in_dim.56), channel_id=1, replica_groups=mesh['batch'=4,'proto'=8] {'batch','proto'}, dimensions={0} | all-to-all | bytes 262144 | tf_op jit(solution)/shard_map/all_to_all | solution.py:298
  118.2 27.8 %gradients.1 = (f32[4,64,2048]{2,1,0:T(8,128)}, f32[2,4,4,32,512]{4,3,2,1,0:T(8,128)}, f32[1,1]{1,0:T(1,128)}) custom-call(s32[3]{0:T(128)} %copy-done.13, bf16[2048,256]{1,0:T(8,128)(2,1)} %copy-done, bf16[256,2048]{1,0:T(8,128)(2,1)} %copy-done.5, f32[2048,1]{1,0:T(8,128)} %copy-done.6, f32[1,2048]{1,0:T(1,128)} %copy-done.14, ...), custom_call_target="tpu_custom_call" | custom-call | tf_op jit(solution)/shard_map/gradients/pallas_call | solution.py:261
  151.4 3.1 %collective-permute-done.36 = f32[1,128]{1,0:T(1,128)S(1)} collective-permute-done((f32[1,128]{1,0:T(1,128)S(1)}, f32[1,128]{1,0:T(1,128)S(1)}, u32[]{:S(2)}, u32[]{:S(2)}) %collective-permute-start.36) | collective-permute-done | bytes 544 | tf_op jit(solution)/shard_map/ppermute | solution.py:41
  156.2 4.4 %collective-permute-done.37 = f32[1,128]{1,0:T(1,128)S(1)} collective-permute-done((f32[1,128]{1,0:T(1,128)S(1)}, f32[1,128]{1,0:T(1,128)S(1)}, u32[]{:S(2)}, u32[]{:S(2)}) %collective-permute-start.37) | collective-permute-done | bytes 544 | tf_op jit(solution)/shard_map/ppermute | solution.py:41
  166.4 18.9 %collective-permute-done.39 = f32[1,128]{1,0:T(1,128)S(1)} collective-permute-done((f32[1,128]{1,0:T(1,128)S(1)}, f32[1,128]{1,0:T(1,128)S(1)}, u32[]{:S(2)}, u32[]{:S(2)}) %collective-permute-start.39) | collective-permute-done | bytes 544 | tf_op jit(solution)/shard_map/ppermute | solution.py:41
  186.5 2.9 %collective-permute-start.29 = (f32[1,2,32,512]{3,2,1,0:T(8,128)S(1)}, f32[1,2,32,512]{3,2,1,0:T(8,128)S(1)}, u32[]{:S(2)}, u32[]{:S(2)}) collective-permute-start(f32[1,2,32,512]{3,2,1,0:T(8,128)S(1)} %get-tuple-element.34), channel_id=1, source_target_pairs={{0,6},{1,7},{2,4},{3,5},{4,2},{5,3},{6,0},{7,1},{8,14},{9,15},{10,... | collective-permute-start | bytes 393224 | tf_op jit(solution)/shard_map/ppermute | solution.py:41
  189.4 8.9 %collective-permute-done.29 = f32[1,2,32,512]{3,2,1,0:T(8,128)S(1)} collective-permute-done((f32[1,2,32,512]{3,2,1,0:T(8,128)S(1)}, f32[1,2,32,512]{3,2,1,0:T(8,128)S(1)}, u32[]{:S(2)}, u32[]{:S(2)}) %collective-permute-start.29) | collective-permute-done | bytes 131104 | tf_op jit(solution)/shard_map/ppermute | solution.py:41
  198.4 5.2 %collective-permute-start.32 = (f32[1,2,32,512]{3,2,1,0:T(8,128)S(1)}, f32[1,2,32,512]{3,2,1,0:T(8,128)S(1)}, u32[]{:S(2)}, u32[]{:S(2)}) collective-permute-start(f32[1,2,32,512]{3,2,1,0:T(8,128)S(1)} %get-tuple-element.33), channel_id=1, source_target_pairs={{0,2},{1,3},{2,0},{3,1},{4,6},{5,7},{6,4},{7,5},{8,10},{9,11},{10,... | collective-permute-start | bytes 393224 | tf_op jit(solution)/shard_map/ppermute | solution.py:41
  204.0 2.5 %collective-permute-done.32 = f32[1,2,32,512]{3,2,1,0:T(8,128)S(1)} collective-permute-done((f32[1,2,32,512]{3,2,1,0:T(8,128)S(1)}, f32[1,2,32,512]{3,2,1,0:T(8,128)S(1)}, u32[]{:S(2)}, u32[]{:S(2)}) %collective-permute-start.32) | collective-permute-done | bytes 131104 | tf_op jit(solution)/shard_map/ppermute | solution.py:41
  (173 shorter events, 54.7 us)
Async XLA Ops:
  0.7 9.3 %collective-permute-start.3 = (bf16[32,512]{1,0:T(8,128)(2,1)}, bf16[32,512]{1,0:T(8,128)(2,1)S(1)}, u32[]{:S(2)}, u32[]{:S(2)}) collective-permute-start(bf16[32,512]{1,0:T(8,128)(2,1)} %param.3), channel_id=1, source_target_pairs={{0,8},{1,9},{2,10},{3,11},{4,12},{5,13},{6,14},{7,15},{8,0},{9,1},... | collective-permute-start | bytes 98312 | tf_op jit(solution)/shard_map/ppermute | solution.py:41
  3.7 6.4 %collective-permute-start.8 = (bf16[32,512]{1,0:T(8,128)(2,1)}, bf16[32,512]{1,0:T(8,128)(2,1)S(1)}, u32[]{:S(2)}, u32[]{:S(2)}) collective-permute-start(bf16[32,512]{1,0:T(8,128)(2,1)} %param.3), channel_id=1, source_target_pairs={{0,24},{1,25},{2,26},{3,27},{4,28},{5,29},{6,30},{7,31},{8,16},{9,... | collective-permute-start | bytes 98312 | tf_op jit(solution)/shard_map/ppermute | solution.py:41
  5.2 7.9 %collective-permute-start.7 = (bf16[32,512]{1,0:T(8,128)(2,1)}, bf16[32,512]{1,0:T(8,128)(2,1)S(1)}, u32[]{:S(2)}, u32[]{:S(2)}) collective-permute-start(bf16[32,512]{1,0:T(8,128)(2,1)} %param.3), channel_id=1, source_target_pairs={{0,16},{1,17},{2,18},{3,19},{4,20},{5,21},{6,22},{7,23},{8,24},{9,... | collective-permute-start | bytes 98312 | tf_op jit(solution)/shard_map/ppermute | solution.py:41
  5.2 8.4 %collective-permute-start.13 = (bf16[32,512]{1,0:T(8,128)(2,1)}, bf16[32,512]{1,0:T(8,128)(2,1)S(1)}, u32[]{:S(2)}, u32[]{:S(2)}) collective-permute-start(bf16[32,512]{1,0:T(8,128)(2,1)} %param.4), channel_id=1, source_target_pairs={{0,8},{1,9},{2,10},{3,11},{4,12},{5,13},{6,14},{7,15},{8,0},{9,1},... | collective-permute-start | bytes 98312 | tf_op jit(solution)/shard_map/ppermute | solution.py:41
  7.2 6.6 %collective-permute-start.18 = (bf16[32,512]{1,0:T(8,128)(2,1)}, bf16[32,512]{1,0:T(8,128)(2,1)S(1)}, u32[]{:S(2)}, u32[]{:S(2)}) collective-permute-start(bf16[32,512]{1,0:T(8,128)(2,1)} %param.4), channel_id=1, source_target_pairs={{0,24},{1,25},{2,26},{3,27},{4,28},{5,29},{6,30},{7,31},{8,16},{9,... | collective-permute-start | bytes 98312 | tf_op jit(solution)/shard_map/ppermute | solution.py:41
  10.0 6.7 %collective-permute-start.17 = (bf16[32,512]{1,0:T(8,128)(2,1)S(1)}, bf16[32,512]{1,0:T(8,128)(2,1)S(1)}, u32[]{:S(2)}, u32[]{:S(2)}) collective-permute-start(bf16[32,512]{1,0:T(8,128)(2,1)S(1)} %copy-done.20), channel_id=1, source_target_pairs={{0,16},{1,17},{2,18},{3,19},{4,20},{5,21},{6,22},{7,23},{8,24},{9,... | collective-permute-start | bytes 98312 | tf_op jit(solution)/shard_map/ppermute | solution.py:41
  10.1 35.4 %collective-permute-start.2 = (bf16[64,2048]{1,0:T(8,128)(2,1)S(1)}, bf16[64,2048]{1,0:T(8,128)(2,1)S(1)}, u32[]{:S(2)}, u32[]{:S(2)}) collective-permute-start(bf16[64,2048]{1,0:T(8,128)(2,1)S(1)} %get-tuple-element.37), channel_id=1, source_target_pairs={{0,24},{1,25},{2,26},{3,27},{4,28},{5,29},{6,30},{7,31},{8,16},{9,... | collective-permute-start | bytes 786440 | tf_op jit(solution)/shard_map/ppermute | solution.py:41
  13.1 33.4 %collective-permute-start = (bf16[64,2048]{1,0:T(8,128)(2,1)S(1)}, bf16[64,2048]{1,0:T(8,128)(2,1)S(1)}, u32[]{:S(2)}, u32[]{:S(2)}) collective-permute-start(bf16[64,2048]{1,0:T(8,128)(2,1)S(1)} %get-tuple-element.38), channel_id=1, source_target_pairs={{0,8},{1,9},{2,10},{3,11},{4,12},{5,13},{6,14},{7,15},{8,0},{9,1},... | collective-permute-start | bytes 786440 | tf_op jit(solution)/shard_map/ppermute | solution.py:41
  13.6 33.0 %collective-permute-start.1 = (bf16[64,2048]{1,0:T(8,128)(2,1)S(1)}, bf16[64,2048]{1,0:T(8,128)(2,1)S(1)}, u32[]{:S(2)}, u32[]{:S(2)}) collective-permute-start(bf16[64,2048]{1,0:T(8,128)(2,1)S(1)} %get-tuple-element.40), channel_id=1, source_target_pairs={{0,16},{1,17},{2,18},{3,19},{4,20},{5,21},{6,22},{7,23},{8,24},{9,... | collective-permute-start | bytes 786440 | tf_op jit(solution)/shard_map/ppermute | solution.py:41
  13.8 14.4 %collective-permute-start.14 = (bf16[1,2,32,512]{3,2,1,0:T(8,128)(2,1)S(1)}, bf16[1,2,32,512]{3,2,1,0:T(8,128)(2,1)S(1)}, u32[]{:S(2)}, u32[]{:S(2)}) collective-permute-start(bf16[1,2,32,512]{3,2,1,0:T(8,128)(2,1)S(1)} %maximum_bitcast_fusion.2), channel_id=1, source_target_pairs={{0,2},{1,3},{2,0},{3,1},{4,6},{5,7},{6,4},{7,5},{8,10},{9,11},{10,... | collective-permute-start | bytes 196616 | tf_op jit(solution)/shard_map/ppermute | solution.py:41
  28.2 10.0 %collective-permute-start.5 = (bf16[2,2,32,512]{3,2,1,0:T(8,128)(2,1)S(1)}, bf16[2,2,32,512]{3,2,1,0:T(8,128)(2,1)S(1)}, u32[]{:S(2)}, u32[]{:S(2)}) collective-permute-start(bf16[2,2,32,512]{3,2,1,0:T(8,128)(2,1)S(1)} %pad_maximum_fusion.5), channel_id=1, source_target_pairs={{0,6},{1,7},{2,4},{3,5},{4,2},{5,3},{6,0},{7,1},{8,14},{9,15},{10,... | collective-permute-start | bytes 393224 | tf_op jit(solution)/shard_map/ppermute | solution.py:41
  33.8 10.5 %collective-permute-start.15 = (bf16[2,2,32,512]{3,2,1,0:T(8,128)(2,1)S(1)}, bf16[2,2,32,512]{3,2,1,0:T(8,128)(2,1)}, u32[]{:S(2)}, u32[]{:S(2)}) collective-permute-start(bf16[2,2,32,512]{3,2,1,0:T(8,128)(2,1)S(1)} %pad_maximum_fusion.7), channel_id=1, source_target_pairs={{0,6},{1,7},{2,4},{3,5},{4,2},{5,3},{6,0},{7,1},{8,14},{9,15},{10,... | collective-permute-start | bytes 393224 | tf_op jit(solution)/shard_map/ppermute | solution.py:41
  45.5 14.7 %collective-permute-start.20 = (bf16[2,2,32,512]{3,2,1,0:T(8,128)(2,1)}, bf16[2,2,32,512]{3,2,1,0:T(8,128)(2,1)}, u32[]{:S(2)}, u32[]{:S(2)}) collective-permute-start(bf16[2,2,32,512]{3,2,1,0:T(8,128)(2,1)} %pad_maximum_fusion.8), channel_id=1, source_target_pairs={{0,2},{1,3},{2,0},{3,1},{4,6},{5,7},{6,4},{7,5},{8,10},{9,11},{10,... | collective-permute-start | bytes 393224 | tf_op jit(solution)/shard_map/ppermute | solution.py:41
  46.5 19.7 %collective-permute-start.16 = (bf16[4,2,32,512]{3,2,1,0:T(8,128)(2,1)S(1)}, bf16[4,2,32,512]{3,2,1,0:T(8,128)(2,1)}, u32[]{:S(2)}, u32[]{:S(2)}) collective-permute-start(bf16[4,2,32,512]{3,2,1,0:T(8,128)(2,1)S(1)} %pad_maximum_fusion.2.refs_0_), channel_id=1, source_target_pairs={{0,1},{1,0},{2,3},{3,2},{4,5},{5,4},{6,7},{7,6},{8,9},{9,8},{10,11... | collective-permute-start | bytes 786440 | tf_op jit(solution)/shard_map/ppermute | solution.py:41
  62.1 12.6 %all-to-all-start = ((f32[32,1,1024]{2,1,0:T(1,128)}), f32[32,1,1024]{2,1,0:T(1,128)S(1)}, u32[]{:S(2)}, u32[]{:S(2)}) async-start(f32[32,1,1024]{2,1,0:T(1,128)} %broadcast_in_dim.50), calls=%async_computation | async-start | bytes 262144 | tf_op jit(solution)/shard_map/all_to_all | solution.py:298
  147.5 18.3 %collective-permute-start.27 = (f32[4,4,32,512]{3,2,1,0:T(8,128)S(1)}, f32[4,4,32,512]{3,2,1,0:T(8,128)S(1)}, u32[]{:S(2)}, u32[]{:S(2)}) collective-permute-start(f32[4,4,32,512]{3,2,1,0:T(8,128)S(1)} %slice_bitcast_fusion), channel_id=1, source_target_pairs={{0,1},{1,0},{2,3},{3,2},{4,5},{5,4},{6,7},{7,6},{8,9},{9,8},{10,11... | collective-permute-start | bytes 3145736 | tf_op jit(solution)/shard_map/ppermute | solution.py:41
  161.6 47.0 %collective-permute-start.26 = (f32[64,2048]{1,0:T(8,128)S(1)}, f32[64,2048]{1,0:T(8,128)S(1)}, u32[]{:S(2)}, u32[]{:S(2)}) collective-permute-start(f32[64,2048]{1,0:T(8,128)S(1)} %get-tuple-element.29), channel_id=1, source_target_pairs={{0,24},{1,25},{2,26},{3,27},{4,28},{5,29},{6,30},{7,31},{8,16},{9,... | collective-permute-start | bytes 1572872 | tf_op jit(solution)/shard_map/ppermute | solution.py:41
  163.1 26.3 %collective-permute-start.25 = (f32[64,2048]{1,0:T(8,128)S(1)}, f32[64,2048]{1,0:T(8,128)S(1)}, u32[]{:S(2)}, u32[]{:S(2)}) collective-permute-start(f32[64,2048]{1,0:T(8,128)S(1)} %get-tuple-element.30), channel_id=1, source_target_pairs={{0,16},{1,17},{2,18},{3,19},{4,20},{5,21},{6,22},{7,23},{8,24},{9,... | collective-permute-start | bytes 1572872 | tf_op jit(solution)/shard_map/ppermute | solution.py:41
  164.3 22.2 %collective-permute-start.24 = (f32[64,2048]{1,0:T(8,128)S(1)}, f32[64,2048]{1,0:T(8,128)S(1)}, u32[]{:S(2)}, u32[]{:S(2)}) collective-permute-start(f32[64,2048]{1,0:T(8,128)S(1)} %get-tuple-element.31), channel_id=1, source_target_pairs={{0,8},{1,9},{2,10},{3,11},{4,12},{5,13},{6,14},{7,15},{8,0},{9,1},... | collective-permute-start | bytes 1572872 | tf_op jit(solution)/shard_map/ppermute | solution.py:41
  165.1 20.1 %collective-permute-start.39 = (f32[1,128]{1,0:T(1,128)S(1)}, f32[1,128]{1,0:T(1,128)S(1)}, u32[]{:S(2)}, u32[]{:S(2)}) collective-permute-start(f32[1,128]{1,0:T(1,128)S(1)} %add.113), channel_id=1, source_target_pairs={{0,16},{1,17},{2,18},{3,19},{4,20},{5,21},{6,22},{7,23},{8,24},{9,... | collective-permute-start | bytes 1544 | tf_op jit(solution)/shard_map/ppermute | solution.py:41
  166.1 19.2 %collective-permute-start.28 = (f32[2,2,32,512]{3,2,1,0:T(8,128)S(1)}, f32[2,2,32,512]{3,2,1,0:T(8,128)S(1)}, u32[]{:S(2)}, u32[]{:S(2)}) collective-permute-start(f32[2,2,32,512]{3,2,1,0:T(8,128)S(1)} %stack.72), channel_id=1, source_target_pairs={{0,2},{1,3},{2,0},{3,1},{4,6},{5,7},{6,4},{7,5},{8,10},{9,11},{10,... | collective-permute-start | bytes 786440 | tf_op jit(solution)/shard_map/ppermute | solution.py:41
  185.4 12.9 %collective-permute-start.31 = (f32[2,2,32,512]{3,2,1,0:T(8,128)S(1)}, f32[2,2,32,512]{3,2,1,0:T(8,128)S(1)}, u32[]{:S(2)}, u32[]{:S(2)}) collective-permute-start(f32[2,2,32,512]{3,2,1,0:T(8,128)S(1)} %pad_maximum_fusion.4), channel_id=1, source_target_pairs={{0,6},{1,7},{2,4},{3,5},{4,2},{5,3},{6,0},{7,1},{8,14},{9,15},{10,... | collective-permute-start | bytes 786440 | tf_op jit(solution)/shard_map/ppermute | solution.py:41
  186.5 11.8 %collective-permute-start.29 = (f32[1,2,32,512]{3,2,1,0:T(8,128)S(1)}, f32[1,2,32,512]{3,2,1,0:T(8,128)S(1)}, u32[]{:S(2)}, u32[]{:S(2)}) collective-permute-start(f32[1,2,32,512]{3,2,1,0:T(8,128)S(1)} %get-tuple-element.34), channel_id=1, source_target_pairs={{0,6},{1,7},{2,4},{3,5},{4,2},{5,3},{6,0},{7,1},{8,14},{9,15},{10,... | collective-permute-start | bytes 393224 | tf_op jit(solution)/shard_map/ppermute | solution.py:41
  198.4 8.2 %collective-permute-start.32 = (f32[1,2,32,512]{3,2,1,0:T(8,128)S(1)}, f32[1,2,32,512]{3,2,1,0:T(8,128)S(1)}, u32[]{:S(2)}, u32[]{:S(2)}) collective-permute-start(f32[1,2,32,512]{3,2,1,0:T(8,128)S(1)} %get-tuple-element.33), channel_id=1, source_target_pairs={{0,2},{1,3},{2,0},{3,1},{4,6},{5,7},{6,4},{7,5},{8,10},{9,11},{10,... | collective-permute-start | bytes 393224 | tf_op jit(solution)/shard_map/ppermute | solution.py:41
  (38 other events, 269.2 us)

commit v2 on v0

v2 whole, which is shorter than its diff:
```python
import functools
import math

import jax
import jax.numpy as jnp
from jax import lax
from jax.experimental import pallas as pl
from jax.experimental.pallas import tpu as pltpu
from jax.sharding import PartitionSpec as P


ITERS = 3
CORES = 2
AXES = ("batch", "proto")

teacher_temp = 0.07
student_temp = 0.1
epsilon = 1e-06
LOG2E = 1.0 / math.log(2.0)
T_GAIN = LOG2E / teacher_temp
S_GAIN = LOG2E / student_temp

SMEM = pl.BlockSpec(memory_space=pltpu.SMEM)
VMEM = pl.BlockSpec(memory_space=pltpu.VMEM)


def params(megabytes=24):
    return pltpu.CompilerParams(vmem_limit_bytes=megabytes << 20)


def swap(x, over_batch, over_z, over_core):
    batch, proto = lax.axis_size("batch"), lax.axis_size("proto")
    pairs = []
    for b in range(batch):
        for p in range(proto):
            other = p ^ (over_z * CORES + over_core)
            pairs.append((b * proto + p, (b ^ over_batch) * proto + other))
    return lax.ppermute(x, AXES, pairs)


def z_masks(nz):
    return [(2 << i) - 1 for i in range(nz.bit_length() - 1)]


def join(parts):
    return jnp.concatenate(parts, axis=0)


def gather_crops(x):
    batch = lax.axis_size("batch")
    nz = lax.axis_size("proto") // CORES
    pieces = join([x[None]] + [swap(x[None], o, 0, 0) for o in range(1, batch)])
    masks = z_masks(nz)
    found = []
    for first, order in ((0, masks), (batch // 2, masks[::-1])):
        held = pieces[None, first : first + batch // 2]
        offsets = [0]
        for mask in order:
            held = join([held, swap(held, 0, mask, 0)])
            offsets = offsets + [o ^ mask for o in offsets]
        found.append((held, offsets, first, 0))
        found.append((swap(held, 0, 0, 1), offsets, first, 1))
    return found


def unit_crops_body(plan, at_ref, *refs):
    pieces, (unit_ref, scale_ref, raw, sems) = refs[: len(plan)], refs[len(plan) :]
    j, z, c = at_ref[0], at_ref[1], at_ref[2]
    copies = []
    for ref, (offsets, first, core) in zip(pieces, plan):
        rows, cols = ref.shape[2:]
        for i, oz in enumerate(offsets):
            top = pl.multiple_of(((z ^ oz) * CORES + (c ^ core)) * rows, rows)
            for k in range(ref.shape[1]):
                left = pl.multiple_of((j ^ (first + k)) * cols, cols)
                target = raw.at[pl.ds(top, rows), pl.ds(left, cols)]
                copies.append(pltpu.make_async_copy(ref.at[i, k], target, sems.at[len(copies)]))
                copies[-1].start()
    for copy in copies:
        copy.wait()
    for left in range(0, raw.shape[1], cols):
        part = slice(left, left + cols)
        values = raw[:, part].astype(jnp.float32)
        factor = lax.rsqrt(jnp.sum(values * values, axis=0, keepdims=True) + epsilon)
        unit_ref[:, part] = (values * factor).astype(jnp.bfloat16)
        scale_ref[:, part] = factor


def unit_crops(at, found, width, crops, megabytes):
    plan = [(offsets, first, core) for _, offsets, first, core in found]
    copies = sum(piece.shape[0] * piece.shape[1] for piece, *_ in found)
    return pl.pallas_call(
        functools.partial(unit_crops_body, plan),
        out_shape=(
            jax.ShapeDtypeStruct((width, crops), jnp.bfloat16),
            jax.ShapeDtypeStruct((1, crops), jnp.float32),
        ),
        in_specs=[SMEM] + [pl.BlockSpec(memory_space=pltpu.HBM)] * len(found),
        out_specs=(VMEM, VMEM),
        scratch_shapes=[
            pltpu.VMEM((width, crops), jnp.bfloat16),
            pltpu.SemaphoreType.DMA((copies,)),
        ],
        compiler_params=params(megabytes),
    )(at, *[piece for piece, *_ in found])


def unit_protos_body(at_ref, *refs):
    blocks, (turned_ref, scale_ref, raw) = refs[:-3], refs[-3:]
    j = at_ref[0]
    rows, step = blocks[0].shape[0], raw.shape[1]
    for low in range(0, blocks[0].shape[1], step):
        part = slice(low, low + step)
        for o, ref in enumerate(blocks):
            top = pl.multiple_of((j ^ o) * rows, rows)
            raw[pl.ds(top, rows), :] = ref[:, part]
        values = raw[...].astype(jnp.float32)
        factor = lax.rsqrt(jnp.sum(values * values, axis=0, keepdims=True) + epsilon)
        turned_ref[part, :] = (values * factor).astype(jnp.bfloat16).T
        scale_ref[:, part] = factor


def unit_protos(at, blocks):
    rows, protos = blocks[0].shape
    width = rows * len(blocks)
    return pl.pallas_call(
        unit_protos_body,
        out_shape=(
            jax.ShapeDtypeStruct((protos, width), jnp.bfloat16),
            jax.ShapeDtypeStruct((1, protos), jnp.float32),
        ),
        in_specs=[SMEM] + [VMEM] * len(blocks),
        out_specs=(VMEM, VMEM),
        scratch_shapes=[pltpu.VMEM((width, min(512, protos)), jnp.bfloat16)],
        compiler_params=params(),
        name="unit_protos",
    )(at, *blocks)


def to_row(row_ref, tiles):
    for q in range(tiles.shape[0]):
        row_ref[:, q * 128 : (q + 1) * 128] = tiles[q : q + 1, :]


def to_tiles(tiles_ref, row_ref):
    for q in range(tiles_ref.shape[0]):
        tiles_ref[q : q + 1, :] = row_ref[:, q * 128 : (q + 1) * 128]


def received(got_ref, n):
    cores = []
    for core in range(CORES):
        total = got_ref[core, n]
        for device in range(core + CORES, got_ref.shape[0], CORES):
            total = total + got_ref[device, n]
        cores.append(total)
    return jnp.concatenate(cores, axis=0)


def sweep_body(gain, weigh, before, invert, turned_ref, unit_ref, *refs):
    if weigh:
        got_ref, *refs = refs
        if before:
            before_ref, *refs = refs
        sums_ref, crop_out, *refs = refs
        if invert:
            inv_ref, *refs = refs
        crop_row, total = refs
        crop = 1.0 / received(got_ref, 0)
        if before:
            crop = before_ref[...] * crop
        crop_out[...] = crop
        to_row(crop_row, crop)
    else:
        sums_ref, total = refs
    protos = turned_ref.shape[0]
    step = min(512, protos)
    total[...] = jnp.zeros_like(total)

    def block(i, carry):
        part = pl.ds(pl.multiple_of(i * step, step), step)
        mass = jnp.exp2(jnp.dot(turned_ref[part, :], unit_ref[...], preferred_element_type=jnp.float32) * gain)
        if weigh:
            mass = mass * crop_row[...]
        if gain == T_GAIN:
            inv = 1.0 / jnp.sum(mass, axis=1, keepdims=True)
            if invert:
                inv_ref[:, part] = inv.T
            mass = mass * inv
        total[...] += jnp.sum(mass.reshape(step // 8, 8, mass.shape[1]), axis=0)
        return carry

    lax.fori_loop(0, protos // step, block, 0)
    total[0:1, :] = jnp.sum(total[...], axis=0, keepdims=True)
    to_tiles(sums_ref, total.at[0:1, :])


def sweep(gain, turned, unit, got=None, before=None, invert=False):
    crops = unit.shape[1]
    tiles = jax.ShapeDtypeStruct((crops // 128, 128), jnp.float32)
    weigh = got is not None
    operands = [x for x in (turned, unit, got, before) if x is not None]
    out_shape = [tiles] + [tiles] * weigh
    if invert:
        out_shape.append(jax.ShapeDtypeStruct((1, turned.shape[0]), jnp.float32))
    row = pltpu.VMEM((1, crops), jnp.float32)
    return pl.pallas_call(
        functools.partial(sweep_body, gain, weigh, before is not None, invert),
        out_shape=out_shape,
        in_specs=[VMEM] * len(operands),
        out_specs=[VMEM] * len(out_shape),
        scratch_shapes=[row] * weigh + [pltpu.VMEM((8, crops), jnp.float32)],
        compiler_params=params(),
    )(*operands)


def grads_body(plan, at_ref, turned_ref, inv_ref, got_ref, both_ref, before_ref, *refs):
    nb, nz, rows, chunk, grain = plan
    teacher_ref, student_ref, crop_scale_ref, crop_out, by_proto, *refs = refs
    grad_ref, result, protos, inverse, crop_row, total_row, loss_sum = refs
    j, z, c = at_ref[0], at_ref[1], at_ref[2]
    count = turned_ref.shape[0]
    tile = student_ref.shape[1]
    step = pl.program_id(0)

    @pl.when(step == 0)
    def _():
        to_row(crop_row, jnp.log2(before_ref[...] / (received(got_ref, 0) * grain)))
        to_row(total_row, -jnp.log2(received(both_ref, 1) * grain))
        loss_sum[...] = jnp.zeros_like(loss_sum)
        for low in range(0, count, chunk):
            part = slice(low, low + chunk)
            protos[:, part] = turned_ref[part, :].T
            inverse[part, :] = jnp.broadcast_to(inv_ref[:, part], (128, chunk)).T
            by_proto[part, :] = jnp.zeros((chunk, by_proto.shape[1]), jnp.float32)

    inner = crop_row.shape[1] // nb // tile
    block, within = lax.div(step, inner), lax.rem(step, inner)
    here = pl.ds(pl.multiple_of(((j ^ block) * inner + within) * tile, tile), tile)
    loss = loss_sum[...]
    for low in range(0, count, chunk):
        part = slice(low, low + chunk)
        turned = turned_ref[part, :]
        by_teacher = jnp.dot(turned, teacher_ref[...], preferred_element_type=jnp.float32)
        by_student = jnp.dot(turned, student_ref[...], preferred_element_type=jnp.float32)
        inv = jnp.concatenate([inverse[part, :]] * (tile // 128), axis=1)
        targets = jnp.exp2(by_teacher * T_GAIN + crop_row[:, here]) * inv
        power = by_student * S_GAIN + total_row[:, here]
        grad_ref[part, :] = (jnp.exp2(power) - targets).astype(jnp.bfloat16)
        loss += jnp.sum((targets * power).reshape(chunk // 8, 8, tile), axis=0)
    loss_sum[...] = loss
    by_crop = jnp.dot(protos[...], grad_ref[...], preferred_element_type=jnp.float32)
    student = student_ref[...]
    values = student.astype(jnp.float32)
    radial = jnp.sum(values * by_crop, axis=0, keepdims=True)
    result[...] = (by_crop - values * radial) * crop_scale_ref[...]
    across = pl.ds(pl.multiple_of(within * tile, tile), tile)
    for oc in range(CORES):
        for oz in range(nz):
            top = pl.multiple_of(((z ^ oz) * CORES + (c ^ oc)) * rows, rows)
            target = pl.ds(pl.multiple_of((oz * nb + block) * rows, rows), rows)
            crop_out[oc, target, across] = result[pl.ds(top, rows), :]
    turned_student = student.T
    for low in range(0, count, chunk):
        part = slice(low, low + chunk)
        by_proto[part, :] += jnp.dot(grad_ref[part, :], turned_student, preferred_element_type=jnp.float32)

    @pl.when(step == pl.num_programs(0) - 1)
    def _():
        total = jnp.sum(jnp.sum(loss_sum[...], axis=0, keepdims=True), axis=1, keepdims=True)
        for oc in range(CORES):
            crop_out[oc, -8:, :] = jnp.broadcast_to(total, (8, crop_out.shape[2]))


def gradients(at, sizes, turned, inv, sums, teacher, student, crop_scale):
    nb, nz = sizes
    count, width = turned.shape
    crops = teacher.shape[1]
    rows, cols = width // (nz * CORES), crops // nb
    tile = min(256, cols)
    inner = cols // tile
    chunk = min(256, count)

    def across(height):
        return pl.BlockSpec((height, tile), lambda i, at_ref: (0, (at_ref[0] ^ (i // inner)) * inner + i % inner))

    fixed = [turned, inv] + list(sums)
    return pl.pallas_call(
        functools.partial(grads_body, (nb, nz, rows, chunk, crops * student_temp)),
        grid_spec=pltpu.PrefetchScalarGridSpec(
            num_scalar_prefetch=1,
            grid=(crops // tile,),
            in_specs=[VMEM] * len(fixed) + [across(width), across(width), across(1)],
            out_specs=[VMEM, VMEM],
            scratch_shapes=[
                pltpu.VMEM((count, tile), jnp.bfloat16),
                pltpu.VMEM((width, tile), jnp.float32),
                pltpu.VMEM((width, count), jnp.bfloat16),
                pltpu.VMEM((count, 128), jnp.float32),
                pltpu.VMEM((1, crops), jnp.float32),
                pltpu.VMEM((1, crops), jnp.float32),
                pltpu.VMEM((8, tile), jnp.float32),
            ],
        ),
        out_shape=[
            jax.ShapeDtypeStruct((CORES, nz * nb * rows + 8, cols), jnp.float32),
            jax.ShapeDtypeStruct((count, width), jnp.float32),
        ],
        compiler_params=params(),
        name="gradients",
    )(at, *fixed, teacher, student, crop_scale)


def finish_protos_body(nb, at_ref, by_proto, turned_ref, scale_ref, out_ref, top_ref, result):
    j = at_ref[0]
    count, width = by_proto.shape
    chunk = result.shape[1]
    wide = width // nb
    tops = jnp.zeros((1, chunk), jnp.float32)
    for low in range(0, count, chunk):
        part = slice(low, low + chunk)
        total = by_proto[part, :]
        values = turned_ref[part, :].astype(jnp.float32)
        radial = jnp.sum(values * total, axis=1, keepdims=True)
        final = (total - values * radial).T * scale_ref[:, part]
        result[...] = final
        tops = jnp.maximum(tops, jnp.max(jnp.abs(final), axis=0, keepdims=True))
        for o in range(nb):
            out_ref[o, :, part] = result[pl.ds(pl.multiple_of((j ^ o) * wide, wide), wide), :]
    top_ref[...] = jnp.broadcast_to(jnp.max(tops, axis=1, keepdims=True), top_ref.shape)


def finish_protos(at, nb, by_proto, turned, scale):
    count, width = turned.shape
    return pl.pallas_call(
        functools.partial(finish_protos_body, nb),
        out_shape=[
            jax.ShapeDtypeStruct((nb, width // nb, count), jnp.float32),
            jax.ShapeDtypeStruct((1, 128), jnp.float32),
        ],
        in_specs=[SMEM, VMEM, VMEM, VMEM],
        out_specs=[VMEM, VMEM],
        scratch_shapes=[pltpu.VMEM((width, min(256, count)), jnp.float32)],
        compiler_params=params(),
        name="finish_protos",
    )(at, by_proto, turned, scale)


def finish_crops_body(grain, crops, *refs):
    parts, (grad_ref, loss_ref) = refs[:-2], refs[-2:]
    total = parts[0][...]
    for ref in parts[1:]:
        total = total + ref[...]
    rows = grad_ref.shape[0]
    grad_ref[...] = total[:rows]
    loss_ref[...] = (total[rows : rows + 1, :128] * grain + math.log2(grain) * crops) * (-1.0 / (LOG2E * crops))


def finish_crops(parts, grain, crops):
    rows, cols = parts[0].shape
    return pl.pallas_call(
        functools.partial(finish_crops_body, grain, crops),
        out_shape=[
            jax.ShapeDtypeStruct((rows - 8, cols), jnp.float32),
            jax.ShapeDtypeStruct((1, 128), jnp.float32),
        ],
        in_specs=[VMEM] * len(parts),
        out_specs=[VMEM, VMEM],
        compiler_params=params(4),
        name="finish_crops",
    )(*parts)


def pack_body(at_ref, *refs):
    mine, theirs, out_ref = refs[: len(refs) // 2], refs[len(refs) // 2 : -1], refs[-1]
    half = out_ref.shape[2]
    part = pl.ds(pl.multiple_of(at_ref[2] * half, half), half)
    for n in range(len(mine)):
        total = mine[n][part, :] + theirs[n][part, :]
        for device in range(out_ref.shape[0]):
            out_ref[device, n] = total


def sum_everywhere(at, *tiles):
    devices = lax.axis_size("batch") * lax.axis_size("proto")
    theirs = [swap(x, 0, 0, 1) for x in tiles]
    sent = pl.pallas_call(
        pack_body,
        out_shape=jax.ShapeDtypeStruct((devices, len(tiles), tiles[0].shape[0] // CORES, 128), jnp.float32),
        in_specs=[SMEM] + [VMEM] * (2 * len(tiles)),
        out_specs=VMEM,
        compiler_params=params(),
        name="pack",
    )(at, *tiles, *theirs)
    return lax.all_to_all(sent, AXES, 0, 0)


def scatter_crops(parts, nz, nb, rows):
    kept = parts[0] + swap(parts[1], 0, 0, 1)
    extra = kept[nz * nb * rows :]
    kept = kept[: nz * nb * rows].reshape(nz, nb * rows, -1)
    masks = z_masks(nz)
    size = nb // 2 * rows
    held = [[kept[o, :size] for o in range(nz)], [kept[o, size:] for o in range(nz)]]
    for i in range(len(masks)):
        for side, order in enumerate((masks, masks[::-1])):
            span = [0]
            for later in order[i + 1 :]:
                span = span + [o ^ later for o in span]
            sent = [held[side][o ^ order[i]] for o in span] + [extra] * (side == 0)
            got = swap(jnp.concatenate(sent, axis=0), 0, order[i], 0)
            held[side] = {o: held[side][o] + got[n * size : (n + 1) * size] for n, o in enumerate(span)}
            if side == 0:
                more = extra + got[len(span) * size :]
        extra = more
    mine = [half[0][i * rows : (i + 1) * rows] for half in held for i in range(nb // 2)]
    return [jnp.concatenate([part, extra], axis=0) for part in mine]


def place_body(at_ref, *refs):
    parts, (out_ref, sems) = refs[:-2], refs[-2:]
    cols = parts[0].shape[1]
    copies = []
    for o, ref in enumerate(parts):
        left = pl.multiple_of((at_ref[0] ^ o) * cols, cols)
        copies.append(pltpu.make_async_copy(ref, out_ref.at[:, pl.ds(left, cols)], sems.at[o]))
        copies[-1].start()
    for copy in copies:
        copy.wait()


def place(at, parts):
    rows, cols = parts[0].shape
    return pl.pallas_call(
        place_body,
        out_shape=jax.ShapeDtypeStruct((rows, cols * len(parts)), jnp.float32),
        in_specs=[SMEM] + [VMEM] * len(parts),
        out_specs=pl.BlockSpec(memory_space=pl.ANY),
        scratch_shapes=[pltpu.SemaphoreType.DMA((len(parts),))],
        compiler_params=params(4),
        name="place",
    )(at, *parts)


def shards(teacher_emb, student_emb, prototypes):
    nb, nproto = lax.axis_size("batch"), lax.axis_size("proto")
    nz = nproto // CORES
    j, p = lax.axis_index("batch"), lax.axis_index("proto")
    at = jnp.stack([j, p // CORES, p % CORES]).astype(jnp.int32)
    width = teacher_emb.shape[0] * nproto
    crops = teacher_emb.shape[1] * nb
    count = prototypes.shape[1] // nb
    grain = crops * student_temp

    prototypes, at = lax.optimization_barrier((prototypes, at))

    def columns(o):
        return lax.dynamic_slice_in_dim(prototypes, (j ^ o) * count, count, 1)

    blocks = [columns(0)] + [swap(columns(o), o, 0, 0) for o in range(1, nb)]
    turned, proto_scale = unit_protos(at, blocks)
    teacher = unit_crops(at, gather_crops(teacher_emb), width, crops, 24)[0]
    student, crop_unit_scale = unit_crops(at, gather_crops(student_emb), width, crops, 60)

    (sums,) = sweep(T_GAIN, turned, teacher)
    got = sum_everywhere(at, sums)
    (softmax_sums,) = sweep(S_GAIN, turned, student)
    crop = None
    for iteration in range(1, ITERS):
        final = iteration == ITERS - 1
        sums, crop, *inv = sweep(T_GAIN, turned, teacher, got, crop, invert=final)
        got = sum_everywhere(at, sums, softmax_sums) if iteration == 1 else sum_everywhere(at, sums)
        both = got if iteration == 1 else both
    totals = (got, both, crop)
    crop_parts, by_proto = gradients(
        at, (nb, nz), turned, inv[0], totals, teacher, student, crop_unit_scale
    )
    mine = scatter_crops(crop_parts, nz, nb, teacher_emb.shape[0])
    proto_parts, top = finish_protos(at, nb, by_proto, turned, proto_scale)
    power = jnp.ceil(jnp.log2(jnp.maximum(top, 1e-30))) - 15.0
    edge = jnp.broadcast_to(power, (proto_parts.shape[1], 128))
    sent = [
        jnp.concatenate([proto_parts[o] * jnp.exp2(-power[:, :1]), edge], axis=1).astype(jnp.float16)
        for o in range(1, nb)
    ]
    got = [swap(x, o + 1, 0, 0).astype(jnp.float32) for o, x in enumerate(sent)]
    ready = [x[:, :count] * jnp.exp2(x[:1, count : count + 1]) for x in got]
    grad_proto = place(at, [proto_parts[0]] + ready)
    outs = [mine[0]] + [swap(mine[o], o, 0, 0) for o in range(1, nb)]
    grad_student, loss = finish_crops(outs, grain, crops)
    return (grad_proto, grad_student, loss[0, 0])


def solution(mesh):
    in_specs = (P("proto", "batch"), P("proto", "batch"), P("batch", "proto"))
    out_specs = (P("batch", "proto"), P("proto", "batch"), P())
    return jax.shard_map(shards, mesh=mesh, in_specs=in_specs, out_specs=out_specs, check_vma=False)
```

time: 382 us -> 175 us (0.46)
  blocking collectives: 186 us -> 26 us
  other arithmetic: 70.2 us -> 1.28 us
  starting transfers between devices: 0.12 us -> 47.8 us
  Pallas kernels: 0 us -> 45 us
  waiting for transfers between devices: 77.5 us -> 45.5 us
  matrix products: 26.6 us -> 0 us
  between operations: 16.3 us -> 3.29 us
    psum x9 -> x0, blocking collectives: 155 us -> none  [the longest x3 45.8 us: shards(): column_total = lax.psum(jnp.sum(targets, axis=0), 'batch')]
    reduce_sum x11 -> x0, other arithmetic: 61.9 us -> none  [the longest x3 24.2 us: shards(): row_total = lax.psum(jnp.sum(targets, axis=1), 'proto')]
    reduce_scatter x2 -> x0, waiting for transfers between devices: 50.4 us -> none  [the longest x1 50.4 us: shards(): lax.psum_scatter(jnp.dot(rows, grad_logit, preferred_element_type=jnp.flo...]
    ppermute x0 -> x36, waiting for transfers between devices: none -> 45.5 us  [swap(): return lax.ppermute(x, AXES, pairs)]
    pallas_call x0 -> x14, Pallas kernels: none -> 45 us  [the longest x4 17.2 us: sweep(): pl.pallas_call(functools.partial(sweep_body, gain, weigh, before is not N...]
    ppermute x0 -> x36, starting transfers between devices: none -> 43.7 us  [swap(): return lax.ppermute(x, AXES, pairs)]
    all_gather x2 -> x0, blocking collectives: 30.5 us -> none  [the longest x1 16.1 us: shards(): lax.all_gather(teacher_emb, 'proto', axis=0, tiled=True)]
    dot_general x4 -> x0, matrix products: 26.6 us -> none  [the longest x2 14.4 us: cosine(): lax.dot_general(left, right, (((0,), (0,)), ((), ())), preferred_element_...]
  transfers between devices with their start and end apart: 3 -> 37, of which waited for: 2 -> 19; matrix products, arithmetic and copies ran while one was open for 3% -> 2% of each run, Pallas kernels for 0% -> 13%
where the time goes in v2:
time: 175 us
  starting transfers between devices  47.8 us (27%)
  waiting for transfers between devices  45.5 us (26%)
  Pallas kernels  45 us (26%)
  blocking collectives  26 us (15%)
  local copies, waits for them, and re-layouts  5.67 us (3%)
  between operations  3.29 us (2%)
    ppermute x36, waiting for transfers between devices, swap(): return lax.ppermute(x, AXES, pairs)  45.5 us
    ppermute x36, starting transfers between devices, swap(): return lax.ppermute(x, AXES, pairs)  43.7 us
    all_to_all x2, blocking collectives, sum_everywhere(): return lax.all_to_all(sent, AXES, 0, 0)  26 us
    pallas_call x4, Pallas kernels, sweep(): pl.pallas_call(functools.partial(sweep_body, gain, weigh, before is not N...  17.2 us
    pallas_call x1, Pallas kernels, gradients(): pl.pallas_call(functools.partial(grads_body, (nb, nz, rows, chunk, crops...  14.6 us
    pallas_call x2, Pallas kernels, unit_crops(): pl.pallas_call(functools.partial(unit_crops_body, plan), out_shape=(jax.S...  5.73 us
    all_to_all x1, starting transfers between devices, sum_everywhere(): return lax.all_to_all(sent, AXES, 0, 0)  4.08 us
  transfers between devices with their start and end apart: 37, of which 19 were waited for; matrix products, arithmetic and copies ran while one was open for 2% of the time, Pallas kernels for 13%

profile of v2, /device:TPU:0, one launch (start us, length us, event | category | flops | bytes accessed | tf_op | source)
XLA Modules:
  0.0 174.6 jit_solution(13371122327840980114)
XLA Ops:
  0.6 4.0 %collective-permute-start.8 = (bf16[1,32,512]{2,1,0:T(8,128)(2,1)}, bf16[1,32,512]{2,1,0:T(8,128)(2,1)S(1)}, u32[]{:S(2)}, u32[]{:S(2)}) collective-permute-start(bf16[1,32,512]{2,1,0:T(8,128)(2,1)} %bitcast.67), channel_id=1, source_target_pairs={{0,24},{1,25},{2,26},{3,27},{4,28},{5,29},{6,30},{7,31},{8,16},{9,... | collective-permute-start | bytes 98312 | tf_op jit(solution)/shard_map/ppermute | solution.py:38
  5.3 2.8 %collective-permute-start.18 = (bf16[1,32,512]{2,1,0:T(8,128)(2,1)}, bf16[1,32,512]{2,1,0:T(8,128)(2,1)S(1)}, u32[]{:S(2)}, u32[]{:S(2)}) collective-permute-start(bf16[1,32,512]{2,1,0:T(8,128)(2,1)} %bitcast.63), channel_id=1, source_target_pairs={{0,24},{1,25},{2,26},{3,27},{4,28},{5,29},{6,30},{7,31},{8,16},{9,... | collective-permute-start | bytes 98312 | tf_op jit(solution)/shard_map/ppermute | solution.py:38
  10.2 3.8 %collective-permute-done.13 = bf16[1,32,512]{2,1,0:T(8,128)(2,1)S(1)} collective-permute-done((bf16[1,32,512]{2,1,0:T(8,128)(2,1)S(1)}, bf16[1,32,512]{2,1,0:T(8,128)(2,1)S(1)}, u32[]{:S(2)}, u32[]{:S(2)}) %collective-permute-start.13) | collective-permute-done | bytes 32800 | tf_op jit(solution)/shard_map/ppermute | solution.py:38
  17.7 2.5 %collective-permute-start.19 = (bf16[1,2,32,512]{3,2,1,0:T(8,128)(2,1)S(1)}, bf16[1,2,32,512]{3,2,1,0:T(8,128)(2,1)S(1)}, u32[]{:S(2)}, u32[]{:S(2)}) collective-permute-start(bf16[1,2,32,512]{3,2,1,0:T(8,128)(2,1)S(1)} %maximum_bitcast_fusion.3), channel_id=1, source_target_pairs={{0,6},{1,7},{2,4},{3,5},{4,2},{5,3},{6,0},{7,1},{8,14},{9,15},{10,... | collective-permute-start | bytes 196616 | tf_op jit(solution)/shard_map/ppermute | solution.py:38
  21.1 2.9 %collective-permute-start.9 = (bf16[1,2,32,512]{3,2,1,0:T(8,128)(2,1)S(1)}, bf16[1,2,32,512]{3,2,1,0:T(8,128)(2,1)S(1)}, u32[]{:S(2)}, u32[]{:S(2)}) collective-permute-start(bf16[1,2,32,512]{3,2,1,0:T(8,128)(2,1)S(1)} %maximum_bitcast_fusion.1), channel_id=1, source_target_pairs={{0,6},{1,7},{2,4},{3,5},{4,2},{5,3},{6,0},{7,1},{8,14},{9,15},{10,... | collective-permute-start | bytes 196616 | tf_op jit(solution)/shard_map/ppermute | solution.py:38
  24.6 2.5 %collective-permute-start.15 = (bf16[2,2,32,512]{3,2,1,0:T(8,128)(2,1)S(1)}, bf16[2,2,32,512]{3,2,1,0:T(8,128)(2,1)S(1)}, u32[]{:S(2)}, u32[]{:S(2)}) collective-permute-start(bf16[2,2,32,512]{3,2,1,0:T(8,128)(2,1)S(1)} %pad_maximum_fusion.16), channel_id=1, source_target_pairs={{0,6},{1,7},{2,4},{3,5},{4,2},{5,3},{6,0},{7,1},{8,14},{9,15},{10,... | collective-permute-start | bytes 393224 | tf_op jit(solution)/shard_map/ppermute | solution.py:38
  28.0 2.8 %collective-permute-start.5 = (bf16[2,2,32,512]{3,2,1,0:T(8,128)(2,1)S(1)}, bf16[2,2,32,512]{3,2,1,0:T(8,128)(2,1)S(1)}, u32[]{:S(2)}, u32[]{:S(2)}) collective-permute-start(bf16[2,2,32,512]{3,2,1,0:T(8,128)(2,1)S(1)} %pad_maximum_fusion.14), channel_id=1, source_target_pairs={{0,6},{1,7},{2,4},{3,5},{4,2},{5,3},{6,0},{7,1},{8,14},{9,15},{10,... | collective-permute-start | bytes 393224 | tf_op jit(solution)/shard_map/ppermute | solution.py:38
  31.8 3.1 %collective-permute-done.5 = bf16[2,2,32,512]{3,2,1,0:T(8,128)(2,1)S(1)} collective-permute-done((bf16[2,2,32,512]{3,2,1,0:T(8,128)(2,1)S(1)}, bf16[2,2,32,512]{3,2,1,0:T(8,128)(2,1)S(1)}, u32[]{:S(2)}, u32[]{:S(2)}) %collective-permute-start.5) | collective-permute-done | bytes 131104 | tf_op jit(solution)/shard_map/ppermute | solution.py:38
  40.8 3.3 %collective-permute-done.refs_1_ = bf16[64,2048]{1,0:T(8,128)(2,1)S(1)} collective-permute-done((bf16[64,2048]{1,0:T(8,128)(2,1)S(1)}, bf16[64,2048]{1,0:T(8,128)(2,1)S(1)}, u32[]{:S(2)}, u32[]{:S(2)}) %collective-permute-start) | collective-permute-done | bytes 262176 | tf_op jit(solution)/shard_map/ppermute | solution.py:38
  45.1 2.2 %shard_map.58 = (bf16[256,2048]{1,0:T(8,128)(2,1)S(1)}, f32[1,2048]{1,0:T(1,128)}) custom-call(s32[3]{0:T(128)S(1)} %pad_add_fusion.at_ref, bf16[4,2,32,512]{3,2,1,0:T(8,128)(2,1)S(1)} %pad_maximum_fusion.4.refs_0_, bf16[4,2,32,512]{3,2,1,0:T(8,128)(2,1)S(1)} %collective-permute-done.6.refs_1_, bf16[4,2,32,512]{3,2,1,0:T(8,128)(2,1)S(1)} %pad_maximum_fusion.5.refs_2_, ...), custom_call_target="tpu_custom_call" | custom-call | tf_op jit(solution)/shard_map/pallas_call | solution.py:92
  47.3 4.4 %shard_map.59.refs_0_ = f32[16,128]{1,0:T(8,128)S(1)} custom-call(bf16[2048,256]{1,0:T(8,128)(2,1)S(1)} %get-tuple-element.23.turned_ref, bf16[256,2048]{1,0:T(8,128)(2,1)S(1)} %get-tuple-element.24.unit_ref.refs_0_), custom_call_target="tpu_custom_call" | custom-call | tf_op jit(solution)/shard_map/pallas_call | solution.py:207
  54.2 4.1 %all-to-all-start = ((f32[32,1,8,128]{3,2,1,0:T(8,128)}), f32[32,1,8,128]{3,2,1,0:T(8,128)S(1)}, u32[]{:S(2)}, u32[]{:S(2)}) async-start(f32[32,1,8,128]{3,2,1,0:T(8,128)} %pack.3), calls=%async_computation | async-start | bytes 262144 | tf_op jit(solution)/shard_map/all_to_all | solution.py:395
  59.7 3.5 %shard_map.61 = (bf16[256,2048]{1,0:T(8,128)(2,1)}, f32[1,2048]{1,0:T(1,128)}) custom-call(s32[3]{0:T(128)} %copy-done.2, bf16[4,2,32,512]{3,2,1,0:T(8,128)(2,1)} %copy-done.5, bf16[4,2,32,512]{3,2,1,0:T(8,128)(2,1)} %copy-done.8, bf16[4,2,32,512]{3,2,1,0:T(8,128)(2,1)} %copy-done.6, bf16[4,2,32,512]{3,2,1,0:T(8,128)(2,1)} %copy-done.7), custom_call_target="tpu_custom_call" | custom-call | tf_op jit(solution)/shard_map/pallas_call | solution.py:92
  64.4 2.9 %shard_map.62.refs_1_ = f32[16,128]{1,0:T(8,128)S(1)} custom-call(bf16[2048,256]{1,0:T(8,128)(2,1)S(1)} %get-tuple-element.23.turned_ref, bf16[256,2048]{1,0:T(8,128)(2,1)S(1)} %copy-done), custom_call_target="tpu_custom_call" | custom-call | tf_op jit(solution)/shard_map/pallas_call | solution.py:207
  67.6 4.8 %shard_map.60 = (f32[16,128]{1,0:T(8,128)S(1)}, f32[16,128]{1,0:T(8,128)S(1)}) custom-call(bf16[2048,256]{1,0:T(8,128)(2,1)S(1)} %get-tuple-element.23.turned_ref, bf16[256,2048]{1,0:T(8,128)(2,1)S(1)} %get-tuple-element.24.unit_ref.refs_0_, f32[32,1,8,128]{3,2,1,0:T(8,128)S(1)} %all-to-all-done.refs_0_), custom_call_target="tpu_custom_call" | custom-call | tf_op jit(solution)/shard_map/pallas_call | solution.py:207
  74.3 15.6 %all_to_all.15.refs_0_.both_ref = f32[32,2,8,128]{3,2,1,0:T(8,128)S(1)} all-to-all(f32[32,2,8,128]{3,2,1,0:T(8,128)S(1)} %pack.4), channel_id=1, replica_groups=mesh['batch'=4,'proto'=8] {'batch','proto'}, dimensions={0} | all-to-all | bytes 524288 | tf_op jit(solution)/shard_map/all_to_all | solution.py:395
  89.8 5.1 %shard_map.63 = (f32[16,128]{1,0:T(8,128)S(1)}, f32[16,128]{1,0:T(8,128)S(1)}, f32[1,2048]{1,0:T(1,128)S(1)}) custom-call(bf16[2048,256]{1,0:T(8,128)(2,1)S(1)} %get-tuple-element.23.turned_ref, bf16[256,2048]{1,0:T(8,128)(2,1)S(1)} %get-tuple-element.24.unit_ref.refs_0_, f32[32,2,8,128]{3,2,1,0:T(8,128)S(1)} %all_to_all.15.refs_0_.both_ref, ...), custom_call_target="tpu_custom_call" | custom-call | tf_op jit(solution)/shard_map/pallas_call | solution.py:207
  97.1 10.4 %all_to_all.16.got_ref = f32[32,1,8,128]{3,2,1,0:T(8,128)S(1)} all-to-all(f32[32,1,8,128]{3,2,1,0:T(8,128)S(1)} %pack.5), channel_id=1, replica_groups=mesh['batch'=4,'proto'=8] {'batch','proto'}, dimensions={0} | all-to-all | bytes 262144 | tf_op jit(solution)/shard_map/all_to_all | solution.py:395
  107.6 14.6 %gradients.1 = (f32[2,520,512]{2,1,0:T(8,128)S(1)}, f32[2048,256]{1,0:T(8,128)S(1)}) custom-call(s32[3]{0:T(128)S(1)} %copy-done.3, bf16[2048,256]{1,0:T(8,128)(2,1)S(1)} %get-tuple-element.23.turned_ref, f32[1,2048]{1,0:T(1,128)S(1)} %get-tuple-element.28.inv_ref, f32[32,1,8,128]{3,2,1,0:T(8,128)S(1)} %all_to_all.16.got_ref, ...), custom_call_target="tpu_custom_call" | custom-call | tf_op jit(solution)/shard_map/gradients/pallas_call | solution.py:288
  128.3 7.0 %collective-permute-done.27 = f16[64,2176]{1,0:T(8,128)(2,1)S(1)} collective-permute-done((f16[64,2176]{1,0:T(8,128)(2,1)S(1)}, f16[64,2176]{1,0:T(8,128)(2,1)S(1)}, u32[]{:S(2)}, u32[]{:S(2)}) %collective-permute-start.27) | collective-permute-done | bytes 278560 | tf_op jit(solution)/shard_map/ppermute | solution.py:38
  136.5 3.7 %collective-permute-done.26 = f16[64,2176]{1,0:T(8,128)(2,1)S(1)} collective-permute-done((f16[64,2176]{1,0:T(8,128)(2,1)S(1)}, f16[64,2176]{1,0:T(8,128)(2,1)S(1)}, u32[]{:S(2)}, u32[]{:S(2)}) %collective-permute-start.26) | collective-permute-done | bytes 278560 | tf_op jit(solution)/shard_map/ppermute | solution.py:38
  144.5 8.5 %collective-permute-done.32 = f32[128,512]{1,0:T(8,128)S(1)} collective-permute-done((f32[128,512]{1,0:T(8,128)S(1)}, f32[128,512]{1,0:T(8,128)S(1)}, u32[]{:S(2)}, u32[]{:S(2)}) %collective-permute-start.32) | collective-permute-done | bytes 262176 | tf_op jit(solution)/shard_map/ppermute | solution.py:38
  153.0 2.7 %collective-permute-start.33 = (f32[64,512]{1,0:T(8,128)S(1)}, f32[64,512]{1,0:T(8,128)S(1)}, u32[]{:S(2)}, u32[]{:S(2)}) collective-permute-start(f32[64,512]{1,0:T(8,128)S(1)} %slice_add_fusion), channel_id=1, source_target_pairs={{0,2},{1,3},{2,0},{3,1},{4,6},{5,7},{6,4},{7,5},{8,10},{9,11},{10,... | collective-permute-start | bytes 393224 | tf_op jit(solution)/shard_map/ppermute | solution.py:38
  162.2 4.9 %collective-permute-done.30 = f32[72,512]{1,0:T(8,128)S(1)} collective-permute-done((f32[72,512]{1,0:T(8,128)S(1)}, f32[72,512]{1,0:T(8,128)S(1)}, u32[]{:S(2)}, u32[]{:S(2)}) %collective-permute-start.30) | collective-permute-done | bytes 147488 | tf_op jit(solution)/shard_map/ppermute | solution.py:38
  (131 shorter events, 49.2 us)
Async XLA Ops:
  0.6 17.0 %collective-permute-start.8 = (bf16[1,32,512]{2,1,0:T(8,128)(2,1)}, bf16[1,32,512]{2,1,0:T(8,128)(2,1)S(1)}, u32[]{:S(2)}, u32[]{:S(2)}) collective-permute-start(bf16[1,32,512]{2,1,0:T(8,128)(2,1)} %bitcast.67), channel_id=1, source_target_pairs={{0,24},{1,25},{2,26},{3,27},{4,28},{5,29},{6,30},{7,31},{8,16},{9,... | collective-permute-start | bytes 98312 | tf_op jit(solution)/shard_map/ppermute | solution.py:38
  4.6 15.6 %collective-permute-start.7 = (bf16[1,32,512]{2,1,0:T(8,128)(2,1)}, bf16[1,32,512]{2,1,0:T(8,128)(2,1)S(1)}, u32[]{:S(2)}, u32[]{:S(2)}) collective-permute-start(bf16[1,32,512]{2,1,0:T(8,128)(2,1)} %bitcast.68), channel_id=1, source_target_pairs={{0,16},{1,17},{2,18},{3,19},{4,20},{5,21},{6,22},{7,23},{8,24},{9,... | collective-permute-start | bytes 98312 | tf_op jit(solution)/shard_map/ppermute | solution.py:38
  5.3 10.2 %collective-permute-start.18 = (bf16[1,32,512]{2,1,0:T(8,128)(2,1)}, bf16[1,32,512]{2,1,0:T(8,128)(2,1)S(1)}, u32[]{:S(2)}, u32[]{:S(2)}) collective-permute-start(bf16[1,32,512]{2,1,0:T(8,128)(2,1)} %bitcast.63), channel_id=1, source_target_pairs={{0,24},{1,25},{2,26},{3,27},{4,28},{5,29},{6,30},{7,31},{8,16},{9,... | collective-permute-start | bytes 98312 | tf_op jit(solution)/shard_map/ppermute | solution.py:38
  8.1 7.7 %collective-permute-start.17 = (bf16[1,32,512]{2,1,0:T(8,128)(2,1)}, bf16[1,32,512]{2,1,0:T(8,128)(2,1)S(1)}, u32[]{:S(2)}, u32[]{:S(2)}) collective-permute-start(bf16[1,32,512]{2,1,0:T(8,128)(2,1)} %bitcast.64), channel_id=1, source_target_pairs={{0,16},{1,17},{2,18},{3,19},{4,20},{5,21},{6,22},{7,23},{8,24},{9,... | collective-permute-start | bytes 98312 | tf_op jit(solution)/shard_map/ppermute | solution.py:38
  14.0 26.1 %collective-permute-start.2 = (bf16[64,2048]{1,0:T(8,128)(2,1)S(1)}, bf16[64,2048]{1,0:T(8,128)(2,1)S(1)}, u32[]{:S(2)}, u32[]{:S(2)}) collective-permute-start(bf16[64,2048]{1,0:T(8,128)(2,1)S(1)} %get-tuple-element.51), channel_id=1, source_target_pairs={{0,24},{1,25},{2,26},{3,27},{4,28},{5,29},{6,30},{7,31},{8,16},{9,... | collective-permute-start | bytes 786440 | tf_op jit(solution)/shard_map/ppermute | solution.py:38
  15.5 25.2 %collective-permute-start.1 = (bf16[64,2048]{1,0:T(8,128)(2,1)S(1)}, bf16[64,2048]{1,0:T(8,128)(2,1)S(1)}, u32[]{:S(2)}, u32[]{:S(2)}) collective-permute-start(bf16[64,2048]{1,0:T(8,128)(2,1)S(1)} %get-tuple-element.52), channel_id=1, source_target_pairs={{0,16},{1,17},{2,18},{3,19},{4,20},{5,21},{6,22},{7,23},{8,24},{9,... | collective-permute-start | bytes 786440 | tf_op jit(solution)/shard_map/ppermute | solution.py:38
  17.7 13.2 %collective-permute-start.19 = (bf16[1,2,32,512]{3,2,1,0:T(8,128)(2,1)S(1)}, bf16[1,2,32,512]{3,2,1,0:T(8,128)(2,1)S(1)}, u32[]{:S(2)}, u32[]{:S(2)}) collective-permute-start(bf16[1,2,32,512]{3,2,1,0:T(8,128)(2,1)S(1)} %maximum_bitcast_fusion.3), channel_id=1, source_target_pairs={{0,6},{1,7},{2,4},{3,5},{4,2},{5,3},{6,0},{7,1},{8,14},{9,15},{10,... | collective-permute-start | bytes 196616 | tf_op jit(solution)/shard_map/ppermute | solution.py:38
  21.1 6.9 %collective-permute-start.9 = (bf16[1,2,32,512]{3,2,1,0:T(8,128)(2,1)S(1)}, bf16[1,2,32,512]{3,2,1,0:T(8,128)(2,1)S(1)}, u32[]{:S(2)}, u32[]{:S(2)}) collective-permute-start(bf16[1,2,32,512]{3,2,1,0:T(8,128)(2,1)S(1)} %maximum_bitcast_fusion.1), channel_id=1, source_target_pairs={{0,6},{1,7},{2,4},{3,5},{4,2},{5,3},{6,0},{7,1},{8,14},{9,15},{10,... | collective-permute-start | bytes 196616 | tf_op jit(solution)/shard_map/ppermute | solution.py:38
  24.6 14.6 %collective-permute-start.15 = (bf16[2,2,32,512]{3,2,1,0:T(8,128)(2,1)S(1)}, bf16[2,2,32,512]{3,2,1,0:T(8,128)(2,1)S(1)}, u32[]{:S(2)}, u32[]{:S(2)}) collective-permute-start(bf16[2,2,32,512]{3,2,1,0:T(8,128)(2,1)S(1)} %pad_maximum_fusion.16), channel_id=1, source_target_pairs={{0,6},{1,7},{2,4},{3,5},{4,2},{5,3},{6,0},{7,1},{8,14},{9,15},{10,... | collective-permute-start | bytes 393224 | tf_op jit(solution)/shard_map/ppermute | solution.py:38
  28.0 6.9 %collective-permute-start.5 = (bf16[2,2,32,512]{3,2,1,0:T(8,128)(2,1)S(1)}, bf16[2,2,32,512]{3,2,1,0:T(8,128)(2,1)S(1)}, u32[]{:S(2)}, u32[]{:S(2)}) collective-permute-start(bf16[2,2,32,512]{3,2,1,0:T(8,128)(2,1)S(1)} %pad_maximum_fusion.14), channel_id=1, source_target_pairs={{0,6},{1,7},{2,4},{3,5},{4,2},{5,3},{6,0},{7,1},{8,14},{9,15},{10,... | collective-permute-start | bytes 393224 | tf_op jit(solution)/shard_map/ppermute | solution.py:38
  30.8 6.8 %collective-permute-start.10 = (bf16[2,2,32,512]{3,2,1,0:T(8,128)(2,1)S(1)}, bf16[2,2,32,512]{3,2,1,0:T(8,128)(2,1)S(1)}, u32[]{:S(2)}, u32[]{:S(2)}) collective-permute-start(bf16[2,2,32,512]{3,2,1,0:T(8,128)(2,1)S(1)} %pad_maximum_fusion.15), channel_id=1, source_target_pairs={{0,2},{1,3},{2,0},{3,1},{4,6},{5,7},{6,4},{7,5},{8,10},{9,11},{10,... | collective-permute-start | bytes 393224 | tf_op jit(solution)/shard_map/ppermute | solution.py:38
  37.7 6.4 %collective-permute-start = (bf16[64,2048]{1,0:T(8,128)(2,1)S(1)}, bf16[64,2048]{1,0:T(8,128)(2,1)S(1)}, u32[]{:S(2)}, u32[]{:S(2)}) collective-permute-start(bf16[64,2048]{1,0:T(8,128)(2,1)S(1)} %get-tuple-element.53), channel_id=1, source_target_pairs={{0,8},{1,9},{2,10},{3,11},{4,12},{5,13},{6,14},{7,15},{8,0},{9,1},... | collective-permute-start | bytes 786440 | tf_op jit(solution)/shard_map/ppermute | solution.py:38
  39.2 5.9 %collective-permute-start.11 = (bf16[4,2,32,512]{3,2,1,0:T(8,128)(2,1)S(1)}, bf16[4,2,32,512]{3,2,1,0:T(8,128)(2,1)S(1)}, u32[]{:S(2)}, u32[]{:S(2)}) collective-permute-start(bf16[4,2,32,512]{3,2,1,0:T(8,128)(2,1)S(1)} %pad_maximum_fusion.5.refs_2_), channel_id=1, source_target_pairs={{0,1},{1,0},{2,3},{3,2},{4,5},{5,4},{6,7},{7,6},{8,9},{9,8},{10,11... | collective-permute-start | bytes 786440 | tf_op jit(solution)/shard_map/ppermute | solution.py:38
  40.1 18.2 %collective-permute-start.21 = (bf16[4,2,32,512]{3,2,1,0:T(8,128)(2,1)S(1)}, bf16[4,2,32,512]{3,2,1,0:T(8,128)(2,1)S(1)}, u32[]{:S(2)}, u32[]{:S(2)}) collective-permute-start(bf16[4,2,32,512]{3,2,1,0:T(8,128)(2,1)S(1)} %pad_maximum_fusion.7.refs_2_), channel_id=1, source_target_pairs={{0,1},{1,0},{2,3},{3,2},{4,5},{5,4},{6,7},{7,6},{8,9},{9,8},{10,11... | collective-permute-start | bytes 786440 | tf_op jit(solution)/shard_map/ppermute | solution.py:38
  40.7 17.6 %collective-permute-start.16 = (bf16[4,2,32,512]{3,2,1,0:T(8,128)(2,1)S(1)}, bf16[4,2,32,512]{3,2,1,0:T(8,128)(2,1)S(1)}, u32[]{:S(2)}, u32[]{:S(2)}) collective-permute-start(bf16[4,2,32,512]{3,2,1,0:T(8,128)(2,1)S(1)} %pad_maximum_fusion.6.refs_0_), channel_id=1, source_target_pairs={{0,1},{1,0},{2,3},{3,2},{4,5},{5,4},{6,7},{7,6},{8,9},{9,8},{10,11... | collective-permute-start | bytes 786440 | tf_op jit(solution)/shard_map/ppermute | solution.py:38
  54.2 13.5 %all-to-all-start = ((f32[32,1,8,128]{3,2,1,0:T(8,128)}), f32[32,1,8,128]{3,2,1,0:T(8,128)S(1)}, u32[]{:S(2)}, u32[]{:S(2)}) async-start(f32[32,1,8,128]{3,2,1,0:T(8,128)} %pack.3), calls=%async_computation | async-start | bytes 262144 | tf_op jit(solution)/shard_map/all_to_all | solution.py:395
  124.0 17.5 %collective-permute-start.28 = (f32[520,512]{1,0:T(8,128)S(1)}, f32[520,512]{1,0:T(8,128)S(1)}, u32[]{:S(2)}, u32[]{:S(2)}) collective-permute-start(f32[520,512]{1,0:T(8,128)S(1)} %slice_bitcast_fusion), channel_id=1, source_target_pairs={{0,1},{1,0},{2,3},{3,2},{4,5},{5,4},{6,7},{7,6},{8,9},{9,8},{10,11... | collective-permute-start | bytes 3194888 | tf_op jit(solution)/shard_map/ppermute | solution.py:38
  124.7 10.5 %collective-permute-start.27 = (f16[64,2176]{1,0:T(8,128)(2,1)S(1)}, f16[64,2176]{1,0:T(8,128)(2,1)S(1)}, u32[]{:S(2)}, u32[]{:S(2)}) collective-permute-start(f16[64,2176]{1,0:T(8,128)(2,1)S(1)} %get-tuple-element.63), channel_id=1, source_target_pairs={{0,24},{1,25},{2,26},{3,27},{4,28},{5,29},{6,30},{7,31},{8,16},{9,... | collective-permute-start | bytes 835592 | tf_op jit(solution)/shard_map/ppermute | solution.py:38
  125.5 14.7 %collective-permute-start.26 = (f16[64,2176]{1,0:T(8,128)(2,1)S(1)}, f16[64,2176]{1,0:T(8,128)(2,1)S(1)}, u32[]{:S(2)}, u32[]{:S(2)}) collective-permute-start(f16[64,2176]{1,0:T(8,128)(2,1)S(1)} %get-tuple-element.64), channel_id=1, source_target_pairs={{0,16},{1,17},{2,18},{3,19},{4,20},{5,21},{6,22},{7,23},{8,24},{9,... | collective-permute-start | bytes 835592 | tf_op jit(solution)/shard_map/ppermute | solution.py:38
  126.8 16.4 %collective-permute-start.25 = (f16[64,2176]{1,0:T(8,128)(2,1)S(1)}, f16[64,2176]{1,0:T(8,128)(2,1)S(1)}, u32[]{:S(2)}, u32[]{:S(2)}) collective-permute-start(f16[64,2176]{1,0:T(8,128)(2,1)S(1)} %get-tuple-element.65), channel_id=1, source_target_pairs={{0,8},{1,9},{2,10},{3,11},{4,12},{5,13},{6,14},{7,15},{8,0},{9,1},... | collective-permute-start | bytes 835592 | tf_op jit(solution)/shard_map/ppermute | solution.py:38
  141.9 11.0 %collective-permute-start.32 = (f32[128,512]{1,0:T(8,128)S(1)}, f32[128,512]{1,0:T(8,128)S(1)}, u32[]{:S(2)}, u32[]{:S(2)}) collective-permute-start(f32[128,512]{1,0:T(8,128)S(1)} %pad_maximum_fusion.8), channel_id=1, source_target_pairs={{0,6},{1,7},{2,4},{3,5},{4,2},{5,3},{6,0},{7,1},{8,14},{9,15},{10,... | collective-permute-start | bytes 786440 | tf_op jit(solution)/shard_map/ppermute | solution.py:38
  143.1 14.8 %collective-permute-start.29 = (f32[136,512]{1,0:T(8,128)S(1)}, f32[136,512]{1,0:T(8,128)S(1)}, u32[]{:S(2)}, u32[]{:S(2)}) collective-permute-start(f32[136,512]{1,0:T(8,128)S(1)} %pad_maximum_fusion.3), channel_id=1, source_target_pairs={{0,2},{1,3},{2,0},{3,1},{4,6},{5,7},{6,4},{7,5},{8,10},{9,11},{10,... | collective-permute-start | bytes 835592 | tf_op jit(solution)/shard_map/ppermute | solution.py:38
  153.0 6.9 %collective-permute-start.33 = (f32[64,512]{1,0:T(8,128)S(1)}, f32[64,512]{1,0:T(8,128)S(1)}, u32[]{:S(2)}, u32[]{:S(2)}) collective-permute-start(f32[64,512]{1,0:T(8,128)S(1)} %slice_add_fusion), channel_id=1, source_target_pairs={{0,2},{1,3},{2,0},{3,1},{4,6},{5,7},{6,4},{7,5},{8,10},{9,11},{10,... | collective-permute-start | bytes 393224 | tf_op jit(solution)/shard_map/ppermute | solution.py:38
  160.0 7.1 %collective-permute-start.30 = (f32[72,512]{1,0:T(8,128)S(1)}, f32[72,512]{1,0:T(8,128)S(1)}, u32[]{:S(2)}, u32[]{:S(2)}) collective-permute-start(f32[72,512]{1,0:T(8,128)S(1)} %pad_maximum_fusion.13), channel_id=1, source_target_pairs={{0,6},{1,7},{2,4},{3,5},{4,2},{5,3},{6,0},{7,1},{8,14},{9,15},{10,... | collective-permute-start | bytes 442376 | tf_op jit(solution)/shard_map/ppermute | solution.py:38
  (24 other events, 163.3 us)

commit v3 on v2

--- a/solution.py
+++ b/solution.py
@@ -39,27 +39,37 @@
 
 
 def z_masks(nz):
-    return [(2 << i) - 1 for i in range(nz.bit_length() - 1)]
-
-
-def join(parts):
-    return jnp.concatenate(parts, axis=0)
-
-
-def gather_crops(x):
+    return [1 << i for i in range(nz.bit_length() - 1)]
+
+
+def join(parts, axis=1):
+    return jnp.concatenate(parts, axis=axis)
+
+
+def gather_crops(teacher, student):
     batch = lax.axis_size("batch")
     nz = lax.axis_size("proto") // CORES
-    pieces = join([x[None]] + [swap(x[None], o, 0, 0) for o in range(1, batch)])
+    x = jnp.stack([teacher, student])[:, None]
+    pieces = join([x] + [swap(x, o, 0, 0) for o in range(1, batch)])
     masks = z_masks(nz)
+    held, offsets = [], []
+    for first, order in ((0, masks), (batch // 2, masks[::-1])):
+        now, plan = pieces[:, None, first : first + batch // 2], [0]
+        for mask in order[:-1]:
+            now = join([now, swap(now, 0, mask, 0)])
+            plan = plan + [o ^ mask for o in plan]
+        held.append(now)
+        offsets.append(plan + [o ^ order[-1] for o in plan])
     found = []
-    for first, order in ((0, masks), (batch // 2, masks[::-1])):
-        held = pieces[None, first : first + batch // 2]
-        offsets = [0]
-        for mask in order:
-            held = join([held, swap(held, 0, mask, 0)])
-            offsets = offsets + [o ^ mask for o in offsets]
-        found.append((held, offsets, first, 0))
-        found.append((swap(held, 0, 0, 1), offsets, first, 1))
+    for which in range(2):
+        both = []
+        for side, mask in enumerate((masks[-1], masks[0])):
+            half = held[side][which]
+            half = join([half, swap(half, 0, mask, 0)], 0)
+            first = side * (batch // 2)
+            both.append((half, offsets[side], first, 0))
+            both.append((swap(half, 0, 0, 1), offsets[side], first, 1))
+        found.append(both)
     return found
 
 
@@ -214,7 +224,7 @@
     )(*operands)
 
 
-def grads_body(plan, at_ref, turned_ref, inv_ref, got_ref, both_ref, before_ref, *refs):
+def grads_body(plan, at_ref, turned_ref, inv_ref, got_ref, before_ref, *refs):
     nb, nz, rows, chunk, grain = plan
     teacher_ref, student_ref, crop_scale_ref, crop_out, by_proto, *refs = refs
     grad_ref, result, protos, inverse, crop_row, total_row, loss_sum = refs
@@ -226,7 +236,7 @@
     @pl.when(step == 0)
     def _():
         to_row(crop_row, jnp.log2(before_ref[...] / (received(got_ref, 0) * grain)))
-        to_row(total_row, -jnp.log2(received(both_ref, 1) * grain))
+        to_row(total_row, -jnp.log2(received(got_ref, 1) * grain))
         loss_sum[...] = jnp.zeros_like(loss_sum)
         for low in range(0, count, chunk):
             part = slice(low, low + chunk)
@@ -272,7 +282,7 @@
             crop_out[oc, -8:, :] = jnp.broadcast_to(total, (8, crop_out.shape[2]))
 
 
-def gradients(at, sizes, turned, inv, sums, teacher, student, crop_scale):
+def gradients(at, sizes, turned, inv, got, before, teacher, student, crop_scale):
     nb, nz = sizes
     count, width = turned.shape
     crops = teacher.shape[1]
@@ -284,7 +294,7 @@
     def across(height):
         return pl.BlockSpec((height, tile), lambda i, at_ref: (0, (at_ref[0] ^ (i // inner)) * inner + i % inner))
 
-    fixed = [turned, inv] + list(sums)
+    fixed = [turned, inv, got, before]
     return pl.pallas_call(
         functools.partial(grads_body, (nb, nz, rows, chunk, crops * student_temp)),
         grid_spec=pltpu.PrefetchScalarGridSpec(
@@ -412,18 +422,25 @@
             held[side] = {o: held[side][o] + got[n * size : (n + 1) * size] for n, o in enumerate(span)}
             if side == 0:
                 more = extra + got[len(span) * size :]
+            if i < len(masks) - 1:
+                held[side] = lax.optimization_barrier(held[side])
         extra = more
     mine = [half[0][i * rows : (i + 1) * rows] for half in held for i in range(nb // 2)]
     return [jnp.concatenate([part, extra], axis=0) for part in mine]
 
 
 def place_body(at_ref, *refs):
-    parts, (out_ref, sems) = refs[:-2], refs[-2:]
+    parts, (out_ref, scaled, sems) = refs[:-3], refs[-3:]
     cols = parts[0].shape[1]
     copies = []
     for o, ref in enumerate(parts):
         left = pl.multiple_of((at_ref[0] ^ o) * cols, cols)
-        copies.append(pltpu.make_async_copy(ref, out_ref.at[:, pl.ds(left, cols)], sems.at[o]))
+        source = ref
+        if o:
+            source = scaled.at[o - 1]
+            gain = jnp.exp2(ref[:, cols:])
+            source[...] = ref[:, :cols] * jnp.concatenate([gain] * (cols // 128), axis=1)
+        copies.append(pltpu.make_async_copy(source, out_ref.at[:, pl.ds(left, cols)], sems.at[o]))
         copies[-1].start()
     for copy in copies:
         copy.wait()
@@ -436,8 +453,11 @@
         out_shape=jax.ShapeDtypeStruct((rows, cols * len(parts)), jnp.float32),
         in_specs=[SMEM] + [VMEM] * len(parts),
         out_specs=pl.BlockSpec(memory_space=pl.ANY),
-        scratch_shapes=[pltpu.SemaphoreType.DMA((len(parts),))],
-        compiler_params=params(4),
+        scratch_shapes=[
+            pltpu.VMEM((len(parts) - 1, rows, cols), jnp.float32),
+            pltpu.SemaphoreType.DMA((len(parts),)),
+        ],
+        compiler_params=params(16),
         name="place",
     )(at, *parts)
 
@@ -459,22 +479,21 @@
 
     blocks = [columns(0)] + [swap(columns(o), o, 0, 0) for o in range(1, nb)]
     turned, proto_scale = unit_protos(at, blocks)
-    teacher = unit_crops(at, gather_crops(teacher_emb), width, crops, 24)[0]
-    student, crop_unit_scale = unit_crops(at, gather_crops(student_emb), width, crops, 60)
+    found = gather_crops(teacher_emb, student_emb)
+    teacher = unit_crops(at, found[0], width, crops, 24)[0]
+    student, crop_unit_scale = unit_crops(at, found[1], width, crops, 60)
 
     (sums,) = sweep(T_GAIN, turned, teacher)
-    got = sum_everywhere(at, sums)
-    (softmax_sums,) = sweep(S_GAIN, turned, student)
-    crop = None
+    got, crop, inv = sum_everywhere(at, sums), None, []
     for iteration in range(1, ITERS):
         final = iteration == ITERS - 1
         sums, crop, *inv = sweep(T_GAIN, turned, teacher, got, crop, invert=final)
-        got = sum_everywhere(at, sums, softmax_sums) if iteration == 1 else sum_everywhere(at, sums)
-        both = got if iteration == 1 else both
-    totals = (got, both, crop)
-    crop_parts, by_proto = gradients(
-        at, (nb, nz), turned, inv[0], totals, teacher, student, crop_unit_scale
-    )
+        if final:
+            got = sum_everywhere(at, sums, softmax_total)
+        else:
+            got = sum_everywhere(at, sums)
+            (softmax_total,) = sweep(S_GAIN, turned, student)
+    crop_parts, by_proto = gradients(at, (nb, nz), turned, inv[0], got, crop, teacher, student, crop_unit_scale)
     mine = scatter_crops(crop_parts, nz, nb, teacher_emb.shape[0])
     proto_parts, top = finish_protos(at, nb, by_proto, turned, proto_scale)
     power = jnp.ceil(jnp.log2(jnp.maximum(top, 1e-30))) - 15.0
@@ -483,8 +502,9 @@
         jnp.concatenate([proto_parts[o] * jnp.exp2(-power[:, :1]), edge], axis=1).astype(jnp.float16)
         for o in range(1, nb)
     ]
-    got = [swap(x, o + 1, 0, 0).astype(jnp.float32) for o, x in enumerate(sent)]
-    ready = [x[:, :count] * jnp.exp2(x[:1, count : count + 1]) for x in got]
+    got = [swap(x, o + 1, 0, 0) for o, x in enumerate(sent)]
+    got, mine = lax.optimization_barrier((got, mine))
+    ready = [x.astype(jnp.float32) for x in got]
     grad_proto = place(at, [proto_parts[0]] + ready)
     outs = [mine[0]] + [swap(mine[o], o, 0, 0) for o in range(1, nb)]
     grad_student, loss = finish_crops(outs, grain, crops)

time: 175 us -> 159 us (0.909)
  blocking collectives: 26 us -> 15.6 us
  starting transfers between devices: 47.8 us -> 42.1 us
  waiting for transfers between devices: 45.5 us -> 48.9 us
  local copies, waits for them, and re-layouts: 5.67 us -> 2.95 us
  between operations: 3.29 us -> 1.18 us
    all_to_all x2 -> x1, blocking collectives: 26 us -> 15.6 us  [sum_everywhere(): return lax.all_to_all(sent, AXES, 0, 0)]
    ppermute x36 -> x31, starting transfers between devices: 43.7 us -> 33.8 us  [swap(): return lax.ppermute(x, AXES, pairs)]
    all_to_all x1 -> x2, starting transfers between devices: 4.08 us -> 8.3 us  [sum_everywhere(): return lax.all_to_all(sent, AXES, 0, 0)]
    ppermute x36 -> x31, waiting for transfers between devices: 45.5 us -> 48.9 us  [swap(): return lax.ppermute(x, AXES, pairs)]
  transfers between devices with their start and end apart: 37 -> 33, of which waited for: 19 -> 17; matrix products, arithmetic and copies ran while one was open for 2% -> 1% of each run, Pallas kernels for 13% -> 19%
where the time goes in v3:
time: 159 us; the launch traced here: 158 us
  waiting for transfers between devices  48.9 us (31%)
  Pallas kernels  45.6 us (29%)
  starting transfers between devices  42.1 us (26%)
  blocking collectives  15.6 us (10%)
  local copies, waits for them, and re-layouts  2.95 us (2%)
  other arithmetic  2.03 us (1%)
    ppermute x31, waiting for transfers between devices, swap(): return lax.ppermute(x, AXES, pairs)  48.9 us
    ppermute x31, starting transfers between devices, swap(): return lax.ppermute(x, AXES, pairs)  33.8 us
    pallas_call x4, Pallas kernels, sweep(): pl.pallas_call(functools.partial(sweep_body, gain, weigh, before is not N...  17.2 us
    all_to_all x1, blocking collectives, sum_everywhere(): return lax.all_to_all(sent, AXES, 0, 0)  15.6 us
    pallas_call x1, Pallas kernels, gradients(): pl.pallas_call(functools.partial(grads_body, (nb, nz, rows, chunk, crops...  14.6 us
    all_to_all x2, starting transfers between devices, sum_everywhere(): return lax.all_to_all(sent, AXES, 0, 0)  8.3 us
    pallas_call x2, Pallas kernels, unit_crops(): pl.pallas_call(functools.partial(unit_crops_body, plan), out_shape=(jax.S...  5.73 us
  transfers between devices with their start and end apart: 33, of which 17 were waited for; matrix products, arithmetic and copies ran while one was open for 1% of the time, Pallas kernels for 19%

profile of v3, /device:TPU:0, one launch (start us, length us, event | category | flops | bytes accessed | tf_op | source)
XLA Modules:
  0.0 158.4 jit_solution(17539892459895280357)
XLA Ops:
  1.5 3.0 %collective-permute-start.3 = (bf16[2,1,32,512]{3,2,1,0:T(8,128)(2,1)S(1)}, bf16[2,1,32,512]{3,2,1,0:T(8,128)(2,1)S(1)}, u32[]{:S(2)}, u32[]{:S(2)}) collective-permute-start(bf16[2,1,32,512]{3,2,1,0:T(8,128)(2,1)S(1)} %maximum_bitcast_fusion.2), channel_id=1, source_target_pairs={{0,8},{1,9},{2,10},{3,11},{4,12},{5,13},{6,14},{7,15},{8,0},{9,1},... | collective-permute-start | bytes 196616 | tf_op jit(solution)/shard_map/ppermute | solution.py:38
  7.0 2.0 %collective-permute-start.4 = (bf16[2,1,2,32,512]{4,3,2,0,1:T(8,128)(2,1)S(1)}, bf16[2,1,2,32,512]{4,3,2,0,1:T(8,128)(2,1)S(1)}, u32[]{:S(2)}, u32[]{:S(2)}) collective-permute-start(bf16[2,1,2,32,512]{4,3,2,0,1:T(8,128)(2,1)S(1)} %maximum_bitcast_fusion), channel_id=1, source_target_pairs={{0,2},{1,3},{2,0},{3,1},{4,6},{5,7},{6,4},{7,5},{8,10},{9,11},{10,... | collective-permute-start | bytes 393224 | tf_op jit(solution)/shard_map/ppermute | solution.py:38
  10.6 2.7 %collective-permute-start.9 = (bf16[2,1,2,32,512]{4,3,2,1,0:T(8,128)(2,1)S(1)}, bf16[2,1,2,32,512]{4,3,2,1,0:T(8,128)(2,1)S(1)}, u32[]{:S(2)}, u32[]{:S(2)}) collective-permute-start(bf16[2,1,2,32,512]{4,3,2,1,0:T(8,128)(2,1)S(1)} %maximum_bitcast_fusion.1), channel_id=1, source_target_pairs={{0,4},{1,5},{2,6},{3,7},{4,0},{5,1},{6,2},{7,3},{8,12},{9,13},{10,... | collective-permute-start | bytes 393224 | tf_op jit(solution)/shard_map/ppermute | solution.py:38
  15.0 8.1 %collective-permute-done.9 = bf16[2,1,2,32,512]{4,3,2,1,0:T(8,128)(2,1)S(1)} collective-permute-done((bf16[2,1,2,32,512]{4,3,2,1,0:T(8,128)(2,1)S(1)}, bf16[2,1,2,32,512]{4,3,2,1,0:T(8,128)(2,1)S(1)}, u32[]{:S(2)}, u32[]{:S(2)}) %collective-permute-start.9) | collective-permute-done | bytes 131104 | tf_op jit(solution)/shard_map/ppermute | solution.py:38
  28.9 4.6 %collective-permute-done.2.refs_3_ = bf16[64,2048]{1,0:T(8,128)(2,1)S(1)} collective-permute-done((bf16[64,2048]{1,0:T(8,128)(2,1)S(1)}, bf16[64,2048]{1,0:T(8,128)(2,1)S(1)}, u32[]{:S(2)}, u32[]{:S(2)}) %collective-permute-start.2) | collective-permute-done | bytes 262176 | tf_op jit(solution)/shard_map/ppermute | solution.py:38
  35.1 2.3 %collective-permute-done.1.refs_2_ = bf16[64,2048]{1,0:T(8,128)(2,1)S(1)} collective-permute-done((bf16[64,2048]{1,0:T(8,128)(2,1)S(1)}, bf16[64,2048]{1,0:T(8,128)(2,1)S(1)}, u32[]{:S(2)}, u32[]{:S(2)}) %collective-permute-start.1) | collective-permute-done | bytes 262176 | tf_op jit(solution)/shard_map/ppermute | solution.py:38
  38.5 2.2 %shard_map.58 = (bf16[256,2048]{1,0:T(8,128)(2,1)S(1)}, f32[1,2048]{1,0:T(1,128)}) custom-call(s32[3]{0:T(128)S(1)} %pad_add_fusion.at_ref, bf16[4,2,32,512]{3,2,1,0:T(8,128)(2,1)S(1)} %pad_maximum_fusion.4.refs_0_, bf16[4,2,32,512]{3,2,1,0:T(8,128)(2,1)S(1)} %collective-permute-done.6.refs_1_, bf16[4,2,32,512]{3,2,1,0:T(8,128)(2,1)S(1)} %pad_maximum_fusion.5.refs_2_, ...), custom_call_target="tpu_custom_call" | custom-call | tf_op jit(solution)/shard_map/pallas_call | solution.py:102
  40.7 4.4 %shard_map.59.refs_0_ = f32[16,128]{1,0:T(8,128)S(1)} custom-call(bf16[2048,256]{1,0:T(8,128)(2,1)S(1)} %get-tuple-element.34.turned_ref, bf16[256,2048]{1,0:T(8,128)(2,1)S(1)} %get-tuple-element.35.unit_ref.refs_0_), custom_call_target="tpu_custom_call" | custom-call | tf_op jit(solution)/shard_map/pallas_call | solution.py:217
  47.5 4.7 %all-to-all-start = ((f32[32,1,8,128]{3,2,1,0:T(8,128)}), f32[32,1,8,128]{3,2,1,0:T(8,128)S(1)}, u32[]{:S(2)}, u32[]{:S(2)}) async-start(f32[32,1,8,128]{3,2,1,0:T(8,128)} %pack.3), calls=%async_computation | async-start | bytes 262144 | tf_op jit(solution)/shard_map/all_to_all | solution.py:405
  52.2 2.7 %collective-permute-start.14 = (bf16[2,2,32,512]{3,2,1,0:T(8,128)(2,1)S(1)}, bf16[2,2,32,512]{3,2,1,0:T(8,128)(2,1)S(1)}, u32[]{:S(2)}, u32[]{:S(2)}) collective-permute-start(bf16[2,2,32,512]{3,2,1,0:T(8,128)(2,1)S(1)} %get-tuple-element.83), channel_id=1, source_target_pairs={{0,4},{1,5},{2,6},{3,7},{4,0},{5,1},{6,2},{7,3},{8,12},{9,13},{10,... | collective-permute-start | bytes 393224 | tf_op jit(solution)/shard_map/ppermute | solution.py:38
  55.1 9.3 %collective-permute-done.14 = bf16[2,2,32,512]{3,2,1,0:T(8,128)(2,1)S(1)} collective-permute-done((bf16[2,2,32,512]{3,2,1,0:T(8,128)(2,1)S(1)}, bf16[2,2,32,512]{3,2,1,0:T(8,128)(2,1)S(1)}, u32[]{:S(2)}, u32[]{:S(2)}) %collective-permute-start.14) | collective-permute-done | bytes 131104 | tf_op jit(solution)/shard_map/ppermute | solution.py:38
  64.5 4.8 %shard_map.60 = (f32[16,128]{1,0:T(8,128)S(1)}, f32[16,128]{1,0:T(8,128)S(1)}) custom-call(bf16[2048,256]{1,0:T(8,128)(2,1)S(1)} %get-tuple-element.34.turned_ref, bf16[256,2048]{1,0:T(8,128)(2,1)S(1)} %get-tuple-element.35.unit_ref.refs_0_, f32[32,1,8,128]{3,2,1,0:T(8,128)S(1)} %all-to-all-done.refs_0_), custom_call_target="tpu_custom_call" | custom-call | tf_op jit(solution)/shard_map/pallas_call | solution.py:217
  71.9 3.6 %all-to-all-start.1 = ((f32[32,1,8,128]{3,2,1,0:T(8,128)}), f32[32,1,8,128]{3,2,1,0:T(8,128)S(1)}, u32[]{:S(2)}, u32[]{:S(2)}) async-start(f32[32,1,8,128]{3,2,1,0:T(8,128)} %pack.4), calls=%async_computation.1 | async-start | bytes 262144 | tf_op jit(solution)/shard_map/all_to_all | solution.py:405
  77.0 3.5 %shard_map.62 = (bf16[256,2048]{1,0:T(8,128)(2,1)}, f32[1,2048]{1,0:T(1,128)}) custom-call(s32[3]{0:T(128)} %copy-done.2, bf16[4,2,32,512]{3,2,1,0:T(8,128)(2,1)} %copy-done.7, bf16[4,2,32,512]{3,2,1,0:T(8,128)(2,1)} %copy-done.9, bf16[4,2,32,512]{3,2,1,0:T(8,128)(2,1)} %copy-done.6, bf16[4,2,32,512]{3,2,1,0:T(8,128)(2,1)} %copy-done.8), custom_call_target="tpu_custom_call" | custom-call | tf_op jit(solution)/shard_map/pallas_call | solution.py:102
  81.7 2.9 %shard_map.63.refs_1_ = f32[16,128]{1,0:T(8,128)S(1)} custom-call(bf16[2048,256]{1,0:T(8,128)(2,1)S(1)} %get-tuple-element.34.turned_ref, bf16[256,2048]{1,0:T(8,128)(2,1)S(1)} %copy-done), custom_call_target="tpu_custom_call" | custom-call | tf_op jit(solution)/shard_map/pallas_call | solution.py:217
  85.0 5.1 %shard_map.61 = (f32[16,128]{1,0:T(8,128)S(1)}, f32[16,128]{1,0:T(8,128)S(1)}, f32[1,2048]{1,0:T(1,128)S(1)}) custom-call(bf16[2048,256]{1,0:T(8,128)(2,1)S(1)} %get-tuple-element.34.turned_ref, bf16[256,2048]{1,0:T(8,128)(2,1)S(1)} %get-tuple-element.35.unit_ref.refs_0_, f32[32,1,8,128]{3,2,1,0:T(8,128)S(1)} %all-to-all-done.1.refs_0_, ...), custom_call_target="tpu_custom_call" | custom-call | tf_op jit(solution)/shard_map/pallas_call | solution.py:217
  91.8 15.6 %all_to_all.15.got_ref = f32[32,2,8,128]{3,2,1,0:T(8,128)S(1)} all-to-all(f32[32,2,8,128]{3,2,1,0:T(8,128)S(1)} %pack.5), channel_id=1, replica_groups=mesh['batch'=4,'proto'=8] {'batch','proto'}, dimensions={0} | all-to-all | bytes 524288 | tf_op jit(solution)/shard_map/all_to_all | solution.py:405
  107.4 14.6 %gradients.1 = (f32[2,520,512]{2,1,0:T(8,128)S(1)}, f32[2048,256]{1,0:T(8,128)S(1)}) custom-call(s32[3]{0:T(128)S(1)} %copy-done.3, bf16[2048,256]{1,0:T(8,128)(2,1)S(1)} %get-tuple-element.34.turned_ref, f32[1,2048]{1,0:T(1,128)S(1)} %get-tuple-element.38.inv_ref, f32[32,2,8,128]{3,2,1,0:T(8,128)S(1)} %all_to_all.15.got_ref, ...), custom_call_target="tpu_custom_call" | custom-call | tf_op jit(solution)/shard_map/gradients/pallas_call | solution.py:298
  131.4 9.0 %collective-permute-done.26 = f32[128,512]{1,0:T(8,128)S(1)} collective-permute-done((f32[128,512]{1,0:T(8,128)S(1)}, f32[128,512]{1,0:T(8,128)S(1)}, u32[]{:S(2)}, u32[]{:S(2)}) %collective-permute-start.26) | collective-permute-done | bytes 262176 | tf_op jit(solution)/shard_map/ppermute | solution.py:38
  140.7 2.7 %collective-permute-start.25 = (f32[72,512]{1,0:T(8,128)S(1)}, f32[72,512]{1,0:T(8,128)S(1)}, u32[]{:S(2)}, u32[]{:S(2)}) collective-permute-start(f32[72,512]{1,0:T(8,128)S(1)} %pad_maximum_fusion.13), channel_id=1, source_target_pairs={{0,4},{1,5},{2,6},{3,7},{4,0},{5,1},{6,2},{7,3},{8,12},{9,13},{10,... | collective-permute-start | bytes 442376 | tf_op jit(solution)/shard_map/ppermute | solution.py:38
  143.5 4.3 %collective-permute-done.27 = f32[64,512]{1,0:T(8,128)S(1)} collective-permute-done((f32[64,512]{1,0:T(8,128)S(1)}, f32[64,512]{1,0:T(8,128)S(1)}, u32[]{:S(2)}, u32[]{:S(2)}) %collective-permute-start.27) | collective-permute-done | bytes 131104 | tf_op jit(solution)/shard_map/ppermute | solution.py:38
  147.8 2.8 %collective-permute-done.25 = f32[72,512]{1,0:T(8,128)S(1)} collective-permute-done((f32[72,512]{1,0:T(8,128)S(1)}, f32[72,512]{1,0:T(8,128)S(1)}, u32[]{:S(2)}, u32[]{:S(2)}) %collective-permute-start.25) | collective-permute-done | bytes 147488 | tf_op jit(solution)/shard_map/ppermute | solution.py:38
  152.4 1.8 %collective-permute-start.30 = (f32[40,512]{1,0:T(8,128)S(1)}, f32[40,512]{1,0:T(8,128)S(1)}, u32[]{:S(2)}, u32[]{:S(2)}) collective-permute-start(f32[40,512]{1,0:T(8,128)S(1)} %get-tuple-element.58), channel_id=1, source_target_pairs={{0,24},{1,25},{2,26},{3,27},{4,28},{5,29},{6,30},{7,31},{8,16},{9,... | collective-permute-start | bytes 245768 | tf_op jit(solution)/shard_map/ppermute | solution.py:38
  154.3 1.9 %place.1 = f32[64,8192]{1,0:T(8,128)} custom-call(s32[3]{0:T(128)S(1)} %copy-done.3, f32[64,2048]{1,0:T(8,128)S(1)} %get-tuple-element.66.refs_0_, f32[64,2176]{1,0:T(8,128)S(1)} %convert_element_type.12.refs_1_, f32[64,2176]{1,0:T(8,128)S(1)} %convert_element_type.13.refs_2_, f32[64,2176]{1,0:T(8,128)S(1)} %convert_element_type.14.refs_3_), custom_call_target="tpu_custom_call" | custom-call | tf_op jit(solution)/shard_map/place/pallas_call | solution.py:451
  (111 shorter events, 38.5 us)
Async XLA Ops:
  1.5 5.4 %collective-permute-start.3 = (bf16[2,1,32,512]{3,2,1,0:T(8,128)(2,1)S(1)}, bf16[2,1,32,512]{3,2,1,0:T(8,128)(2,1)S(1)}, u32[]{:S(2)}, u32[]{:S(2)}) collective-permute-start(bf16[2,1,32,512]{3,2,1,0:T(8,128)(2,1)S(1)} %maximum_bitcast_fusion.2), channel_id=1, source_target_pairs={{0,8},{1,9},{2,10},{3,11},{4,12},{5,13},{6,14},{7,15},{8,0},{9,1},... | collective-permute-start | bytes 196616 | tf_op jit(solution)/shard_map/ppermute | solution.py:38
  7.0 6.3 %collective-permute-start.4 = (bf16[2,1,2,32,512]{4,3,2,0,1:T(8,128)(2,1)S(1)}, bf16[2,1,2,32,512]{4,3,2,0,1:T(8,128)(2,1)S(1)}, u32[]{:S(2)}, u32[]{:S(2)}) collective-permute-start(bf16[2,1,2,32,512]{4,3,2,0,1:T(8,128)(2,1)S(1)} %maximum_bitcast_fusion), channel_id=1, source_target_pairs={{0,2},{1,3},{2,0},{3,1},{4,6},{5,7},{6,4},{7,5},{8,10},{9,11},{10,... | collective-permute-start | bytes 393224 | tf_op jit(solution)/shard_map/ppermute | solution.py:38
  10.6 12.6 %collective-permute-start.9 = (bf16[2,1,2,32,512]{4,3,2,1,0:T(8,128)(2,1)S(1)}, bf16[2,1,2,32,512]{4,3,2,1,0:T(8,128)(2,1)S(1)}, u32[]{:S(2)}, u32[]{:S(2)}) collective-permute-start(bf16[2,1,2,32,512]{4,3,2,1,0:T(8,128)(2,1)S(1)} %maximum_bitcast_fusion.1), channel_id=1, source_target_pairs={{0,4},{1,5},{2,6},{3,7},{4,0},{5,1},{6,2},{7,3},{8,12},{9,13},{10,... | collective-permute-start | bytes 393224 | tf_op jit(solution)/shard_map/ppermute | solution.py:38
  13.3 15.0 %collective-permute-start.5 = (bf16[2,2,32,512]{3,2,1,0:T(8,128)(2,1)S(1)}, bf16[2,2,32,512]{3,2,1,0:T(8,128)(2,1)S(1)}, u32[]{:S(2)}, u32[]{:S(2)}) collective-permute-start(bf16[2,2,32,512]{3,2,1,0:T(8,128)(2,1)S(1)} %get-tuple-element.84), channel_id=1, source_target_pairs={{0,4},{1,5},{2,6},{3,7},{4,0},{5,1},{6,2},{7,3},{8,12},{9,13},{10,... | collective-permute-start | bytes 393224 | tf_op jit(solution)/shard_map/ppermute | solution.py:38
  23.4 10.2 %collective-permute-start.2 = (bf16[64,2048]{1,0:T(8,128)(2,1)S(1)}, bf16[64,2048]{1,0:T(8,128)(2,1)S(1)}, u32[]{:S(2)}, u32[]{:S(2)}) collective-permute-start(bf16[64,2048]{1,0:T(8,128)(2,1)S(1)} %get-tuple-element.77), channel_id=1, source_target_pairs={{0,24},{1,25},{2,26},{3,27},{4,28},{5,29},{6,30},{7,31},{8,16},{9,... | collective-permute-start | bytes 786440 | tf_op jit(solution)/shard_map/ppermute | solution.py:38
  24.9 12.6 %collective-permute-start.1 = (bf16[64,2048]{1,0:T(8,128)(2,1)S(1)}, bf16[64,2048]{1,0:T(8,128)(2,1)S(1)}, u32[]{:S(2)}, u32[]{:S(2)}) collective-permute-start(bf16[64,2048]{1,0:T(8,128)(2,1)S(1)} %get-tuple-element.78), channel_id=1, source_target_pairs={{0,16},{1,17},{2,18},{3,19},{4,20},{5,21},{6,22},{7,23},{8,24},{9,... | collective-permute-start | bytes 786440 | tf_op jit(solution)/shard_map/ppermute | solution.py:38
  25.8 11.7 %collective-permute-start = (bf16[64,2048]{1,0:T(8,128)(2,1)S(1)}, bf16[64,2048]{1,0:T(8,128)(2,1)S(1)}, u32[]{:S(2)}, u32[]{:S(2)}) collective-permute-start(bf16[64,2048]{1,0:T(8,128)(2,1)S(1)} %get-tuple-element.79), channel_id=1, source_target_pairs={{0,8},{1,9},{2,10},{3,11},{4,12},{5,13},{6,14},{7,15},{8,0},{9,1},... | collective-permute-start | bytes 786440 | tf_op jit(solution)/shard_map/ppermute | solution.py:38
  28.2 10.2 %collective-permute-start.11 = (bf16[4,2,32,512]{3,2,1,0:T(8,128)(2,1)S(1)}, bf16[4,2,32,512]{3,2,1,0:T(8,128)(2,1)S(1)}, u32[]{:S(2)}, u32[]{:S(2)}) collective-permute-start(bf16[4,2,32,512]{3,2,1,0:T(8,128)(2,1)S(1)} %pad_maximum_fusion.5.refs_2_), channel_id=1, source_target_pairs={{0,1},{1,0},{2,3},{3,2},{4,5},{5,4},{6,7},{7,6},{8,9},{9,8},{10,11... | collective-permute-start | bytes 786440 | tf_op jit(solution)/shard_map/ppermute | solution.py:38
  28.4 10.1 %collective-permute-start.6 = (bf16[4,2,32,512]{3,2,1,0:T(8,128)(2,1)S(1)}, bf16[4,2,32,512]{3,2,1,0:T(8,128)(2,1)S(1)}, u32[]{:S(2)}, u32[]{:S(2)}) collective-permute-start(bf16[4,2,32,512]{3,2,1,0:T(8,128)(2,1)S(1)} %pad_maximum_fusion.4.refs_0_), channel_id=1, source_target_pairs={{0,1},{1,0},{2,3},{3,2},{4,5},{5,4},{6,7},{7,6},{8,9},{9,8},{10,11... | collective-permute-start | bytes 786440 | tf_op jit(solution)/shard_map/ppermute | solution.py:38
  33.5 21.4 %collective-permute-start.16 = (bf16[2,2,32,512]{3,2,1,0:T(8,128)(2,1)S(1)}, bf16[2,2,32,512]{3,2,1,0:T(8,128)(2,1)S(1)}, u32[]{:S(2)}, u32[]{:S(2)}) collective-permute-start(bf16[2,2,32,512]{3,2,1,0:T(8,128)(2,1)S(1)} %get-tuple-element.81), channel_id=1, source_target_pairs={{0,2},{1,3},{2,0},{3,1},{4,6},{5,7},{6,4},{7,5},{8,10},{9,11},{10,... | collective-permute-start | bytes 393224 | tf_op jit(solution)/shard_map/ppermute | solution.py:38
  47.5 17.0 %all-to-all-start = ((f32[32,1,8,128]{3,2,1,0:T(8,128)}), f32[32,1,8,128]{3,2,1,0:T(8,128)S(1)}, u32[]{:S(2)}, u32[]{:S(2)}) async-start(f32[32,1,8,128]{3,2,1,0:T(8,128)} %pack.3), calls=%async_computation | async-start | bytes 262144 | tf_op jit(solution)/shard_map/all_to_all | solution.py:405
  52.2 12.2 %collective-permute-start.14 = (bf16[2,2,32,512]{3,2,1,0:T(8,128)(2,1)S(1)}, bf16[2,2,32,512]{3,2,1,0:T(8,128)(2,1)S(1)}, u32[]{:S(2)}, u32[]{:S(2)}) collective-permute-start(bf16[2,2,32,512]{3,2,1,0:T(8,128)(2,1)S(1)} %get-tuple-element.83), channel_id=1, source_target_pairs={{0,4},{1,5},{2,6},{3,7},{4,0},{5,1},{6,2},{7,3},{8,12},{9,13},{10,... | collective-permute-start | bytes 393224 | tf_op jit(solution)/shard_map/ppermute | solution.py:38
  55.0 20.6 %collective-permute-start.17 = (bf16[4,2,32,512]{3,2,1,0:T(8,128)(2,1)S(1)}, bf16[4,2,32,512]{3,2,1,0:T(8,128)(2,1)S(1)}, u32[]{:S(2)}, u32[]{:S(2)}) collective-permute-start(bf16[4,2,32,512]{3,2,1,0:T(8,128)(2,1)S(1)} %pad_maximum_fusion.7.refs_2_), channel_id=1, source_target_pairs={{0,1},{1,0},{2,3},{3,2},{4,5},{5,4},{6,7},{7,6},{8,9},{9,8},{10,11... | collective-permute-start | bytes 786440 | tf_op jit(solution)/shard_map/ppermute | solution.py:38
  64.4 11.2 %collective-permute-start.15 = (bf16[4,2,32,512]{3,2,1,0:T(8,128)(2,1)S(1)}, bf16[4,2,32,512]{3,2,1,0:T(8,128)(2,1)S(1)}, u32[]{:S(2)}, u32[]{:S(2)}) collective-permute-start(bf16[4,2,32,512]{3,2,1,0:T(8,128)(2,1)S(1)} %pad_maximum_fusion.6.refs_0_), channel_id=1, source_target_pairs={{0,1},{1,0},{2,3},{3,2},{4,5},{5,4},{6,7},{7,6},{8,9},{9,8},{10,11... | collective-permute-start | bytes 786440 | tf_op jit(solution)/shard_map/ppermute | solution.py:38
  71.9 13.0 %all-to-all-start.1 = ((f32[32,1,8,128]{3,2,1,0:T(8,128)}), f32[32,1,8,128]{3,2,1,0:T(8,128)S(1)}, u32[]{:S(2)}, u32[]{:S(2)}) async-start(f32[32,1,8,128]{3,2,1,0:T(8,128)} %pack.4), calls=%async_computation.1 | async-start | bytes 262144 | tf_op jit(solution)/shard_map/all_to_all | solution.py:405
  84.6 5.7 %collective-permute-start.19 = (f32[16,128]{1,0:T(8,128)S(1)}, f32[16,128]{1,0:T(8,128)S(1)}, u32[]{:S(2)}, u32[]{:S(2)}) collective-permute-start(f32[16,128]{1,0:T(8,128)S(1)} %shard_map.63.refs_1_), channel_id=1, source_target_pairs={{0,1},{1,0},{2,3},{3,2},{4,5},{5,4},{6,7},{7,6},{8,9},{9,8},{10,11... | collective-permute-start | bytes 24584 | tf_op jit(solution)/shard_map/ppermute | solution.py:38
  125.6 14.7 %collective-permute-start.26 = (f32[128,512]{1,0:T(8,128)S(1)}, f32[128,512]{1,0:T(8,128)S(1)}, u32[]{:S(2)}, u32[]{:S(2)}) collective-permute-start(f32[128,512]{1,0:T(8,128)S(1)} %pad_maximum_fusion.8), channel_id=1, source_target_pairs={{0,4},{1,5},{2,6},{3,7},{4,0},{5,1},{6,2},{7,3},{8,12},{9,13},{10,... | collective-permute-start | bytes 786440 | tf_op jit(solution)/shard_map/ppermute | solution.py:38
  126.1 14.3 %collective-permute-start.24 = (f32[136,512]{1,0:T(8,128)S(1)}, f32[136,512]{1,0:T(8,128)S(1)}, u32[]{:S(2)}, u32[]{:S(2)}) collective-permute-start(f32[136,512]{1,0:T(8,128)S(1)} %pad_maximum_fusion.3), channel_id=1, source_target_pairs={{0,2},{1,3},{2,0},{3,1},{4,6},{5,7},{6,4},{7,5},{8,10},{9,11},{10,... | collective-permute-start | bytes 835592 | tf_op jit(solution)/shard_map/ppermute | solution.py:38
  127.8 22.8 %collective-permute-start.22 = (f16[64,2176]{1,0:T(8,128)(2,1)S(1)}, f16[64,2176]{1,0:T(8,128)(2,1)S(1)}, u32[]{:S(2)}, u32[]{:S(2)}) collective-permute-start(f16[64,2176]{1,0:T(8,128)(2,1)S(1)} %get-tuple-element.93), channel_id=1, source_target_pairs={{0,24},{1,25},{2,26},{3,27},{4,28},{5,29},{6,30},{7,31},{8,16},{9,... | collective-permute-start | bytes 835592 | tf_op jit(solution)/shard_map/ppermute | solution.py:38
  129.3 21.3 %collective-permute-start.21 = (f16[64,2176]{1,0:T(8,128)(2,1)S(1)}, f16[64,2176]{1,0:T(8,128)(2,1)S(1)}, u32[]{:S(2)}, u32[]{:S(2)}) collective-permute-start(f16[64,2176]{1,0:T(8,128)(2,1)S(1)} %get-tuple-element.94), channel_id=1, source_target_pairs={{0,16},{1,17},{2,18},{3,19},{4,20},{5,21},{6,22},{7,23},{8,24},{9,... | collective-permute-start | bytes 835592 | tf_op jit(solution)/shard_map/ppermute | solution.py:38
  130.2 20.4 %collective-permute-start.20 = (f16[64,2176]{1,0:T(8,128)(2,1)S(1)}, f16[64,2176]{1,0:T(8,128)(2,1)S(1)}, u32[]{:S(2)}, u32[]{:S(2)}) collective-permute-start(f16[64,2176]{1,0:T(8,128)(2,1)S(1)} %get-tuple-element.95), channel_id=1, source_target_pairs={{0,8},{1,9},{2,10},{3,11},{4,12},{5,13},{6,14},{7,15},{8,0},{9,1},... | collective-permute-start | bytes 835592 | tf_op jit(solution)/shard_map/ppermute | solution.py:38
  140.4 7.3 %collective-permute-start.27 = (f32[64,512]{1,0:T(8,128)S(1)}, f32[64,512]{1,0:T(8,128)S(1)}, u32[]{:S(2)}, u32[]{:S(2)}) collective-permute-start(f32[64,512]{1,0:T(8,128)S(1)} %get-tuple-element.51), channel_id=1, source_target_pairs={{0,2},{1,3},{2,0},{3,1},{4,6},{5,7},{6,4},{7,5},{8,10},{9,11},{10,... | collective-permute-start | bytes 393224 | tf_op jit(solution)/shard_map/ppermute | solution.py:38
  140.7 9.8 %collective-permute-start.25 = (f32[72,512]{1,0:T(8,128)S(1)}, f32[72,512]{1,0:T(8,128)S(1)}, u32[]{:S(2)}, u32[]{:S(2)}) collective-permute-start(f32[72,512]{1,0:T(8,128)S(1)} %pad_maximum_fusion.13), channel_id=1, source_target_pairs={{0,4},{1,5},{2,6},{3,7},{4,0},{5,1},{6,2},{7,3},{8,12},{9,13},{10,... | collective-permute-start | bytes 442376 | tf_op jit(solution)/shard_map/ppermute | solution.py:38
  150.7 5.6 %collective-permute-start.28 = (f32[40,512]{1,0:T(8,128)S(1)}, f32[40,512]{1,0:T(8,128)S(1)}, u32[]{:S(2)}, u32[]{:S(2)}) collective-permute-start(f32[40,512]{1,0:T(8,128)S(1)} %get-tuple-element.56), channel_id=1, source_target_pairs={{0,8},{1,9},{2,10},{3,11},{4,12},{5,13},{6,14},{7,15},{8,0},{9,1},... | collective-permute-start | bytes 245768 | tf_op jit(solution)/shard_map/ppermute | solution.py:38
  (19 other events, 185.1 us)

commit v4 on v3

--- a/solution.py
+++ b/solution.py
@@ -42,49 +42,35 @@
     return [1 << i for i in range(nz.bit_length() - 1)]
 
 
-def join(parts, axis=1):
-    return jnp.concatenate(parts, axis=axis)
+def join(parts):
+    return jnp.concatenate(parts, axis=0)
 
 
 def gather_crops(teacher, student):
     batch = lax.axis_size("batch")
     nz = lax.axis_size("proto") // CORES
-    x = jnp.stack([teacher, student])[:, None]
-    pieces = join([x] + [swap(x, o, 0, 0) for o in range(1, batch)])
-    masks = z_masks(nz)
-    held, offsets = [], []
-    for first, order in ((0, masks), (batch // 2, masks[::-1])):
-        now, plan = pieces[:, None, first : first + batch // 2], [0]
-        for mask in order[:-1]:
-            now = join([now, swap(now, 0, mask, 0)])
-            plan = plan + [o ^ mask for o in plan]
-        held.append(now)
-        offsets.append(plan + [o ^ order[-1] for o in plan])
+    both = jnp.stack([teacher, student])
+    passed = [both] + [swap(both, 0, o, 0) for o in range(1, nz)]
     found = []
     for which in range(2):
-        both = []
-        for side, mask in enumerate((masks[-1], masks[0])):
-            half = held[side][which]
-            half = join([half, swap(half, 0, mask, 0)], 0)
-            first = side * (batch // 2)
-            both.append((half, offsets[side], first, 0))
-            both.append((swap(half, 0, 0, 1), offsets[side], first, 1))
-        found.append(both)
+        mine = join([x[which][None] for x in passed])[None]
+        pieces = join([mine] + [swap(mine, o, 0, 0) for o in range(1, batch)])
+        found.append([pieces, swap(pieces, 0, 0, 1)])
     return found
 
 
-def unit_crops_body(plan, at_ref, *refs):
-    pieces, (unit_ref, scale_ref, raw, sems) = refs[: len(plan)], refs[len(plan) :]
+def unit_crops_body(at_ref, *refs):
+    pieces, (unit_ref, scale_ref, raw, sems) = refs[:CORES], refs[CORES:]
     j, z, c = at_ref[0], at_ref[1], at_ref[2]
     copies = []
-    for ref, (offsets, first, core) in zip(pieces, plan):
-        rows, cols = ref.shape[2:]
-        for i, oz in enumerate(offsets):
-            top = pl.multiple_of(((z ^ oz) * CORES + (c ^ core)) * rows, rows)
-            for k in range(ref.shape[1]):
-                left = pl.multiple_of((j ^ (first + k)) * cols, cols)
+    for core, ref in enumerate(pieces):
+        batch, nz, rows, cols = ref.shape
+        for ob in range(batch):
+            left = pl.multiple_of((j ^ ob) * cols, cols)
+            for oz in range(nz):
+                top = pl.multiple_of(((z ^ oz) * CORES + (c ^ core)) * rows, rows)
                 target = raw.at[pl.ds(top, rows), pl.ds(left, cols)]
-                copies.append(pltpu.make_async_copy(ref.at[i, k], target, sems.at[len(copies)]))
+                copies.append(pltpu.make_async_copy(ref.at[ob, oz], target, sems.at[len(copies)]))
                 copies[-1].start()
     for copy in copies:
         copy.wait()
@@ -97,10 +83,9 @@
 
 
 def unit_crops(at, found, width, crops, megabytes):
-    plan = [(offsets, first, core) for _, offsets, first, core in found]
-    copies = sum(piece.shape[0] * piece.shape[1] for piece, *_ in found)
-    return pl.pallas_call(
-        functools.partial(unit_crops_body, plan),
+    copies = CORES * found[0].shape[0] * found[0].shape[1]
+    return pl.pallas_call(
+        unit_crops_body,
         out_shape=(
             jax.ShapeDtypeStruct((width, crops), jnp.bfloat16),
             jax.ShapeDtypeStruct((1, crops), jnp.float32),
@@ -112,7 +97,7 @@
             pltpu.SemaphoreType.DMA((copies,)),
         ],
         compiler_params=params(megabytes),
-    )(at, *[piece for piece, *_ in found])
+    )(at, *found)
 
 
 def unit_protos_body(at_ref, *refs):
@@ -224,101 +209,108 @@
     )(*operands)
 
 
-def grads_body(plan, at_ref, turned_ref, inv_ref, got_ref, before_ref, *refs):
-    nb, nz, rows, chunk, grain = plan
-    teacher_ref, student_ref, crop_scale_ref, crop_out, by_proto, *refs = refs
-    grad_ref, result, protos, inverse, crop_row, total_row, loss_sum = refs
+def prepare_body(grain, turned_ref, inv_ref, got_ref, before_ref, protos, inverse, crop_row, total_row):
+    to_row(crop_row, jnp.log2(before_ref[...] / (received(got_ref, 0) * grain)))
+    to_row(total_row, -jnp.log2(received(got_ref, 1) * grain))
+    count = turned_ref.shape[0]
+    chunk = min(256, count)
+    for low in range(0, count, chunk):
+        part = slice(low, low + chunk)
+        protos[:, part] = turned_ref[part, :].T
+        inverse[part, :] = jnp.broadcast_to(inv_ref[:, part], (128, chunk)).T
+
+
+def prepare(turned, inv, got, before, grain):
+    count, width = turned.shape
+    crops = before.shape[0] * 128
+    return pl.pallas_call(
+        functools.partial(prepare_body, grain),
+        out_shape=[
+            jax.ShapeDtypeStruct((width, count), jnp.bfloat16),
+            jax.ShapeDtypeStruct((count, 128), jnp.float32),
+            jax.ShapeDtypeStruct((1, crops), jnp.float32),
+            jax.ShapeDtypeStruct((1, crops), jnp.float32),
+        ],
+        in_specs=[VMEM] * 4,
+        out_specs=[VMEM] * 4,
+        compiler_params=params(16),
+        name="prepare",
+    )(turned, inv, got, before)
+
+
+def grads_body(plan, at_ref, turned_ref, protos_ref, inverse_ref, *refs):
+    nz, first, blocks, rows, chunk, tile, end = plan
+    if first:
+        before_ref, loss_before_ref, *refs = refs
+    crop_ref, total_ref, teacher_ref, student_ref, crop_scale_ref, crop_out, by_proto, loss_sum, grad_ref, result = refs
     j, z, c = at_ref[0], at_ref[1], at_ref[2]
     count = turned_ref.shape[0]
-    tile = student_ref.shape[1]
-    step = pl.program_id(0)
-
-    @pl.when(step == 0)
-    def _():
-        to_row(crop_row, jnp.log2(before_ref[...] / (received(got_ref, 0) * grain)))
-        to_row(total_row, -jnp.log2(received(got_ref, 1) * grain))
-        loss_sum[...] = jnp.zeros_like(loss_sum)
+    cols = crop_out.shape[2]
+    loss = loss_before_ref[...] if first else jnp.zeros_like(loss_sum)
+    for step in range(blocks * cols // tile):
+        block, within = divmod(step * tile, cols)
+        here = pl.ds(pl.multiple_of((j ^ (first + block)) * cols + within, tile), tile)
+        teacher, student = teacher_ref[:, here], student_ref[:, here]
+        crop, total = crop_ref[:, here], total_ref[:, here]
+        grads = grad_ref.at[step % 2]
         for low in range(0, count, chunk):
             part = slice(low, low + chunk)
-            protos[:, part] = turned_ref[part, :].T
-            inverse[part, :] = jnp.broadcast_to(inv_ref[:, part], (128, chunk)).T
-            by_proto[part, :] = jnp.zeros((chunk, by_proto.shape[1]), jnp.float32)
-
-    inner = crop_row.shape[1] // nb // tile
-    block, within = lax.div(step, inner), lax.rem(step, inner)
-    here = pl.ds(pl.multiple_of(((j ^ block) * inner + within) * tile, tile), tile)
-    loss = loss_sum[...]
-    for low in range(0, count, chunk):
-        part = slice(low, low + chunk)
-        turned = turned_ref[part, :]
-        by_teacher = jnp.dot(turned, teacher_ref[...], preferred_element_type=jnp.float32)
-        by_student = jnp.dot(turned, student_ref[...], preferred_element_type=jnp.float32)
-        inv = jnp.concatenate([inverse[part, :]] * (tile // 128), axis=1)
-        targets = jnp.exp2(by_teacher * T_GAIN + crop_row[:, here]) * inv
-        power = by_student * S_GAIN + total_row[:, here]
-        grad_ref[part, :] = (jnp.exp2(power) - targets).astype(jnp.bfloat16)
-        loss += jnp.sum((targets * power).reshape(chunk // 8, 8, tile), axis=0)
+            turned = turned_ref[part, :]
+            by_teacher = jnp.dot(turned, teacher, preferred_element_type=jnp.float32)
+            by_student = jnp.dot(turned, student, preferred_element_type=jnp.float32)
+            inv = jnp.concatenate([inverse_ref[part, :]] * (tile // 128), axis=1)
+            targets = jnp.exp2(by_teacher * T_GAIN + crop) * inv
+            power = by_student * S_GAIN + total
+            grads[part, :] = (jnp.exp2(power) - targets).astype(jnp.bfloat16)
+            loss += jnp.sum((targets * power).reshape(chunk // 8, 8, tile), axis=0)
+        by_crop = jnp.dot(protos_ref[...], grads[...], preferred_element_type=jnp.float32)
+        values = student.astype(jnp.float32)
+        radial = jnp.sum(values * by_crop, axis=0, keepdims=True)
+        result[step % 2] = (by_crop - values * radial) * crop_scale_ref[:, here]
+        for oc in range(CORES):
+            for oz in range(nz):
+                top = pl.multiple_of(((z ^ oz) * CORES + (c ^ oc)) * rows, rows)
+                low = (oz * blocks + block) * rows
+                crop_out[oc, low : low + rows, within : within + tile] = result[step % 2, pl.ds(top, rows), :]
+        turned_student = student.T
+        for low in range(0, count, chunk):
+            part = slice(low, low + chunk)
+            more = jnp.dot(grads[part, :], turned_student, preferred_element_type=jnp.float32)
+            old = by_proto if step else before_ref if first else None
+            by_proto[part, :] = more if old is None else old[part, :] + more
     loss_sum[...] = loss
-    by_crop = jnp.dot(protos[...], grad_ref[...], preferred_element_type=jnp.float32)
-    student = student_ref[...]
-    values = student.astype(jnp.float32)
-    radial = jnp.sum(values * by_crop, axis=0, keepdims=True)
-    result[...] = (by_crop - values * radial) * crop_scale_ref[...]
-    across = pl.ds(pl.multiple_of(within * tile, tile), tile)
-    for oc in range(CORES):
-        for oz in range(nz):
-            top = pl.multiple_of(((z ^ oz) * CORES + (c ^ oc)) * rows, rows)
-            target = pl.ds(pl.multiple_of((oz * nb + block) * rows, rows), rows)
-            crop_out[oc, target, across] = result[pl.ds(top, rows), :]
-    turned_student = student.T
-    for low in range(0, count, chunk):
-        part = slice(low, low + chunk)
-        by_proto[part, :] += jnp.dot(grad_ref[part, :], turned_student, preferred_element_type=jnp.float32)
-
-    @pl.when(step == pl.num_programs(0) - 1)
-    def _():
-        total = jnp.sum(jnp.sum(loss_sum[...], axis=0, keepdims=True), axis=1, keepdims=True)
+    if end:
+        total = jnp.sum(jnp.sum(loss, axis=0, keepdims=True), axis=1, keepdims=True)
         for oc in range(CORES):
-            crop_out[oc, -8:, :] = jnp.broadcast_to(total, (8, crop_out.shape[2]))
-
-
-def gradients(at, sizes, turned, inv, got, before, teacher, student, crop_scale):
+            crop_out[oc, -8:, :] = jnp.broadcast_to(total, (8, cols))
+
+
+def gradients(at, sizes, group, groups, turned, prepared, sums, teacher, student, crop_scale):
     nb, nz = sizes
     count, width = turned.shape
     crops = teacher.shape[1]
     rows, cols = width // (nz * CORES), crops // nb
+    blocks = nb // groups
     tile = min(256, cols)
-    inner = cols // tile
     chunk = min(256, count)
-
-    def across(height):
-        return pl.BlockSpec((height, tile), lambda i, at_ref: (0, (at_ref[0] ^ (i // inner)) * inner + i % inner))
-
-    fixed = [turned, inv, got, before]
-    return pl.pallas_call(
-        functools.partial(grads_body, (nb, nz, rows, chunk, crops * student_temp)),
-        grid_spec=pltpu.PrefetchScalarGridSpec(
-            num_scalar_prefetch=1,
-            grid=(crops // tile,),
-            in_specs=[VMEM] * len(fixed) + [across(width), across(width), across(1)],
-            out_specs=[VMEM, VMEM],
-            scratch_shapes=[
-                pltpu.VMEM((count, tile), jnp.bfloat16),
-                pltpu.VMEM((width, tile), jnp.float32),
-                pltpu.VMEM((width, count), jnp.bfloat16),
-                pltpu.VMEM((count, 128), jnp.float32),
-                pltpu.VMEM((1, crops), jnp.float32),
-                pltpu.VMEM((1, crops), jnp.float32),
-                pltpu.VMEM((8, tile), jnp.float32),
-            ],
-        ),
+    end = group == groups - 1
+    protos, inverse, crop_row, total_row = prepared
+    operands = [turned, protos, inverse] + list(sums) + [crop_row, total_row, teacher, student, crop_scale]
+    return pl.pallas_call(
+        functools.partial(grads_body, (nz, group * blocks, blocks, rows, chunk, tile, end)),
+        in_specs=[SMEM] + [VMEM] * len(operands),
+        out_specs=[VMEM, VMEM, VMEM],
+        scratch_shapes=[
+            pltpu.VMEM((2, count, tile), jnp.bfloat16),
+            pltpu.VMEM((2, width, tile), jnp.float32),
+        ],
         out_shape=[
-            jax.ShapeDtypeStruct((CORES, nz * nb * rows + 8, cols), jnp.float32),
+            jax.ShapeDtypeStruct((CORES, nz * blocks * rows + 8 * end, cols), jnp.float32),
             jax.ShapeDtypeStruct((count, width), jnp.float32),
-        ],
-        compiler_params=params(),
-        name="gradients",
-    )(at, *fixed, teacher, student, crop_scale)
+            jax.ShapeDtypeStruct((8, tile), jnp.float32),
+        ],
+        compiler_params=params(20),
+    )(at, *operands)
 
 
 def finish_protos_body(nb, at_ref, by_proto, turned_ref, scale_ref, out_ref, top_ref, result):
@@ -405,28 +397,23 @@
     return lax.all_to_all(sent, AXES, 0, 0)
 
 
-def scatter_crops(parts, nz, nb, rows):
+def scatter_crops(parts, nz, rows):
     kept = parts[0] + swap(parts[1], 0, 0, 1)
-    extra = kept[nz * nb * rows :]
-    kept = kept[: nz * nb * rows].reshape(nz, nb * rows, -1)
+    blocks = kept.shape[0] // (nz * rows)
+    size = blocks * rows
+    extra = kept[nz * size :]
+    held = {o: kept[o * size : (o + 1) * size] for o in range(nz)}
     masks = z_masks(nz)
-    size = nb // 2 * rows
-    held = [[kept[o, :size] for o in range(nz)], [kept[o, size:] for o in range(nz)]]
-    for i in range(len(masks)):
-        for side, order in enumerate((masks, masks[::-1])):
-            span = [0]
-            for later in order[i + 1 :]:
-                span = span + [o ^ later for o in span]
-            sent = [held[side][o ^ order[i]] for o in span] + [extra] * (side == 0)
-            got = swap(jnp.concatenate(sent, axis=0), 0, order[i], 0)
-            held[side] = {o: held[side][o] + got[n * size : (n + 1) * size] for n, o in enumerate(span)}
-            if side == 0:
-                more = extra + got[len(span) * size :]
-            if i < len(masks) - 1:
-                held[side] = lax.optimization_barrier(held[side])
-        extra = more
-    mine = [half[0][i * rows : (i + 1) * rows] for half in held for i in range(nb // 2)]
-    return [jnp.concatenate([part, extra], axis=0) for part in mine]
+    for i, mask in enumerate(masks):
+        span = [0]
+        for later in masks[i + 1 :]:
+            span = span + [o ^ later for o in span]
+        sent = [held[o ^ mask] for o in span] + [extra] * bool(extra.shape[0])
+        got = swap(jnp.concatenate(sent, axis=0), 0, mask, 0)
+        held = {o: held[o] + got[n * size : (n + 1) * size] for n, o in enumerate(span)}
+        extra = extra + got[len(span) * size :]
+        held, extra = lax.optimization_barrier((held, extra))
+    return [held[0][i * rows : (i + 1) * rows] for i in range(blocks)], extra
 
 
 def place_body(at_ref, *refs):
@@ -493,8 +480,17 @@
         else:
             got = sum_everywhere(at, sums)
             (softmax_total,) = sweep(S_GAIN, turned, student)
-    crop_parts, by_proto = gradients(at, (nb, nz), turned, inv[0], got, crop, teacher, student, crop_unit_scale)
-    mine = scatter_crops(crop_parts, nz, nb, teacher_emb.shape[0])
+    prepared = prepare(turned, inv[0], got, crop, grain)
+    groups = min(4, nb)
+    mine, sums = [], []
+    for group in range(groups):
+        crop_parts, *sums = gradients(
+            at, (nb, nz), group, groups, turned, prepared, sums, teacher, student, crop_unit_scale
+        )
+        more, extra = scatter_crops(crop_parts, nz, teacher_emb.shape[0])
+        mine += more
+    by_proto = sums[0]
+    mine = [jnp.concatenate([part, extra], axis=0) for part in mine]
     proto_parts, top = finish_protos(at, nb, by_proto, turned, proto_scale)
     power = jnp.ceil(jnp.log2(jnp.maximum(top, 1e-30))) - 15.0
     edge = jnp.broadcast_to(power, (proto_parts.shape[1], 128))

time: 159 us -> 162 us (1.019)
  blocking collectives: 15.6 us -> 26.8 us
  waiting for transfers between devices: 48.9 us -> 43.3 us
  starting transfers between devices: 42.1 us -> 39.4 us
    all_to_all x1 -> x2, blocking collectives: 15.6 us -> 26.8 us  [sum_everywhere(): return lax.all_to_all(sent, AXES, 0, 0)]
    all_to_all x2 -> x1, starting transfers between devices: 8.3 us -> 2.57 us  [sum_everywhere(): return lax.all_to_all(sent, AXES, 0, 0)]
    ppermute x31 -> x36, waiting for transfers between devices: 48.9 us -> 43.3 us  [swap(): return lax.ppermute(x, AXES, pairs)]
    ppermute x31 -> x36, starting transfers between devices: 33.8 us -> 36.8 us  [swap(): return lax.ppermute(x, AXES, pairs)]
    pallas_call x3 -> x7, Pallas kernels: 20.4 us -> 21.2 us  [the longest x4 14.7 us: gradients(): pl.pallas_call(functools.partial(grads_body, (nz, group * blocks, blocks,...]
  transfers between devices with their start and end apart: 33 -> 37, of which waited for: 17 -> 18; matrix products, arithmetic and copies ran while one was open for 1% -> 1% of each run, Pallas kernels for 19% -> 25%
where the time goes in v4:
time: 162 us
  Pallas kernels  45.8 us (28%)
  waiting for transfers between devices  43.3 us (27%)
  starting transfers between devices  39.4 us (24%)
  blocking collectives  26.8 us (17%)
  other arithmetic  2.74 us (2%)
  local copies, waits for them, and re-layouts  2.27 us (1%)
    ppermute x36, waiting for transfers between devices, swap(): return lax.ppermute(x, AXES, pairs)  43.3 us
    ppermute x36, starting transfers between devices, swap(): return lax.ppermute(x, AXES, pairs)  36.8 us
    all_to_all x2, blocking collectives, sum_everywhere(): return lax.all_to_all(sent, AXES, 0, 0)  26.8 us
    pallas_call x4, Pallas kernels, sweep(): pl.pallas_call(functools.partial(sweep_body, gain, weigh, before is not N...  17.2 us
    pallas_call x4, Pallas kernels, gradients(): pl.pallas_call(functools.partial(grads_body, (nz, group * blocks, blocks,...  14.7 us
    pallas_call x2, Pallas kernels, unit_crops(): pl.pallas_call(unit_crops_body, out_shape=(jax.ShapeDtypeStruct((width, c...  5.73 us
  transfers between devices with their start and end apart: 37, of which 18 were waited for; matrix products, arithmetic and copies ran while one was open for 1% of the time, Pallas kernels for 25%

profile of v4, /device:TPU:0, one launch (start us, length us, event | category | flops | bytes accessed | tf_op | source)
XLA Modules:
  0.0 161.6 jit_solution(11060283993966152105)
XLA Ops:
  1.5 3.1 %collective-permute-start.3 = (bf16[2,32,512]{2,1,0:T(8,128)(2,1)S(1)}, bf16[2,32,512]{2,1,0:T(8,128)(2,1)S(1)}, u32[]{:S(2)}, u32[]{:S(2)}) collective-permute-start(bf16[2,32,512]{2,1,0:T(8,128)(2,1)S(1)} %pad_maximum_fusion.14), channel_id=1, source_target_pairs={{0,2},{1,3},{2,0},{3,1},{4,6},{5,7},{6,4},{7,5},{8,10},{9,11},{10,... | collective-permute-start | bytes 196616 | tf_op jit(solution)/shard_map/ppermute | solution.py:38
  4.6 2.6 %collective-permute-start.4 = (bf16[2,32,512]{2,1,0:T(8,128)(2,1)S(1)}, bf16[2,32,512]{2,1,0:T(8,128)(2,1)S(1)}, u32[]{:S(2)}, u32[]{:S(2)}) collective-permute-start(bf16[2,32,512]{2,1,0:T(8,128)(2,1)S(1)} %pad_maximum_fusion.14), channel_id=1, source_target_pairs={{0,4},{1,5},{2,6},{3,7},{4,0},{5,1},{6,2},{7,3},{8,12},{9,13},{10,... | collective-permute-start | bytes 196616 | tf_op jit(solution)/shard_map/ppermute | solution.py:38
  7.2 4.7 %collective-permute-done.4 = bf16[2,32,512]{2,1,0:T(8,128)(2,1)S(1)} collective-permute-done((bf16[2,32,512]{2,1,0:T(8,128)(2,1)S(1)}, bf16[2,32,512]{2,1,0:T(8,128)(2,1)S(1)}, u32[]{:S(2)}, u32[]{:S(2)}) %collective-permute-start.4) | collective-permute-done | bytes 65568 | tf_op jit(solution)/shard_map/ppermute | solution.py:38
  17.7 2.4 %collective-permute-done.6 = bf16[1,4,32,512]{3,2,1,0:T(8,128)(2,1)S(1)} collective-permute-done((bf16[1,4,32,512]{3,2,1,0:T(8,128)(2,1)S(1)}, bf16[1,4,32,512]{3,2,1,0:T(8,128)(2,1)S(1)}, u32[]{:S(2)}, u32[]{:S(2)}) %collective-permute-start.6) | collective-permute-done | bytes 131104 | tf_op jit(solution)/shard_map/ppermute | solution.py:38
  24.4 2.4 %collective-permute-start.2 = (bf16[64,2048]{1,0:T(8,128)(2,1)S(1)}, bf16[64,2048]{1,0:T(8,128)(2,1)S(1)}, u32[]{:S(2)}, u32[]{:S(2)}) collective-permute-start(bf16[64,2048]{1,0:T(8,128)(2,1)S(1)} %get-tuple-element.113), channel_id=1, source_target_pairs={{0,24},{1,25},{2,26},{3,27},{4,28},{5,29},{6,30},{7,31},{8,16},{9,... | collective-permute-start | bytes 786440 | tf_op jit(solution)/shard_map/ppermute | solution.py:38
  27.5 5.1 %collective-permute-done.refs_1_ = bf16[64,2048]{1,0:T(8,128)(2,1)S(1)} collective-permute-done((bf16[64,2048]{1,0:T(8,128)(2,1)S(1)}, bf16[64,2048]{1,0:T(8,128)(2,1)S(1)}, u32[]{:S(2)}, u32[]{:S(2)}) %collective-permute-start) | collective-permute-done | bytes 262176 | tf_op jit(solution)/shard_map/ppermute | solution.py:38
  33.3 6.7 %collective-permute-start.14 = (bf16[1,4,32,512]{3,2,1,0:T(8,128)(2,1)S(1)}, bf16[1,4,32,512]{3,2,1,0:T(8,128)(2,1)S(1)}, u32[]{:S(2)}, u32[]{:S(2)}) collective-permute-start(bf16[1,4,32,512]{3,2,1,0:T(8,128)(2,1)S(1)} %maximum_bitcast_fusion.1), channel_id=1, source_target_pairs={{0,24},{1,25},{2,26},{3,27},{4,28},{5,29},{6,30},{7,31},{8,16},{9,... | collective-permute-start | bytes 393224 | tf_op jit(solution)/shard_map/ppermute | solution.py:38
  43.3 4.4 %shard_map.59.refs_0_ = f32[16,128]{1,0:T(8,128)S(1)} custom-call(bf16[2048,256]{1,0:T(8,128)(2,1)S(1)} %get-tuple-element.57.turned_ref, bf16[256,2048]{1,0:T(8,128)(2,1)S(1)} %get-tuple-element.58.unit_ref.refs_2_.refs_4_), custom_call_target="tpu_custom_call" | custom-call | tf_op jit(solution)/shard_map/pallas_call | solution.py:202
  49.5 11.2 %all_to_all.15.refs_0_ = f32[32,1,8,128]{3,2,1,0:T(8,128)S(1)} all-to-all(f32[32,1,8,128]{3,2,1,0:T(8,128)S(1)} %pack.3), channel_id=1, replica_groups=mesh['batch'=4,'proto'=8] {'batch','proto'}, dimensions={0} | all-to-all | bytes 262144 | tf_op jit(solution)/shard_map/all_to_all | solution.py:397
  60.7 4.8 %shard_map.60 = (f32[16,128]{1,0:T(8,128)S(1)}, f32[16,128]{1,0:T(8,128)S(1)}) custom-call(bf16[2048,256]{1,0:T(8,128)(2,1)S(1)} %get-tuple-element.57.turned_ref, bf16[256,2048]{1,0:T(8,128)(2,1)S(1)} %get-tuple-element.58.unit_ref.refs_2_.refs_4_, f32[32,1,8,128]{3,2,1,0:T(8,128)S(1)} %all_to_all.15.refs_0_), custom_call_target="tpu_custom_call" | custom-call | tf_op jit(solution)/shard_map/pallas_call | solution.py:202
  67.9 2.6 %all-to-all-start.1 = ((f32[32,1,8,128]{3,2,1,0:T(8,128)}), f32[32,1,8,128]{3,2,1,0:T(8,128)S(1)}, u32[]{:S(2)}, u32[]{:S(2)}) async-start(f32[32,1,8,128]{3,2,1,0:T(8,128)} %pack.4), calls=%async_computation.1 | async-start | bytes 262144 | tf_op jit(solution)/shard_map/all_to_all | solution.py:397
  71.3 3.5 %shard_map.62 = (bf16[256,2048]{1,0:T(8,128)(2,1)}, f32[1,2048]{1,0:T(1,128)}) custom-call(s32[3]{0:T(128)} %copy-done.3, bf16[4,4,32,512]{3,2,1,0:T(8,128)(2,1)} %copy-done.5, bf16[4,4,32,512]{3,2,1,0:T(8,128)(2,1)} %copy-done.7), custom_call_target="tpu_custom_call" | custom-call | tf_op jit(solution)/shard_map/pallas_call | solution.py:87
  76.0 2.9 %shard_map.63.refs_1_ = f32[16,128]{1,0:T(8,128)S(1)} custom-call(bf16[2048,256]{1,0:T(8,128)(2,1)S(1)} %get-tuple-element.57.turned_ref, bf16[256,2048]{1,0:T(8,128)(2,1)S(1)} %copy-done), custom_call_target="tpu_custom_call" | custom-call | tf_op jit(solution)/shard_map/pallas_call | solution.py:202
  79.1 5.1 %shard_map.61 = (f32[16,128]{1,0:T(8,128)S(1)}, f32[16,128]{1,0:T(8,128)S(1)}, f32[1,2048]{1,0:T(1,128)S(1)}) custom-call(bf16[2048,256]{1,0:T(8,128)(2,1)S(1)} %get-tuple-element.57.turned_ref, bf16[256,2048]{1,0:T(8,128)(2,1)S(1)} %get-tuple-element.58.unit_ref.refs_2_.refs_4_, f32[32,1,8,128]{3,2,1,0:T(8,128)S(1)} %all-to-all-done.1.refs_0_, ...), custom_call_target="tpu_custom_call" | custom-call | tf_op jit(solution)/shard_map/pallas_call | solution.py:202
  86.1 15.6 %all_to_all.16.got_ref = f32[32,2,8,128]{3,2,1,0:T(8,128)S(1)} all-to-all(f32[32,2,8,128]{3,2,1,0:T(8,128)S(1)} %pack.5), channel_id=1, replica_groups=mesh['batch'=4,'proto'=8] {'batch','proto'}, dimensions={0} | all-to-all | bytes 524288 | tf_op jit(solution)/shard_map/all_to_all | solution.py:397
  102.5 3.5 %shard_map.64 = (f32[2,128,512]{2,1,0:T(8,128)S(1)}, f32[2048,256]{1,0:T(8,128)S(1)}, f32[8,256]{1,0:T(8,128)S(1)}) custom-call(s32[3]{0:T(128)S(1)} %copy-done.4, bf16[2048,256]{1,0:T(8,128)(2,1)S(1)} %get-tuple-element.57.turned_ref, bf16[256,2048]{1,0:T(8,128)(2,1)S(1)} %get-tuple-element.65.protos_ref, f32[2048,128]{1,0:T(8,128)S(1)} %get-tuple-element.66.inverse_ref, ...), custom_call_target="tpu_custom_call" | custom-call | tf_op jit(solution)/shard_map/pallas_call | solution.py:299
  106.8 3.6 %shard_map.65 = (f32[2,128,512]{2,1,0:T(8,128)S(1)}, f32[2048,256]{1,0:T(8,128)S(1)}, f32[8,256]{1,0:T(8,128)S(1)}) custom-call(s32[3]{0:T(128)S(1)} %copy-done.4, bf16[2048,256]{1,0:T(8,128)(2,1)S(1)} %get-tuple-element.57.turned_ref, bf16[256,2048]{1,0:T(8,128)(2,1)S(1)} %get-tuple-element.65.protos_ref, f32[2048,128]{1,0:T(8,128)S(1)} %get-tuple-element.66.inverse_ref, ...), custom_call_target="tpu_custom_call" | custom-call | tf_op jit(solution)/shard_map/pallas_call | solution.py:299
  110.5 3.6 %shard_map.66 = (f32[2,128,512]{2,1,0:T(8,128)S(1)}, f32[2048,256]{1,0:T(8,128)S(1)}, f32[8,256]{1,0:T(8,128)S(1)}) custom-call(s32[3]{0:T(128)S(1)} %copy-done.4, bf16[2048,256]{1,0:T(8,128)(2,1)S(1)} %get-tuple-element.57.turned_ref, bf16[256,2048]{1,0:T(8,128)(2,1)S(1)} %get-tuple-element.65.protos_ref, f32[2048,128]{1,0:T(8,128)S(1)} %get-tuple-element.66.inverse_ref, ...), custom_call_target="tpu_custom_call" | custom-call | tf_op jit(solution)/shard_map/pallas_call | solution.py:299
  114.8 3.9 %shard_map.67 = (f32[2,136,512]{2,1,0:T(8,128)S(1)}, f32[2048,256]{1,0:T(8,128)S(1)}, f32[8,256]{1,0:T(8,128)}) custom-call(s32[3]{0:T(128)S(1)} %copy-done.4, bf16[2048,256]{1,0:T(8,128)(2,1)S(1)} %get-tuple-element.57.turned_ref, bf16[256,2048]{1,0:T(8,128)(2,1)S(1)} %get-tuple-element.65.protos_ref, f32[2048,128]{1,0:T(8,128)S(1)} %get-tuple-element.66.inverse_ref, ...), custom_call_target="tpu_custom_call" | custom-call | tf_op jit(solution)/shard_map/pallas_call | solution.py:299
  130.7 4.7 %collective-permute-done.28 = f32[64,512]{1,0:T(8,128)S(1)} collective-permute-done((f32[64,512]{1,0:T(8,128)S(1)}, f32[64,512]{1,0:T(8,128)S(1)}, u32[]{:S(2)}, u32[]{:S(2)}) %collective-permute-start.28) | collective-permute-done | bytes 131104 | tf_op jit(solution)/shard_map/ppermute | solution.py:38
  135.5 3.0 %collective-permute-done.25 = f32[72,512]{1,0:T(8,128)S(1)} collective-permute-done((f32[72,512]{1,0:T(8,128)S(1)}, f32[72,512]{1,0:T(8,128)S(1)}, u32[]{:S(2)}, u32[]{:S(2)}) %collective-permute-start.25) | collective-permute-done | bytes 147488 | tf_op jit(solution)/shard_map/ppermute | solution.py:38
  140.1 2.4 %collective-permute-start.20 = (f16[64,2176]{1,0:T(8,128)(2,1)S(1)}, f16[64,2176]{1,0:T(8,128)(2,1)S(1)}, u32[]{:S(2)}, u32[]{:S(2)}) collective-permute-start(f16[64,2176]{1,0:T(8,128)(2,1)S(1)} %get-tuple-element.141), channel_id=1, source_target_pairs={{0,24},{1,25},{2,26},{3,27},{4,28},{5,29},{6,30},{7,31},{8,16},{9,... | collective-permute-start | bytes 835592 | tf_op jit(solution)/shard_map/ppermute | solution.py:38
  144.4 4.0 %collective-permute-done.18 = f16[64,2176]{1,0:T(8,128)(2,1)S(1)} collective-permute-done((f16[64,2176]{1,0:T(8,128)(2,1)S(1)}, f16[64,2176]{1,0:T(8,128)(2,1)S(1)}, u32[]{:S(2)}, u32[]{:S(2)}) %collective-permute-start.18) | collective-permute-done | bytes 278560 | tf_op jit(solution)/shard_map/ppermute | solution.py:38
  148.4 5.1 %collective-permute-done.19 = f16[64,2176]{1,0:T(8,128)(2,1)S(1)} collective-permute-done((f16[64,2176]{1,0:T(8,128)(2,1)S(1)}, f16[64,2176]{1,0:T(8,128)(2,1)S(1)}, u32[]{:S(2)}, u32[]{:S(2)}) %collective-permute-start.19) | collective-permute-done | bytes 278560 | tf_op jit(solution)/shard_map/ppermute | solution.py:38
  (134 shorter events, 49.3 us)
Async XLA Ops:
  4.6 7.3 %collective-permute-start.4 = (bf16[2,32,512]{2,1,0:T(8,128)(2,1)S(1)}, bf16[2,32,512]{2,1,0:T(8,128)(2,1)S(1)}, u32[]{:S(2)}, u32[]{:S(2)}) collective-permute-start(bf16[2,32,512]{2,1,0:T(8,128)(2,1)S(1)} %pad_maximum_fusion.14), channel_id=1, source_target_pairs={{0,4},{1,5},{2,6},{3,7},{4,0},{5,1},{6,2},{7,3},{8,12},{9,13},{10,... | collective-permute-start | bytes 196616 | tf_op jit(solution)/shard_map/ppermute | solution.py:38
  7.2 6.1 %collective-permute-start.5 = (bf16[2,32,512]{2,1,0:T(8,128)(2,1)S(1)}, bf16[2,32,512]{2,1,0:T(8,128)(2,1)S(1)}, u32[]{:S(2)}, u32[]{:S(2)}) collective-permute-start(bf16[2,32,512]{2,1,0:T(8,128)(2,1)S(1)} %pad_maximum_fusion.14), channel_id=1, source_target_pairs={{0,6},{1,7},{2,4},{3,5},{4,2},{5,3},{6,0},{7,1},{8,14},{9,15},{10,... | collective-permute-start | bytes 196616 | tf_op jit(solution)/shard_map/ppermute | solution.py:38
  23.1 18.0 %collective-permute-start.9 = (bf16[4,4,32,512]{3,2,1,0:T(8,128)(2,1)S(1)}, bf16[4,4,32,512]{3,2,1,0:T(8,128)(2,1)S(1)}, u32[]{:S(2)}, u32[]{:S(2)}) collective-permute-start(bf16[4,4,32,512]{3,2,1,0:T(8,128)(2,1)S(1)} %pad_maximum_fusion.refs_0_), channel_id=1, source_target_pairs={{0,1},{1,0},{2,3},{3,2},{4,5},{5,4},{6,7},{7,6},{8,9},{9,8},{10,11... | collective-permute-start | bytes 1572872 | tf_op jit(solution)/shard_map/ppermute | solution.py:38
  23.3 9.2 %collective-permute-start = (bf16[64,2048]{1,0:T(8,128)(2,1)S(1)}, bf16[64,2048]{1,0:T(8,128)(2,1)S(1)}, u32[]{:S(2)}, u32[]{:S(2)}) collective-permute-start(bf16[64,2048]{1,0:T(8,128)(2,1)S(1)} %get-tuple-element.115), channel_id=1, source_target_pairs={{0,8},{1,9},{2,10},{3,11},{4,12},{5,13},{6,14},{7,15},{8,0},{9,1},... | collective-permute-start | bytes 786440 | tf_op jit(solution)/shard_map/ppermute | solution.py:38
  23.9 9.4 %collective-permute-start.1 = (bf16[64,2048]{1,0:T(8,128)(2,1)S(1)}, bf16[64,2048]{1,0:T(8,128)(2,1)S(1)}, u32[]{:S(2)}, u32[]{:S(2)}) collective-permute-start(bf16[64,2048]{1,0:T(8,128)(2,1)S(1)} %get-tuple-element.114), channel_id=1, source_target_pairs={{0,16},{1,17},{2,18},{3,19},{4,20},{5,21},{6,22},{7,23},{8,24},{9,... | collective-permute-start | bytes 786440 | tf_op jit(solution)/shard_map/ppermute | solution.py:38
  24.4 15.6 %collective-permute-start.2 = (bf16[64,2048]{1,0:T(8,128)(2,1)S(1)}, bf16[64,2048]{1,0:T(8,128)(2,1)S(1)}, u32[]{:S(2)}, u32[]{:S(2)}) collective-permute-start(bf16[64,2048]{1,0:T(8,128)(2,1)S(1)} %get-tuple-element.113), channel_id=1, source_target_pairs={{0,24},{1,25},{2,26},{3,27},{4,28},{5,29},{6,30},{7,31},{8,16},{9,... | collective-permute-start | bytes 786440 | tf_op jit(solution)/shard_map/ppermute | solution.py:38
  26.9 20.9 %collective-permute-start.12 = (bf16[1,4,32,512]{3,2,1,0:T(8,128)(2,1)S(1)}, bf16[1,4,32,512]{3,2,1,0:T(8,128)(2,1)S(1)}, u32[]{:S(2)}, u32[]{:S(2)}) collective-permute-start(bf16[1,4,32,512]{3,2,1,0:T(8,128)(2,1)S(1)} %maximum_bitcast_fusion.1), channel_id=1, source_target_pairs={{0,8},{1,9},{2,10},{3,11},{4,12},{5,13},{6,14},{7,15},{8,0},{9,1},... | collective-permute-start | bytes 393224 | tf_op jit(solution)/shard_map/ppermute | solution.py:38
  32.5 15.3 %collective-permute-start.13 = (bf16[1,4,32,512]{3,2,1,0:T(8,128)(2,1)S(1)}, bf16[1,4,32,512]{3,2,1,0:T(8,128)(2,1)S(1)}, u32[]{:S(2)}, u32[]{:S(2)}) collective-permute-start(bf16[1,4,32,512]{3,2,1,0:T(8,128)(2,1)S(1)} %maximum_bitcast_fusion.1), channel_id=1, source_target_pairs={{0,16},{1,17},{2,18},{3,19},{4,20},{5,21},{6,22},{7,23},{8,24},{9,... | collective-permute-start | bytes 393224 | tf_op jit(solution)/shard_map/ppermute | solution.py:38
  33.3 14.5 %collective-permute-start.14 = (bf16[1,4,32,512]{3,2,1,0:T(8,128)(2,1)S(1)}, bf16[1,4,32,512]{3,2,1,0:T(8,128)(2,1)S(1)}, u32[]{:S(2)}, u32[]{:S(2)}) collective-permute-start(bf16[1,4,32,512]{3,2,1,0:T(8,128)(2,1)S(1)} %maximum_bitcast_fusion.1), channel_id=1, source_target_pairs={{0,24},{1,25},{2,26},{3,27},{4,28},{5,29},{6,30},{7,31},{8,16},{9,... | collective-permute-start | bytes 393224 | tf_op jit(solution)/shard_map/ppermute | solution.py:38
  47.9 22.6 %collective-permute-start.15 = (bf16[4,4,32,512]{3,2,1,0:T(8,128)(2,1)S(1)}, bf16[4,4,32,512]{3,2,1,0:T(8,128)(2,1)S(1)}, u32[]{:S(2)}, u32[]{:S(2)}) collective-permute-start(bf16[4,4,32,512]{3,2,1,0:T(8,128)(2,1)S(1)} %pad_maximum_fusion.1.refs_0_), channel_id=1, source_target_pairs={{0,1},{1,0},{2,3},{3,2},{4,5},{5,4},{6,7},{7,6},{8,9},{9,8},{10,11... | collective-permute-start | bytes 1572872 | tf_op jit(solution)/shard_map/ppermute | solution.py:38
  67.9 11.2 %all-to-all-start.1 = ((f32[32,1,8,128]{3,2,1,0:T(8,128)}), f32[32,1,8,128]{3,2,1,0:T(8,128)S(1)}, u32[]{:S(2)}, u32[]{:S(2)}) async-start(f32[32,1,8,128]{3,2,1,0:T(8,128)} %pack.4), calls=%async_computation.1 | async-start | bytes 262144 | tf_op jit(solution)/shard_map/all_to_all | solution.py:397
  106.0 14.7 %collective-permute-start.21 = (f32[128,512]{1,0:T(8,128)S(1)}, f32[128,512]{1,0:T(8,128)S(1)}, u32[]{:S(2)}, u32[]{:S(2)}) collective-permute-start(f32[128,512]{1,0:T(8,128)S(1)} %slice_bitcast_fusion.4), channel_id=1, source_target_pairs={{0,1},{1,0},{2,3},{3,2},{4,5},{5,4},{6,7},{7,6},{8,9},{9,8},{10,11... | collective-permute-start | bytes 786440 | tf_op jit(solution)/shard_map/ppermute | solution.py:38
  114.2 7.3 %collective-permute-start.30 = (f32[128,512]{1,0:T(8,128)S(1)}, f32[128,512]{1,0:T(8,128)S(1)}, u32[]{:S(2)}, u32[]{:S(2)}) collective-permute-start(f32[128,512]{1,0:T(8,128)S(1)} %slice_bitcast_fusion.2), channel_id=1, source_target_pairs={{0,1},{1,0},{2,3},{3,2},{4,5},{5,4},{6,7},{7,6},{8,9},{9,8},{10,11... | collective-permute-start | bytes 786440 | tf_op jit(solution)/shard_map/ppermute | solution.py:38
  114.3 8.8 %collective-permute-start.27 = (f32[128,512]{1,0:T(8,128)S(1)}, f32[128,512]{1,0:T(8,128)S(1)}, u32[]{:S(2)}, u32[]{:S(2)}) collective-permute-start(f32[128,512]{1,0:T(8,128)S(1)} %slice_bitcast_fusion.3), channel_id=1, source_target_pairs={{0,1},{1,0},{2,3},{3,2},{4,5},{5,4},{6,7},{7,6},{8,9},{9,8},{10,11... | collective-permute-start | bytes 786440 | tf_op jit(solution)/shard_map/ppermute | solution.py:38
  120.9 6.4 %collective-permute-start.22 = (f32[64,512]{1,0:T(8,128)S(1)}, f32[64,512]{1,0:T(8,128)S(1)}, u32[]{:S(2)}, u32[]{:S(2)}) collective-permute-start(f32[64,512]{1,0:T(8,128)S(1)} %pad_maximum_fusion.10), channel_id=1, source_target_pairs={{0,2},{1,3},{2,0},{3,1},{4,6},{5,7},{6,4},{7,5},{8,10},{9,11},{10,... | collective-permute-start | bytes 393224 | tf_op jit(solution)/shard_map/ppermute | solution.py:38
  121.5 8.6 %collective-permute-start.31 = (f32[64,512]{1,0:T(8,128)S(1)}, f32[64,512]{1,0:T(8,128)S(1)}, u32[]{:S(2)}, u32[]{:S(2)}) collective-permute-start(f32[64,512]{1,0:T(8,128)S(1)} %pad_maximum_fusion.12), channel_id=1, source_target_pairs={{0,2},{1,3},{2,0},{3,1},{4,6},{5,7},{6,4},{7,5},{8,10},{9,11},{10,... | collective-permute-start | bytes 393224 | tf_op jit(solution)/shard_map/ppermute | solution.py:38
  123.2 12.2 %collective-permute-start.28 = (f32[64,512]{1,0:T(8,128)S(1)}, f32[64,512]{1,0:T(8,128)S(1)}, u32[]{:S(2)}, u32[]{:S(2)}) collective-permute-start(f32[64,512]{1,0:T(8,128)S(1)} %pad_maximum_fusion.11), channel_id=1, source_target_pairs={{0,2},{1,3},{2,0},{3,1},{4,6},{5,7},{6,4},{7,5},{8,10},{9,11},{10,... | collective-permute-start | bytes 393224 | tf_op jit(solution)/shard_map/ppermute | solution.py:38
  123.8 14.6 %collective-permute-start.25 = (f32[72,512]{1,0:T(8,128)S(1)}, f32[72,512]{1,0:T(8,128)S(1)}, u32[]{:S(2)}, u32[]{:S(2)}) collective-permute-start(f32[72,512]{1,0:T(8,128)S(1)} %pad_maximum_fusion.9), channel_id=1, source_target_pairs={{0,2},{1,3},{2,0},{3,1},{4,6},{5,7},{6,4},{7,5},{8,10},{9,11},{10,... | collective-permute-start | bytes 442376 | tf_op jit(solution)/shard_map/ppermute | solution.py:38
  127.3 12.4 %collective-permute-start.23 = (f32[32,512]{1,0:T(8,128)S(1)}, f32[32,512]{1,0:T(8,128)S(1)}, u32[]{:S(2)}, u32[]{:S(2)}) collective-permute-start(f32[32,512]{1,0:T(8,128)S(1)} %get-tuple-element.82), channel_id=1, source_target_pairs={{0,4},{1,5},{2,6},{3,7},{4,0},{5,1},{6,2},{7,3},{8,12},{9,13},{10,... | collective-permute-start | bytes 196616 | tf_op jit(solution)/shard_map/ppermute | solution.py:38
  130.2 9.9 %collective-permute-start.32 = (f32[32,512]{1,0:T(8,128)S(1)}, f32[32,512]{1,0:T(8,128)S(1)}, u32[]{:S(2)}, u32[]{:S(2)}) collective-permute-start(f32[32,512]{1,0:T(8,128)S(1)} %get-tuple-element.95), channel_id=1, source_target_pairs={{0,4},{1,5},{2,6},{3,7},{4,0},{5,1},{6,2},{7,3},{8,12},{9,13},{10,... | collective-permute-start | bytes 196616 | tf_op jit(solution)/shard_map/ppermute | solution.py:38
  135.4 7.1 %collective-permute-start.29 = (f32[32,512]{1,0:T(8,128)S(1)}, f32[32,512]{1,0:T(8,128)S(1)}, u32[]{:S(2)}, u32[]{:S(2)}) collective-permute-start(f32[32,512]{1,0:T(8,128)S(1)} %get-tuple-element.91), channel_id=1, source_target_pairs={{0,4},{1,5},{2,6},{3,7},{4,0},{5,1},{6,2},{7,3},{8,12},{9,13},{10,... | collective-permute-start | bytes 196616 | tf_op jit(solution)/shard_map/ppermute | solution.py:38
  138.8 9.6 %collective-permute-start.18 = (f16[64,2176]{1,0:T(8,128)(2,1)S(1)}, f16[64,2176]{1,0:T(8,128)(2,1)S(1)}, u32[]{:S(2)}, u32[]{:S(2)}) collective-permute-start(f16[64,2176]{1,0:T(8,128)(2,1)S(1)} %get-tuple-element.143), channel_id=1, source_target_pairs={{0,8},{1,9},{2,10},{3,11},{4,12},{5,13},{6,14},{7,15},{8,0},{9,1},... | collective-permute-start | bytes 835592 | tf_op jit(solution)/shard_map/ppermute | solution.py:38
  139.7 13.8 %collective-permute-start.19 = (f16[64,2176]{1,0:T(8,128)(2,1)S(1)}, f16[64,2176]{1,0:T(8,128)(2,1)S(1)}, u32[]{:S(2)}, u32[]{:S(2)}) collective-permute-start(f16[64,2176]{1,0:T(8,128)(2,1)S(1)} %get-tuple-element.142), channel_id=1, source_target_pairs={{0,16},{1,17},{2,18},{3,19},{4,20},{5,21},{6,22},{7,23},{8,24},{9,... | collective-permute-start | bytes 835592 | tf_op jit(solution)/shard_map/ppermute | solution.py:38
  140.1 13.5 %collective-permute-start.20 = (f16[64,2176]{1,0:T(8,128)(2,1)S(1)}, f16[64,2176]{1,0:T(8,128)(2,1)S(1)}, u32[]{:S(2)}, u32[]{:S(2)}) collective-permute-start(f16[64,2176]{1,0:T(8,128)(2,1)S(1)} %get-tuple-element.141), channel_id=1, source_target_pairs={{0,24},{1,25},{2,26},{3,27},{4,28},{5,29},{6,30},{7,31},{8,16},{9,... | collective-permute-start | bytes 835592 | tf_op jit(solution)/shard_map/ppermute | solution.py:38
  (22 other events, 237.6 us)

commit v5 on v4

--- a/solution.py
+++ b/solution.py
@@ -128,7 +128,7 @@
         out_specs=(VMEM, VMEM),
         scratch_shapes=[pltpu.VMEM((width, min(512, protos)), jnp.bfloat16)],
         compiler_params=params(),
-        name="unit_protos",
+        name="up",
     )(at, *blocks)
 
 
@@ -234,7 +234,7 @@
         in_specs=[VMEM] * 4,
         out_specs=[VMEM] * 4,
         compiler_params=params(16),
-        name="prepare",
+        name="pr",
     )(turned, inv, got, before)
 
 
@@ -344,7 +344,7 @@
         out_specs=[VMEM, VMEM],
         scratch_shapes=[pltpu.VMEM((width, min(256, count)), jnp.float32)],
         compiler_params=params(),
-        name="finish_protos",
+        name="fp",
     )(at, by_proto, turned, scale)
 
 
@@ -369,7 +369,7 @@
         in_specs=[VMEM] * len(parts),
         out_specs=[VMEM, VMEM],
         compiler_params=params(4),
-        name="finish_crops",
+        name="fc",
     )(*parts)
 
 
@@ -392,7 +392,7 @@
         in_specs=[SMEM] + [VMEM] * (2 * len(tiles)),
         out_specs=VMEM,
         compiler_params=params(),
-        name="pack",
+        name="pk",
     )(at, *tiles, *theirs)
     return lax.all_to_all(sent, AXES, 0, 0)
 
@@ -445,7 +445,7 @@
             pltpu.SemaphoreType.DMA((len(parts),)),
         ],
         compiler_params=params(16),
-        name="place",
+        name="pl",
     )(at, *parts)
 
 

time: 162 us -> 162 us (level)
  no operation moved by 1% of the time
where the time goes in v5:
time: 162 us
  Pallas kernels  45.8 us (28%)
  waiting for transfers between devices  43.3 us (27%)
  starting transfers between devices  39.4 us (24%)
  blocking collectives  26.8 us (17%)
  other arithmetic  2.74 us (2%)
  local copies, waits for them, and re-layouts  2.27 us (1%)
    ppermute x36, waiting for transfers between devices, swap(): return lax.ppermute(x, AXES, pairs)  43.3 us
    ppermute x36, starting transfers between devices, swap(): return lax.ppermute(x, AXES, pairs)  36.8 us
    all_to_all x2, blocking collectives, sum_everywhere(): return lax.all_to_all(sent, AXES, 0, 0)  26.8 us
    pallas_call x4, Pallas kernels, sweep(): pl.pallas_call(functools.partial(sweep_body, gain, weigh, before is not N...  17.2 us
    pallas_call x4, Pallas kernels, gradients(): pl.pallas_call(functools.partial(grads_body, (nz, group * blocks, blocks,...  14.7 us
    pallas_call x2, Pallas kernels, unit_crops(): pl.pallas_call(unit_crops_body, out_shape=(jax.ShapeDtypeStruct((width, c...  5.73 us
  transfers between devices with their start and end apart: 37, of which 18 were waited for; matrix products, arithmetic and copies ran while one was open for 1% of the time, Pallas kernels for 25%

profile of v5, /device:TPU:0, one launch (start us, length us, event | category | flops | bytes accessed | tf_op | source)
XLA Modules:
  0.0 161.6 jit_solution(11060283993966152105)
XLA Ops:
  1.5 3.1 %collective-permute-start.3 = (bf16[2,32,512]{2,1,0:T(8,128)(2,1)S(1)}, bf16[2,32,512]{2,1,0:T(8,128)(2,1)S(1)}, u32[]{:S(2)}, u32[]{:S(2)}) collective-permute-start(bf16[2,32,512]{2,1,0:T(8,128)(2,1)S(1)} %pad_maximum_fusion.14), channel_id=1, source_target_pairs={{0,2},{1,3},{2,0},{3,1},{4,6},{5,7},{6,4},{7,5},{8,10},{9,11},{10,... | collective-permute-start | bytes 196616 | tf_op jit(solution)/shard_map/ppermute | solution.py:38
  4.6 2.6 %collective-permute-start.4 = (bf16[2,32,512]{2,1,0:T(8,128)(2,1)S(1)}, bf16[2,32,512]{2,1,0:T(8,128)(2,1)S(1)}, u32[]{:S(2)}, u32[]{:S(2)}) collective-permute-start(bf16[2,32,512]{2,1,0:T(8,128)(2,1)S(1)} %pad_maximum_fusion.14), channel_id=1, source_target_pairs={{0,4},{1,5},{2,6},{3,7},{4,0},{5,1},{6,2},{7,3},{8,12},{9,13},{10,... | collective-permute-start | bytes 196616 | tf_op jit(solution)/shard_map/ppermute | solution.py:38
  7.2 4.7 %collective-permute-done.4 = bf16[2,32,512]{2,1,0:T(8,128)(2,1)S(1)} collective-permute-done((bf16[2,32,512]{2,1,0:T(8,128)(2,1)S(1)}, bf16[2,32,512]{2,1,0:T(8,128)(2,1)S(1)}, u32[]{:S(2)}, u32[]{:S(2)}) %collective-permute-start.4) | collective-permute-done | bytes 65568 | tf_op jit(solution)/shard_map/ppermute | solution.py:38
  17.7 2.4 %collective-permute-done.6 = bf16[1,4,32,512]{3,2,1,0:T(8,128)(2,1)S(1)} collective-permute-done((bf16[1,4,32,512]{3,2,1,0:T(8,128)(2,1)S(1)}, bf16[1,4,32,512]{3,2,1,0:T(8,128)(2,1)S(1)}, u32[]{:S(2)}, u32[]{:S(2)}) %collective-permute-start.6) | collective-permute-done | bytes 131104 | tf_op jit(solution)/shard_map/ppermute | solution.py:38
  24.4 2.4 %collective-permute-start.2 = (bf16[64,2048]{1,0:T(8,128)(2,1)S(1)}, bf16[64,2048]{1,0:T(8,128)(2,1)S(1)}, u32[]{:S(2)}, u32[]{:S(2)}) collective-permute-start(bf16[64,2048]{1,0:T(8,128)(2,1)S(1)} %get-tuple-element.113), channel_id=1, source_target_pairs={{0,24},{1,25},{2,26},{3,27},{4,28},{5,29},{6,30},{7,31},{8,16},{9,... | collective-permute-start | bytes 786440 | tf_op jit(solution)/shard_map/ppermute | solution.py:38
  27.5 5.1 %collective-permute-done.refs_1_ = bf16[64,2048]{1,0:T(8,128)(2,1)S(1)} collective-permute-done((bf16[64,2048]{1,0:T(8,128)(2,1)S(1)}, bf16[64,2048]{1,0:T(8,128)(2,1)S(1)}, u32[]{:S(2)}, u32[]{:S(2)}) %collective-permute-start) | collective-permute-done | bytes 262176 | tf_op jit(solution)/shard_map/ppermute | solution.py:38
  33.3 6.7 %collective-permute-start.14 = (bf16[1,4,32,512]{3,2,1,0:T(8,128)(2,1)S(1)}, bf16[1,4,32,512]{3,2,1,0:T(8,128)(2,1)S(1)}, u32[]{:S(2)}, u32[]{:S(2)}) collective-permute-start(bf16[1,4,32,512]{3,2,1,0:T(8,128)(2,1)S(1)} %maximum_bitcast_fusion.1), channel_id=1, source_target_pairs={{0,24},{1,25},{2,26},{3,27},{4,28},{5,29},{6,30},{7,31},{8,16},{9,... | collective-permute-start | bytes 393224 | tf_op jit(solution)/shard_map/ppermute | solution.py:38
  43.3 4.4 %shard_map.59.refs_0_ = f32[16,128]{1,0:T(8,128)S(1)} custom-call(bf16[2048,256]{1,0:T(8,128)(2,1)S(1)} %get-tuple-element.57.turned_ref, bf16[256,2048]{1,0:T(8,128)(2,1)S(1)} %get-tuple-element.58.unit_ref.refs_2_.refs_4_), custom_call_target="tpu_custom_call" | custom-call | tf_op jit(solution)/shard_map/pallas_call | solution.py:202
  49.5 11.2 %all_to_all.15.refs_0_ = f32[32,1,8,128]{3,2,1,0:T(8,128)S(1)} all-to-all(f32[32,1,8,128]{3,2,1,0:T(8,128)S(1)} %pk.3), channel_id=1, replica_groups=mesh['batch'=4,'proto'=8] {'batch','proto'}, dimensions={0} | all-to-all | bytes 262144 | tf_op jit(solution)/shard_map/all_to_all | solution.py:397
  60.7 4.8 %shard_map.60 = (f32[16,128]{1,0:T(8,128)S(1)}, f32[16,128]{1,0:T(8,128)S(1)}) custom-call(bf16[2048,256]{1,0:T(8,128)(2,1)S(1)} %get-tuple-element.57.turned_ref, bf16[256,2048]{1,0:T(8,128)(2,1)S(1)} %get-tuple-element.58.unit_ref.refs_2_.refs_4_, f32[32,1,8,128]{3,2,1,0:T(8,128)S(1)} %all_to_all.15.refs_0_), custom_call_target="tpu_custom_call" | custom-call | tf_op jit(solution)/shard_map/pallas_call | solution.py:202
  67.9 2.6 %all-to-all-start.1 = ((f32[32,1,8,128]{3,2,1,0:T(8,128)}), f32[32,1,8,128]{3,2,1,0:T(8,128)S(1)}, u32[]{:S(2)}, u32[]{:S(2)}) async-start(f32[32,1,8,128]{3,2,1,0:T(8,128)} %pk.4), calls=%async_computation.1 | async-start | bytes 262144 | tf_op jit(solution)/shard_map/all_to_all | solution.py:397
  71.3 3.5 %shard_map.62 = (bf16[256,2048]{1,0:T(8,128)(2,1)}, f32[1,2048]{1,0:T(1,128)}) custom-call(s32[3]{0:T(128)} %copy-done.3, bf16[4,4,32,512]{3,2,1,0:T(8,128)(2,1)} %copy-done.5, bf16[4,4,32,512]{3,2,1,0:T(8,128)(2,1)} %copy-done.7), custom_call_target="tpu_custom_call" | custom-call | tf_op jit(solution)/shard_map/pallas_call | solution.py:87
  76.0 2.9 %shard_map.63.refs_1_ = f32[16,128]{1,0:T(8,128)S(1)} custom-call(bf16[2048,256]{1,0:T(8,128)(2,1)S(1)} %get-tuple-element.57.turned_ref, bf16[256,2048]{1,0:T(8,128)(2,1)S(1)} %copy-done), custom_call_target="tpu_custom_call" | custom-call | tf_op jit(solution)/shard_map/pallas_call | solution.py:202
  79.1 5.1 %shard_map.61 = (f32[16,128]{1,0:T(8,128)S(1)}, f32[16,128]{1,0:T(8,128)S(1)}, f32[1,2048]{1,0:T(1,128)S(1)}) custom-call(bf16[2048,256]{1,0:T(8,128)(2,1)S(1)} %get-tuple-element.57.turned_ref, bf16[256,2048]{1,0:T(8,128)(2,1)S(1)} %get-tuple-element.58.unit_ref.refs_2_.refs_4_, f32[32,1,8,128]{3,2,1,0:T(8,128)S(1)} %all-to-all-done.1.refs_0_, ...), custom_call_target="tpu_custom_call" | custom-call | tf_op jit(solution)/shard_map/pallas_call | solution.py:202
  86.1 15.6 %all_to_all.16.got_ref = f32[32,2,8,128]{3,2,1,0:T(8,128)S(1)} all-to-all(f32[32,2,8,128]{3,2,1,0:T(8,128)S(1)} %pk.5), channel_id=1, replica_groups=mesh['batch'=4,'proto'=8] {'batch','proto'}, dimensions={0} | all-to-all | bytes 524288 | tf_op jit(solution)/shard_map/all_to_all | solution.py:397
  102.5 3.5 %shard_map.64 = (f32[2,128,512]{2,1,0:T(8,128)S(1)}, f32[2048,256]{1,0:T(8,128)S(1)}, f32[8,256]{1,0:T(8,128)S(1)}) custom-call(s32[3]{0:T(128)S(1)} %copy-done.4, bf16[2048,256]{1,0:T(8,128)(2,1)S(1)} %get-tuple-element.57.turned_ref, bf16[256,2048]{1,0:T(8,128)(2,1)S(1)} %get-tuple-element.65.protos_ref, f32[2048,128]{1,0:T(8,128)S(1)} %get-tuple-element.66.inverse_ref, ...), custom_call_target="tpu_custom_call" | custom-call | tf_op jit(solution)/shard_map/pallas_call | solution.py:299
  106.8 3.6 %shard_map.65 = (f32[2,128,512]{2,1,0:T(8,128)S(1)}, f32[2048,256]{1,0:T(8,128)S(1)}, f32[8,256]{1,0:T(8,128)S(1)}) custom-call(s32[3]{0:T(128)S(1)} %copy-done.4, bf16[2048,256]{1,0:T(8,128)(2,1)S(1)} %get-tuple-element.57.turned_ref, bf16[256,2048]{1,0:T(8,128)(2,1)S(1)} %get-tuple-element.65.protos_ref, f32[2048,128]{1,0:T(8,128)S(1)} %get-tuple-element.66.inverse_ref, ...), custom_call_target="tpu_custom_call" | custom-call | tf_op jit(solution)/shard_map/pallas_call | solution.py:299
  110.5 3.6 %shard_map.66 = (f32[2,128,512]{2,1,0:T(8,128)S(1)}, f32[2048,256]{1,0:T(8,128)S(1)}, f32[8,256]{1,0:T(8,128)S(1)}) custom-call(s32[3]{0:T(128)S(1)} %copy-done.4, bf16[2048,256]{1,0:T(8,128)(2,1)S(1)} %get-tuple-element.57.turned_ref, bf16[256,2048]{1,0:T(8,128)(2,1)S(1)} %get-tuple-element.65.protos_ref, f32[2048,128]{1,0:T(8,128)S(1)} %get-tuple-element.66.inverse_ref, ...), custom_call_target="tpu_custom_call" | custom-call | tf_op jit(solution)/shard_map/pallas_call | solution.py:299
  114.8 3.9 %shard_map.67 = (f32[2,136,512]{2,1,0:T(8,128)S(1)}, f32[2048,256]{1,0:T(8,128)S(1)}, f32[8,256]{1,0:T(8,128)}) custom-call(s32[3]{0:T(128)S(1)} %copy-done.4, bf16[2048,256]{1,0:T(8,128)(2,1)S(1)} %get-tuple-element.57.turned_ref, bf16[256,2048]{1,0:T(8,128)(2,1)S(1)} %get-tuple-element.65.protos_ref, f32[2048,128]{1,0:T(8,128)S(1)} %get-tuple-element.66.inverse_ref, ...), custom_call_target="tpu_custom_call" | custom-call | tf_op jit(solution)/shard_map/pallas_call | solution.py:299
  130.7 4.7 %collective-permute-done.28 = f32[64,512]{1,0:T(8,128)S(1)} collective-permute-done((f32[64,512]{1,0:T(8,128)S(1)}, f32[64,512]{1,0:T(8,128)S(1)}, u32[]{:S(2)}, u32[]{:S(2)}) %collective-permute-start.28) | collective-permute-done | bytes 131104 | tf_op jit(solution)/shard_map/ppermute | solution.py:38
  135.5 3.0 %collective-permute-done.25 = f32[72,512]{1,0:T(8,128)S(1)} collective-permute-done((f32[72,512]{1,0:T(8,128)S(1)}, f32[72,512]{1,0:T(8,128)S(1)}, u32[]{:S(2)}, u32[]{:S(2)}) %collective-permute-start.25) | collective-permute-done | bytes 147488 | tf_op jit(solution)/shard_map/ppermute | solution.py:38
  140.1 2.4 %collective-permute-start.20 = (f16[64,2176]{1,0:T(8,128)(2,1)S(1)}, f16[64,2176]{1,0:T(8,128)(2,1)S(1)}, u32[]{:S(2)}, u32[]{:S(2)}) collective-permute-start(f16[64,2176]{1,0:T(8,128)(2,1)S(1)} %get-tuple-element.141), channel_id=1, source_target_pairs={{0,24},{1,25},{2,26},{3,27},{4,28},{5,29},{6,30},{7,31},{8,16},{9,... | collective-permute-start | bytes 835592 | tf_op jit(solution)/shard_map/ppermute | solution.py:38
  144.4 4.0 %collective-permute-done.18 = f16[64,2176]{1,0:T(8,128)(2,1)S(1)} collective-permute-done((f16[64,2176]{1,0:T(8,128)(2,1)S(1)}, f16[64,2176]{1,0:T(8,128)(2,1)S(1)}, u32[]{:S(2)}, u32[]{:S(2)}) %collective-permute-start.18) | collective-permute-done | bytes 278560 | tf_op jit(solution)/shard_map/ppermute | solution.py:38
  148.4 5.1 %collective-permute-done.19 = f16[64,2176]{1,0:T(8,128)(2,1)S(1)} collective-permute-done((f16[64,2176]{1,0:T(8,128)(2,1)S(1)}, f16[64,2176]{1,0:T(8,128)(2,1)S(1)}, u32[]{:S(2)}, u32[]{:S(2)}) %collective-permute-start.19) | collective-permute-done | bytes 278560 | tf_op jit(solution)/shard_map/ppermute | solution.py:38
  (134 shorter events, 49.3 us)
Async XLA Ops:
  4.6 7.3 %collective-permute-start.4 = (bf16[2,32,512]{2,1,0:T(8,128)(2,1)S(1)}, bf16[2,32,512]{2,1,0:T(8,128)(2,1)S(1)}, u32[]{:S(2)}, u32[]{:S(2)}) collective-permute-start(bf16[2,32,512]{2,1,0:T(8,128)(2,1)S(1)} %pad_maximum_fusion.14), channel_id=1, source_target_pairs={{0,4},{1,5},{2,6},{3,7},{4,0},{5,1},{6,2},{7,3},{8,12},{9,13},{10,... | collective-permute-start | bytes 196616 | tf_op jit(solution)/shard_map/ppermute | solution.py:38
  7.2 6.1 %collective-permute-start.5 = (bf16[2,32,512]{2,1,0:T(8,128)(2,1)S(1)}, bf16[2,32,512]{2,1,0:T(8,128)(2,1)S(1)}, u32[]{:S(2)}, u32[]{:S(2)}) collective-permute-start(bf16[2,32,512]{2,1,0:T(8,128)(2,1)S(1)} %pad_maximum_fusion.14), channel_id=1, source_target_pairs={{0,6},{1,7},{2,4},{3,5},{4,2},{5,3},{6,0},{7,1},{8,14},{9,15},{10,... | collective-permute-start | bytes 196616 | tf_op jit(solution)/shard_map/ppermute | solution.py:38
  23.1 18.0 %collective-permute-start.9 = (bf16[4,4,32,512]{3,2,1,0:T(8,128)(2,1)S(1)}, bf16[4,4,32,512]{3,2,1,0:T(8,128)(2,1)S(1)}, u32[]{:S(2)}, u32[]{:S(2)}) collective-permute-start(bf16[4,4,32,512]{3,2,1,0:T(8,128)(2,1)S(1)} %pad_maximum_fusion.refs_0_), channel_id=1, source_target_pairs={{0,1},{1,0},{2,3},{3,2},{4,5},{5,4},{6,7},{7,6},{8,9},{9,8},{10,11... | collective-permute-start | bytes 1572872 | tf_op jit(solution)/shard_map/ppermute | solution.py:38
  23.3 9.2 %collective-permute-start = (bf16[64,2048]{1,0:T(8,128)(2,1)S(1)}, bf16[64,2048]{1,0:T(8,128)(2,1)S(1)}, u32[]{:S(2)}, u32[]{:S(2)}) collective-permute-start(bf16[64,2048]{1,0:T(8,128)(2,1)S(1)} %get-tuple-element.115), channel_id=1, source_target_pairs={{0,8},{1,9},{2,10},{3,11},{4,12},{5,13},{6,14},{7,15},{8,0},{9,1},... | collective-permute-start | bytes 786440 | tf_op jit(solution)/shard_map/ppermute | solution.py:38
  23.9 9.4 %collective-permute-start.1 = (bf16[64,2048]{1,0:T(8,128)(2,1)S(1)}, bf16[64,2048]{1,0:T(8,128)(2,1)S(1)}, u32[]{:S(2)}, u32[]{:S(2)}) collective-permute-start(bf16[64,2048]{1,0:T(8,128)(2,1)S(1)} %get-tuple-element.114), channel_id=1, source_target_pairs={{0,16},{1,17},{2,18},{3,19},{4,20},{5,21},{6,22},{7,23},{8,24},{9,... | collective-permute-start | bytes 786440 | tf_op jit(solution)/shard_map/ppermute | solution.py:38
  24.4 15.6 %collective-permute-start.2 = (bf16[64,2048]{1,0:T(8,128)(2,1)S(1)}, bf16[64,2048]{1,0:T(8,128)(2,1)S(1)}, u32[]{:S(2)}, u32[]{:S(2)}) collective-permute-start(bf16[64,2048]{1,0:T(8,128)(2,1)S(1)} %get-tuple-element.113), channel_id=1, source_target_pairs={{0,24},{1,25},{2,26},{3,27},{4,28},{5,29},{6,30},{7,31},{8,16},{9,... | collective-permute-start | bytes 786440 | tf_op jit(solution)/shard_map/ppermute | solution.py:38
  26.9 20.9 %collective-permute-start.12 = (bf16[1,4,32,512]{3,2,1,0:T(8,128)(2,1)S(1)}, bf16[1,4,32,512]{3,2,1,0:T(8,128)(2,1)S(1)}, u32[]{:S(2)}, u32[]{:S(2)}) collective-permute-start(bf16[1,4,32,512]{3,2,1,0:T(8,128)(2,1)S(1)} %maximum_bitcast_fusion.1), channel_id=1, source_target_pairs={{0,8},{1,9},{2,10},{3,11},{4,12},{5,13},{6,14},{7,15},{8,0},{9,1},... | collective-permute-start | bytes 393224 | tf_op jit(solution)/shard_map/ppermute | solution.py:38
  32.5 15.3 %collective-permute-start.13 = (bf16[1,4,32,512]{3,2,1,0:T(8,128)(2,1)S(1)}, bf16[1,4,32,512]{3,2,1,0:T(8,128)(2,1)S(1)}, u32[]{:S(2)}, u32[]{:S(2)}) collective-permute-start(bf16[1,4,32,512]{3,2,1,0:T(8,128)(2,1)S(1)} %maximum_bitcast_fusion.1), channel_id=1, source_target_pairs={{0,16},{1,17},{2,18},{3,19},{4,20},{5,21},{6,22},{7,23},{8,24},{9,... | collective-permute-start | bytes 393224 | tf_op jit(solution)/shard_map/ppermute | solution.py:38
  33.3 14.5 %collective-permute-start.14 = (bf16[1,4,32,512]{3,2,1,0:T(8,128)(2,1)S(1)}, bf16[1,4,32,512]{3,2,1,0:T(8,128)(2,1)S(1)}, u32[]{:S(2)}, u32[]{:S(2)}) collective-permute-start(bf16[1,4,32,512]{3,2,1,0:T(8,128)(2,1)S(1)} %maximum_bitcast_fusion.1), channel_id=1, source_target_pairs={{0,24},{1,25},{2,26},{3,27},{4,28},{5,29},{6,30},{7,31},{8,16},{9,... | collective-permute-start | bytes 393224 | tf_op jit(solution)/shard_map/ppermute | solution.py:38
  47.9 22.6 %collective-permute-start.15 = (bf16[4,4,32,512]{3,2,1,0:T(8,128)(2,1)S(1)}, bf16[4,4,32,512]{3,2,1,0:T(8,128)(2,1)S(1)}, u32[]{:S(2)}, u32[]{:S(2)}) collective-permute-start(bf16[4,4,32,512]{3,2,1,0:T(8,128)(2,1)S(1)} %pad_maximum_fusion.1.refs_0_), channel_id=1, source_target_pairs={{0,1},{1,0},{2,3},{3,2},{4,5},{5,4},{6,7},{7,6},{8,9},{9,8},{10,11... | collective-permute-start | bytes 1572872 | tf_op jit(solution)/shard_map/ppermute | solution.py:38
  67.9 11.2 %all-to-all-start.1 = ((f32[32,1,8,128]{3,2,1,0:T(8,128)}), f32[32,1,8,128]{3,2,1,0:T(8,128)S(1)}, u32[]{:S(2)}, u32[]{:S(2)}) async-start(f32[32,1,8,128]{3,2,1,0:T(8,128)} %pk.4), calls=%async_computation.1 | async-start | bytes 262144 | tf_op jit(solution)/shard_map/all_to_all | solution.py:397
  106.0 14.7 %collective-permute-start.21 = (f32[128,512]{1,0:T(8,128)S(1)}, f32[128,512]{1,0:T(8,128)S(1)}, u32[]{:S(2)}, u32[]{:S(2)}) collective-permute-start(f32[128,512]{1,0:T(8,128)S(1)} %slice_bitcast_fusion.4), channel_id=1, source_target_pairs={{0,1},{1,0},{2,3},{3,2},{4,5},{5,4},{6,7},{7,6},{8,9},{9,8},{10,11... | collective-permute-start | bytes 786440 | tf_op jit(solution)/shard_map/ppermute | solution.py:38
  114.2 7.3 %collective-permute-start.30 = (f32[128,512]{1,0:T(8,128)S(1)}, f32[128,512]{1,0:T(8,128)S(1)}, u32[]{:S(2)}, u32[]{:S(2)}) collective-permute-start(f32[128,512]{1,0:T(8,128)S(1)} %slice_bitcast_fusion.2), channel_id=1, source_target_pairs={{0,1},{1,0},{2,3},{3,2},{4,5},{5,4},{6,7},{7,6},{8,9},{9,8},{10,11... | collective-permute-start | bytes 786440 | tf_op jit(solution)/shard_map/ppermute | solution.py:38
  114.3 8.8 %collective-permute-start.27 = (f32[128,512]{1,0:T(8,128)S(1)}, f32[128,512]{1,0:T(8,128)S(1)}, u32[]{:S(2)}, u32[]{:S(2)}) collective-permute-start(f32[128,512]{1,0:T(8,128)S(1)} %slice_bitcast_fusion.3), channel_id=1, source_target_pairs={{0,1},{1,0},{2,3},{3,2},{4,5},{5,4},{6,7},{7,6},{8,9},{9,8},{10,11... | collective-permute-start | bytes 786440 | tf_op jit(solution)/shard_map/ppermute | solution.py:38
  120.9 6.4 %collective-permute-start.22 = (f32[64,512]{1,0:T(8,128)S(1)}, f32[64,512]{1,0:T(8,128)S(1)}, u32[]{:S(2)}, u32[]{:S(2)}) collective-permute-start(f32[64,512]{1,0:T(8,128)S(1)} %pad_maximum_fusion.10), channel_id=1, source_target_pairs={{0,2},{1,3},{2,0},{3,1},{4,6},{5,7},{6,4},{7,5},{8,10},{9,11},{10,... | collective-permute-start | bytes 393224 | tf_op jit(solution)/shard_map/ppermute | solution.py:38
  121.5 8.6 %collective-permute-start.31 = (f32[64,512]{1,0:T(8,128)S(1)}, f32[64,512]{1,0:T(8,128)S(1)}, u32[]{:S(2)}, u32[]{:S(2)}) collective-permute-start(f32[64,512]{1,0:T(8,128)S(1)} %pad_maximum_fusion.12), channel_id=1, source_target_pairs={{0,2},{1,3},{2,0},{3,1},{4,6},{5,7},{6,4},{7,5},{8,10},{9,11},{10,... | collective-permute-start | bytes 393224 | tf_op jit(solution)/shard_map/ppermute | solution.py:38
  123.2 12.2 %collective-permute-start.28 = (f32[64,512]{1,0:T(8,128)S(1)}, f32[64,512]{1,0:T(8,128)S(1)}, u32[]{:S(2)}, u32[]{:S(2)}) collective-permute-start(f32[64,512]{1,0:T(8,128)S(1)} %pad_maximum_fusion.11), channel_id=1, source_target_pairs={{0,2},{1,3},{2,0},{3,1},{4,6},{5,7},{6,4},{7,5},{8,10},{9,11},{10,... | collective-permute-start | bytes 393224 | tf_op jit(solution)/shard_map/ppermute | solution.py:38
  123.8 14.6 %collective-permute-start.25 = (f32[72,512]{1,0:T(8,128)S(1)}, f32[72,512]{1,0:T(8,128)S(1)}, u32[]{:S(2)}, u32[]{:S(2)}) collective-permute-start(f32[72,512]{1,0:T(8,128)S(1)} %pad_maximum_fusion.9), channel_id=1, source_target_pairs={{0,2},{1,3},{2,0},{3,1},{4,6},{5,7},{6,4},{7,5},{8,10},{9,11},{10,... | collective-permute-start | bytes 442376 | tf_op jit(solution)/shard_map/ppermute | solution.py:38
  127.3 12.4 %collective-permute-start.23 = (f32[32,512]{1,0:T(8,128)S(1)}, f32[32,512]{1,0:T(8,128)S(1)}, u32[]{:S(2)}, u32[]{:S(2)}) collective-permute-start(f32[32,512]{1,0:T(8,128)S(1)} %get-tuple-element.82), channel_id=1, source_target_pairs={{0,4},{1,5},{2,6},{3,7},{4,0},{5,1},{6,2},{7,3},{8,12},{9,13},{10,... | collective-permute-start | bytes 196616 | tf_op jit(solution)/shard_map/ppermute | solution.py:38
  130.2 9.9 %collective-permute-start.32 = (f32[32,512]{1,0:T(8,128)S(1)}, f32[32,512]{1,0:T(8,128)S(1)}, u32[]{:S(2)}, u32[]{:S(2)}) collective-permute-start(f32[32,512]{1,0:T(8,128)S(1)} %get-tuple-element.95), channel_id=1, source_target_pairs={{0,4},{1,5},{2,6},{3,7},{4,0},{5,1},{6,2},{7,3},{8,12},{9,13},{10,... | collective-permute-start | bytes 196616 | tf_op jit(solution)/shard_map/ppermute | solution.py:38
  135.4 7.1 %collective-permute-start.29 = (f32[32,512]{1,0:T(8,128)S(1)}, f32[32,512]{1,0:T(8,128)S(1)}, u32[]{:S(2)}, u32[]{:S(2)}) collective-permute-start(f32[32,512]{1,0:T(8,128)S(1)} %get-tuple-element.91), channel_id=1, source_target_pairs={{0,4},{1,5},{2,6},{3,7},{4,0},{5,1},{6,2},{7,3},{8,12},{9,13},{10,... | collective-permute-start | bytes 196616 | tf_op jit(solution)/shard_map/ppermute | solution.py:38
  138.8 9.6 %collective-permute-start.18 = (f16[64,2176]{1,0:T(8,128)(2,1)S(1)}, f16[64,2176]{1,0:T(8,128)(2,1)S(1)}, u32[]{:S(2)}, u32[]{:S(2)}) collective-permute-start(f16[64,2176]{1,0:T(8,128)(2,1)S(1)} %get-tuple-element.143), channel_id=1, source_target_pairs={{0,8},{1,9},{2,10},{3,11},{4,12},{5,13},{6,14},{7,15},{8,0},{9,1},... | collective-permute-start | bytes 835592 | tf_op jit(solution)/shard_map/ppermute | solution.py:38
  139.7 13.8 %collective-permute-start.19 = (f16[64,2176]{1,0:T(8,128)(2,1)S(1)}, f16[64,2176]{1,0:T(8,128)(2,1)S(1)}, u32[]{:S(2)}, u32[]{:S(2)}) collective-permute-start(f16[64,2176]{1,0:T(8,128)(2,1)S(1)} %get-tuple-element.142), channel_id=1, source_target_pairs={{0,16},{1,17},{2,18},{3,19},{4,20},{5,21},{6,22},{7,23},{8,24},{9,... | collective-permute-start | bytes 835592 | tf_op jit(solution)/shard_map/ppermute | solution.py:38
  140.1 13.5 %collective-permute-start.20 = (f16[64,2176]{1,0:T(8,128)(2,1)S(1)}, f16[64,2176]{1,0:T(8,128)(2,1)S(1)}, u32[]{:S(2)}, u32[]{:S(2)}) collective-permute-start(f16[64,2176]{1,0:T(8,128)(2,1)S(1)} %get-tuple-element.141), channel_id=1, source_target_pairs={{0,24},{1,25},{2,26},{3,27},{4,28},{5,29},{6,30},{7,31},{8,16},{9,... | collective-permute-start | bytes 835592 | tf_op jit(solution)/shard_map/ppermute | solution.py:38
  (22 other events, 237.6 us)

commit v6 on v5

--- a/solution.py
+++ b/solution.py
@@ -169,7 +169,7 @@
     else:
         sums_ref, total = refs
     protos = turned_ref.shape[0]
-    step = min(512, protos)
+    step = min(1024, protos)
     total[...] = jnp.zeros_like(total)
 
     def block(i, carry):
@@ -468,7 +468,7 @@
     turned, proto_scale = unit_protos(at, blocks)
     found = gather_crops(teacher_emb, student_emb)
     teacher = unit_crops(at, found[0], width, crops, 24)[0]
-    student, crop_unit_scale = unit_crops(at, found[1], width, crops, 60)
+    student, crop_unit_scale = unit_crops(at, found[1], width, crops, 24)
 
     (sums,) = sweep(T_GAIN, turned, teacher)
     got, crop, inv = sum_everywhere(at, sums), None, []
@@ -499,7 +499,7 @@
         for o in range(1, nb)
     ]
     got = [swap(x, o + 1, 0, 0) for o, x in enumerate(sent)]
-    got, mine = lax.optimization_barrier((got, mine))
+    got = lax.optimization_barrier((got, mine))[0]
     ready = [x.astype(jnp.float32) for x in got]
     grad_proto = place(at, [proto_parts[0]] + ready)
     outs = [mine[0]] + [swap(mine[o], o, 0, 0) for o in range(1, nb)]

time: 162 us -> 154 us (0.951)
  starting transfers between devices: 39.4 us -> 34.8 us
  Pallas kernels: 45.8 us -> 43.2 us
    ppermute x36, starting transfers between devices: 36.8 us -> 32.1 us  [swap(): return lax.ppermute(x, AXES, pairs)]
    pallas_call x2, Pallas kernels: 5.73 us -> 3.91 us  [unit_crops(): pl.pallas_call(unit_crops_body, out_shape=(jax.ShapeDtypeStruct((width, c...]
  transfers between devices with their start and end apart: 37 -> 37, of which waited for: 18 -> 21; matrix products, arithmetic and copies ran while one was open for 1% -> 1% of each run, Pallas kernels for 25% -> 25%
where the time goes in v6:
time: 154 us
  Pallas kernels  43.2 us (28%)
  waiting for transfers between devices  42.9 us (28%)
  starting transfers between devices  34.8 us (23%)
  blocking collectives  25.7 us (17%)
  local copies, waits for them, and re-layouts  3.18 us (2%)
  other arithmetic  2.72 us (2%)
    ppermute x36, waiting for transfers between devices, swap(): return lax.ppermute(x, AXES, pairs)  42.2 us
    ppermute x36, starting transfers between devices, swap(): return lax.ppermute(x, AXES, pairs)  32.1 us
    all_to_all x2, blocking collectives, sum_everywhere(): return lax.all_to_all(sent, AXES, 0, 0)  25.7 us
    pallas_call x4, Pallas kernels, sweep(): pl.pallas_call(functools.partial(sweep_body, gain, weigh, before is not N...  16.4 us
    pallas_call x4, Pallas kernels, gradients(): pl.pallas_call(functools.partial(grads_body, (nz, group * blocks, blocks,...  14.6 us
    pallas_call x2, Pallas kernels, unit_crops(): pl.pallas_call(unit_crops_body, out_shape=(jax.ShapeDtypeStruct((width, c...  3.91 us
  transfers between devices with their start and end apart: 37, of which 21 were waited for; matrix products, arithmetic and copies ran while one was open for 1% of the time, Pallas kernels for 25%

profile of v6, /device:TPU:0, one launch (start us, length us, event | category | flops | bytes accessed | tf_op | source)
XLA Modules:
  0.0 153.8 jit_solution(12427835332561902199)
XLA Ops:
  1.5 5.1 %collective-permute-start.5 = (bf16[2,32,512]{2,1,0:T(8,128)(2,1)S(1)}, bf16[2,32,512]{2,1,0:T(8,128)(2,1)S(1)}, u32[]{:S(2)}, u32[]{:S(2)}) collective-permute-start(bf16[2,32,512]{2,1,0:T(8,128)(2,1)S(1)} %pad_maximum_fusion.10), channel_id=1, source_target_pairs={{0,6},{1,7},{2,4},{3,5},{4,2},{5,3},{6,0},{7,1},{8,14},{9,15},{10,... | collective-permute-start | bytes 196616 | tf_op jit(solution)/shard_map/ppermute | solution.py:38
  9.1 3.1 %collective-permute-done.4 = bf16[2,32,512]{2,1,0:T(8,128)(2,1)S(1)} collective-permute-done((bf16[2,32,512]{2,1,0:T(8,128)(2,1)S(1)}, bf16[2,32,512]{2,1,0:T(8,128)(2,1)S(1)}, u32[]{:S(2)}, u32[]{:S(2)}) %collective-permute-start.4) | collective-permute-done | bytes 65568 | tf_op jit(solution)/shard_map/ppermute | solution.py:38
  13.1 2.5 %collective-permute-start.8 = (bf16[1,4,32,512]{3,2,1,0:T(8,128)(2,1)S(1)}, bf16[1,4,32,512]{3,2,1,0:T(8,128)(2,1)S(1)}, u32[]{:S(2)}, u32[]{:S(2)}) collective-permute-start(bf16[1,4,32,512]{3,2,1,0:T(8,128)(2,1)S(1)} %maximum_bitcast_fusion), channel_id=1, source_target_pairs={{0,24},{1,25},{2,26},{3,27},{4,28},{5,29},{6,30},{7,31},{8,16},{9,... | collective-permute-start | bytes 393224 | tf_op jit(solution)/shard_map/ppermute | solution.py:38
  16.7 2.8 %collective-permute-done.8 = bf16[1,4,32,512]{3,2,1,0:T(8,128)(2,1)S(1)} collective-permute-done((bf16[1,4,32,512]{3,2,1,0:T(8,128)(2,1)S(1)}, bf16[1,4,32,512]{3,2,1,0:T(8,128)(2,1)S(1)}, u32[]{:S(2)}, u32[]{:S(2)}) %collective-permute-start.8) | collective-permute-done | bytes 131104 | tf_op jit(solution)/shard_map/ppermute | solution.py:38
  19.5 2.4 %collective-permute-done.7 = bf16[1,4,32,512]{3,2,1,0:T(8,128)(2,1)S(1)} collective-permute-done((bf16[1,4,32,512]{3,2,1,0:T(8,128)(2,1)S(1)}, bf16[1,4,32,512]{3,2,1,0:T(8,128)(2,1)S(1)}, u32[]{:S(2)}, u32[]{:S(2)}) %collective-permute-start.7) | collective-permute-done | bytes 131104 | tf_op jit(solution)/shard_map/ppermute | solution.py:38
  27.6 5.0 %collective-permute-done.2.refs_3_ = bf16[64,2048]{1,0:T(8,128)(2,1)S(1)} collective-permute-done((bf16[64,2048]{1,0:T(8,128)(2,1)S(1)}, bf16[64,2048]{1,0:T(8,128)(2,1)S(1)}, u32[]{:S(2)}, u32[]{:S(2)}) %collective-permute-start.2) | collective-permute-done | bytes 262176 | tf_op jit(solution)/shard_map/ppermute | solution.py:38
  34.0 4.2 %collective-permute-done.1.refs_2_ = bf16[64,2048]{1,0:T(8,128)(2,1)S(1)} collective-permute-done((bf16[64,2048]{1,0:T(8,128)(2,1)S(1)}, bf16[64,2048]{1,0:T(8,128)(2,1)S(1)}, u32[]{:S(2)}, u32[]{:S(2)}) %collective-permute-start.1) | collective-permute-done | bytes 262176 | tf_op jit(solution)/shard_map/ppermute | solution.py:38
  40.8 2.3 %shard_map.58 = (bf16[256,2048]{1,0:T(8,128)(2,1)S(1)}, f32[1,2048]{1,0:T(1,128)}) custom-call(s32[3]{0:T(128)S(1)} %pad_add_fusion.at_ref, bf16[4,4,32,512]{3,2,1,0:T(8,128)(2,1)S(1)} %pad_maximum_fusion.refs_0_, bf16[4,4,32,512]{3,2,1,0:T(8,128)(2,1)S(1)} %collective-permute-done.9.refs_1_), custom_call_target="tpu_custom_call" | custom-call | tf_op jit(solution)/shard_map/pallas_call | solution.py:87
  43.0 4.2 %shard_map.59.refs_0_ = f32[16,128]{1,0:T(8,128)S(1)} custom-call(bf16[2048,256]{1,0:T(8,128)(2,1)S(1)} %get-tuple-element.53.turned_ref, bf16[256,2048]{1,0:T(8,128)(2,1)S(1)} %get-tuple-element.54.unit_ref.refs_2_.refs_4_), custom_call_target="tpu_custom_call" | custom-call | tf_op jit(solution)/shard_map/pallas_call | solution.py:202
  49.0 10.9 %all_to_all.15.refs_0_ = f32[32,1,8,128]{3,2,1,0:T(8,128)S(1)} all-to-all(f32[32,1,8,128]{3,2,1,0:T(8,128)S(1)} %pk.3), channel_id=1, replica_groups=mesh['batch'=4,'proto'=8] {'batch','proto'}, dimensions={0} | all-to-all | bytes 262144 | tf_op jit(solution)/shard_map/all_to_all | solution.py:397
  59.9 4.5 %shard_map.60 = (f32[16,128]{1,0:T(8,128)S(1)}, f32[16,128]{1,0:T(8,128)S(1)}) custom-call(bf16[2048,256]{1,0:T(8,128)(2,1)S(1)} %get-tuple-element.53.turned_ref, bf16[256,2048]{1,0:T(8,128)(2,1)S(1)} %get-tuple-element.54.unit_ref.refs_2_.refs_4_, f32[32,1,8,128]{3,2,1,0:T(8,128)S(1)} %all_to_all.15.refs_0_), custom_call_target="tpu_custom_call" | custom-call | tf_op jit(solution)/shard_map/pallas_call | solution.py:202
  66.9 2.7 %all-to-all-start.1 = ((f32[32,1,8,128]{3,2,1,0:T(8,128)}), f32[32,1,8,128]{3,2,1,0:T(8,128)S(1)}, u32[]{:S(2)}, u32[]{:S(2)}) async-start(f32[32,1,8,128]{3,2,1,0:T(8,128)} %pk.4), calls=%async_computation.1 | async-start | bytes 262144 | tf_op jit(solution)/shard_map/all_to_all | solution.py:397
  74.2 2.5 %shard_map.63.refs_1_ = f32[16,128]{1,0:T(8,128)S(1)} custom-call(bf16[2048,256]{1,0:T(8,128)(2,1)S(1)} %get-tuple-element.53.turned_ref, bf16[256,2048]{1,0:T(8,128)(2,1)S(1)} %get-tuple-element.59.unit_ref.refs_3_.refs_5_), custom_call_target="tpu_custom_call" | custom-call | tf_op jit(solution)/shard_map/pallas_call | solution.py:202
  77.6 5.1 %shard_map.61 = (f32[16,128]{1,0:T(8,128)S(1)}, f32[16,128]{1,0:T(8,128)S(1)}, f32[1,2048]{1,0:T(1,128)S(1)}) custom-call(bf16[2048,256]{1,0:T(8,128)(2,1)S(1)} %get-tuple-element.53.turned_ref, bf16[256,2048]{1,0:T(8,128)(2,1)S(1)} %get-tuple-element.54.unit_ref.refs_2_.refs_4_, f32[32,1,8,128]{3,2,1,0:T(8,128)S(1)} %all-to-all-done.1.refs_0_, ...), custom_call_target="tpu_custom_call" | custom-call | tf_op jit(solution)/shard_map/pallas_call | solution.py:202
  84.6 14.8 %all_to_all.16.got_ref = f32[32,2,8,128]{3,2,1,0:T(8,128)S(1)} all-to-all(f32[32,2,8,128]{3,2,1,0:T(8,128)S(1)} %pk.5), channel_id=1, replica_groups=mesh['batch'=4,'proto'=8] {'batch','proto'}, dimensions={0} | all-to-all | bytes 524288 | tf_op jit(solution)/shard_map/all_to_all | solution.py:397
  100.1 3.5 %shard_map.64 = (f32[2,128,512]{2,1,0:T(8,128)S(1)}, f32[2048,256]{1,0:T(8,128)S(1)}, f32[8,256]{1,0:T(8,128)S(1)}) custom-call(s32[3]{0:T(128)S(1)} %pad_add_fusion.at_ref, bf16[2048,256]{1,0:T(8,128)(2,1)S(1)} %get-tuple-element.53.turned_ref, bf16[256,2048]{1,0:T(8,128)(2,1)S(1)} %get-tuple-element.61.protos_ref, ...), custom_call_target="tpu_custom_call" | custom-call | tf_op jit(solution)/shard_map/pallas_call | solution.py:299
  104.5 3.6 %shard_map.65 = (f32[2,128,512]{2,1,0:T(8,128)S(1)}, f32[2048,256]{1,0:T(8,128)S(1)}, f32[8,256]{1,0:T(8,128)S(1)}) custom-call(s32[3]{0:T(128)S(1)} %pad_add_fusion.at_ref, bf16[2048,256]{1,0:T(8,128)(2,1)S(1)} %get-tuple-element.53.turned_ref, bf16[256,2048]{1,0:T(8,128)(2,1)S(1)} %get-tuple-element.61.protos_ref, ...), custom_call_target="tpu_custom_call" | custom-call | tf_op jit(solution)/shard_map/pallas_call | solution.py:299
  108.3 3.6 %shard_map.66 = (f32[2,128,512]{2,1,0:T(8,128)S(1)}, f32[2048,256]{1,0:T(8,128)S(1)}, f32[8,256]{1,0:T(8,128)S(1)}) custom-call(s32[3]{0:T(128)S(1)} %pad_add_fusion.at_ref, bf16[2048,256]{1,0:T(8,128)(2,1)S(1)} %get-tuple-element.53.turned_ref, bf16[256,2048]{1,0:T(8,128)(2,1)S(1)} %get-tuple-element.61.protos_ref, ...), custom_call_target="tpu_custom_call" | custom-call | tf_op jit(solution)/shard_map/pallas_call | solution.py:299
  111.9 3.9 %shard_map.67 = (f32[2,136,512]{2,1,0:T(8,128)S(1)}, f32[2048,256]{1,0:T(8,128)S(1)}, f32[8,256]{1,0:T(8,128)}) custom-call(s32[3]{0:T(128)S(1)} %pad_add_fusion.at_ref, bf16[2048,256]{1,0:T(8,128)(2,1)S(1)} %get-tuple-element.53.turned_ref, bf16[256,2048]{1,0:T(8,128)(2,1)S(1)} %get-tuple-element.61.protos_ref, ...), custom_call_target="tpu_custom_call" | custom-call | tf_op jit(solution)/shard_map/pallas_call | solution.py:299
  123.8 3.7 %collective-permute-done.22 = f32[64,512]{1,0:T(8,128)S(1)} collective-permute-done((f32[64,512]{1,0:T(8,128)S(1)}, f32[64,512]{1,0:T(8,128)S(1)}, u32[]{:S(2)}, u32[]{:S(2)}) %collective-permute-start.22) | collective-permute-done | bytes 131104 | tf_op jit(solution)/shard_map/ppermute | solution.py:38
  127.7 2.6 %collective-permute-done.28 = f32[64,512]{1,0:T(8,128)S(1)} collective-permute-done((f32[64,512]{1,0:T(8,128)S(1)}, f32[64,512]{1,0:T(8,128)S(1)}, u32[]{:S(2)}, u32[]{:S(2)}) %collective-permute-start.28) | collective-permute-done | bytes 131104 | tf_op jit(solution)/shard_map/ppermute | solution.py:38
  131.2 2.6 %collective-permute-done.31 = f32[64,512]{1,0:T(8,128)S(1)} collective-permute-done((f32[64,512]{1,0:T(8,128)S(1)}, f32[64,512]{1,0:T(8,128)S(1)}, u32[]{:S(2)}, u32[]{:S(2)}) %collective-permute-start.31) | collective-permute-done | bytes 131104 | tf_op jit(solution)/shard_map/ppermute | solution.py:38
  134.1 3.0 %collective-permute-done.25 = f32[72,512]{1,0:T(8,128)S(1)} collective-permute-done((f32[72,512]{1,0:T(8,128)S(1)}, f32[72,512]{1,0:T(8,128)S(1)}, u32[]{:S(2)}, u32[]{:S(2)}) %collective-permute-start.25) | collective-permute-done | bytes 147488 | tf_op jit(solution)/shard_map/ppermute | solution.py:38
  143.0 3.2 %collective-permute-done.26 = f32[40,512]{1,0:T(8,128)S(1)} collective-permute-done((f32[40,512]{1,0:T(8,128)S(1)}, f32[40,512]{1,0:T(8,128)S(1)}, u32[]{:S(2)}, u32[]{:S(2)}) %collective-permute-start.26) | collective-permute-done | bytes 81952 | tf_op jit(solution)/shard_map/ppermute | solution.py:38
  (130 shorter events, 50.6 us)
Async XLA Ops:
  1.5 7.6 %collective-permute-start.5 = (bf16[2,32,512]{2,1,0:T(8,128)(2,1)S(1)}, bf16[2,32,512]{2,1,0:T(8,128)(2,1)S(1)}, u32[]{:S(2)}, u32[]{:S(2)}) collective-permute-start(bf16[2,32,512]{2,1,0:T(8,128)(2,1)S(1)} %pad_maximum_fusion.10), channel_id=1, source_target_pairs={{0,6},{1,7},{2,4},{3,5},{4,2},{5,3},{6,0},{7,1},{8,14},{9,15},{10,... | collective-permute-start | bytes 196616 | tf_op jit(solution)/shard_map/ppermute | solution.py:38
  13.1 6.4 %collective-permute-start.8 = (bf16[1,4,32,512]{3,2,1,0:T(8,128)(2,1)S(1)}, bf16[1,4,32,512]{3,2,1,0:T(8,128)(2,1)S(1)}, u32[]{:S(2)}, u32[]{:S(2)}) collective-permute-start(bf16[1,4,32,512]{3,2,1,0:T(8,128)(2,1)S(1)} %maximum_bitcast_fusion), channel_id=1, source_target_pairs={{0,24},{1,25},{2,26},{3,27},{4,28},{5,29},{6,30},{7,31},{8,16},{9,... | collective-permute-start | bytes 393224 | tf_op jit(solution)/shard_map/ppermute | solution.py:38
  15.6 6.3 %collective-permute-start.7 = (bf16[1,4,32,512]{3,2,1,0:T(8,128)(2,1)S(1)}, bf16[1,4,32,512]{3,2,1,0:T(8,128)(2,1)S(1)}, u32[]{:S(2)}, u32[]{:S(2)}) collective-permute-start(bf16[1,4,32,512]{3,2,1,0:T(8,128)(2,1)S(1)} %maximum_bitcast_fusion), channel_id=1, source_target_pairs={{0,16},{1,17},{2,18},{3,19},{4,20},{5,21},{6,22},{7,23},{8,24},{9,... | collective-permute-start | bytes 393224 | tf_op jit(solution)/shard_map/ppermute | solution.py:38
  22.1 18.6 %collective-permute-start.9 = (bf16[4,4,32,512]{3,2,1,0:T(8,128)(2,1)S(1)}, bf16[4,4,32,512]{3,2,1,0:T(8,128)(2,1)S(1)}, u32[]{:S(2)}, u32[]{:S(2)}) collective-permute-start(bf16[4,4,32,512]{3,2,1,0:T(8,128)(2,1)S(1)} %pad_maximum_fusion.refs_0_), channel_id=1, source_target_pairs={{0,1},{1,0},{2,3},{3,2},{4,5},{5,4},{6,7},{7,6},{8,9},{9,8},{10,11... | collective-permute-start | bytes 1572872 | tf_op jit(solution)/shard_map/ppermute | solution.py:38
  22.3 10.2 %collective-permute-start.2 = (bf16[64,2048]{1,0:T(8,128)(2,1)S(1)}, bf16[64,2048]{1,0:T(8,128)(2,1)S(1)}, u32[]{:S(2)}, u32[]{:S(2)}) collective-permute-start(bf16[64,2048]{1,0:T(8,128)(2,1)S(1)} %get-tuple-element.105), channel_id=1, source_target_pairs={{0,24},{1,25},{2,26},{3,27},{4,28},{5,29},{6,30},{7,31},{8,16},{9,... | collective-permute-start | bytes 786440 | tf_op jit(solution)/shard_map/ppermute | solution.py:38
  24.0 14.2 %collective-permute-start.1 = (bf16[64,2048]{1,0:T(8,128)(2,1)S(1)}, bf16[64,2048]{1,0:T(8,128)(2,1)S(1)}, u32[]{:S(2)}, u32[]{:S(2)}) collective-permute-start(bf16[64,2048]{1,0:T(8,128)(2,1)S(1)} %get-tuple-element.106), channel_id=1, source_target_pairs={{0,16},{1,17},{2,18},{3,19},{4,20},{5,21},{6,22},{7,23},{8,24},{9,... | collective-permute-start | bytes 786440 | tf_op jit(solution)/shard_map/ppermute | solution.py:38
  25.4 14.3 %collective-permute-start = (bf16[64,2048]{1,0:T(8,128)(2,1)S(1)}, bf16[64,2048]{1,0:T(8,128)(2,1)S(1)}, u32[]{:S(2)}, u32[]{:S(2)}) collective-permute-start(bf16[64,2048]{1,0:T(8,128)(2,1)S(1)} %get-tuple-element.107), channel_id=1, source_target_pairs={{0,8},{1,9},{2,10},{3,11},{4,12},{5,13},{6,14},{7,15},{8,0},{9,1},... | collective-permute-start | bytes 786440 | tf_op jit(solution)/shard_map/ppermute | solution.py:38
  25.9 21.4 %collective-permute-start.14 = (bf16[1,4,32,512]{3,2,1,0:T(8,128)(2,1)S(1)}, bf16[1,4,32,512]{3,2,1,0:T(8,128)(2,1)S(1)}, u32[]{:S(2)}, u32[]{:S(2)}) collective-permute-start(bf16[1,4,32,512]{3,2,1,0:T(8,128)(2,1)S(1)} %maximum_bitcast_fusion.1), channel_id=1, source_target_pairs={{0,24},{1,25},{2,26},{3,27},{4,28},{5,29},{6,30},{7,31},{8,16},{9,... | collective-permute-start | bytes 393224 | tf_op jit(solution)/shard_map/ppermute | solution.py:38
  32.5 14.8 %collective-permute-start.13 = (bf16[1,4,32,512]{3,2,1,0:T(8,128)(2,1)S(1)}, bf16[1,4,32,512]{3,2,1,0:T(8,128)(2,1)S(1)}, u32[]{:S(2)}, u32[]{:S(2)}) collective-permute-start(bf16[1,4,32,512]{3,2,1,0:T(8,128)(2,1)S(1)} %maximum_bitcast_fusion.1), channel_id=1, source_target_pairs={{0,16},{1,17},{2,18},{3,19},{4,20},{5,21},{6,22},{7,23},{8,24},{9,... | collective-permute-start | bytes 393224 | tf_op jit(solution)/shard_map/ppermute | solution.py:38
  38.2 9.1 %collective-permute-start.12 = (bf16[1,4,32,512]{3,2,1,0:T(8,128)(2,1)S(1)}, bf16[1,4,32,512]{3,2,1,0:T(8,128)(2,1)S(1)}, u32[]{:S(2)}, u32[]{:S(2)}) collective-permute-start(bf16[1,4,32,512]{3,2,1,0:T(8,128)(2,1)S(1)} %maximum_bitcast_fusion.1), channel_id=1, source_target_pairs={{0,8},{1,9},{2,10},{3,11},{4,12},{5,13},{6,14},{7,15},{8,0},{9,1},... | collective-permute-start | bytes 393224 | tf_op jit(solution)/shard_map/ppermute | solution.py:38
  47.4 22.3 %collective-permute-start.15 = (bf16[4,4,32,512]{3,2,1,0:T(8,128)(2,1)S(1)}, bf16[4,4,32,512]{3,2,1,0:T(8,128)(2,1)S(1)}, u32[]{:S(2)}, u32[]{:S(2)}) collective-permute-start(bf16[4,4,32,512]{3,2,1,0:T(8,128)(2,1)S(1)} %pad_maximum_fusion.1.refs_0_), channel_id=1, source_target_pairs={{0,1},{1,0},{2,3},{3,2},{4,5},{5,4},{6,7},{7,6},{8,9},{9,8},{10,11... | collective-permute-start | bytes 1572872 | tf_op jit(solution)/shard_map/ppermute | solution.py:38
  66.9 10.7 %all-to-all-start.1 = ((f32[32,1,8,128]{3,2,1,0:T(8,128)}), f32[32,1,8,128]{3,2,1,0:T(8,128)S(1)}, u32[]{:S(2)}, u32[]{:S(2)}) async-start(f32[32,1,8,128]{3,2,1,0:T(8,128)} %pk.4), calls=%async_computation.1 | async-start | bytes 262144 | tf_op jit(solution)/shard_map/all_to_all | solution.py:397
  76.8 6.3 %collective-permute-start.17 = (f32[16,128]{1,0:T(8,128)S(1)}, f32[16,128]{1,0:T(8,128)S(1)}, u32[]{:S(2)}, u32[]{:S(2)}) collective-permute-start(f32[16,128]{1,0:T(8,128)S(1)} %shard_map.63.refs_1_), channel_id=1, source_target_pairs={{0,1},{1,0},{2,3},{3,2},{4,5},{5,4},{6,7},{7,6},{8,9},{9,8},{10,11... | collective-permute-start | bytes 24584 | tf_op jit(solution)/shard_map/ppermute | solution.py:38
  103.7 15.8 %collective-permute-start.21 = (f32[128,512]{1,0:T(8,128)S(1)}, f32[128,512]{1,0:T(8,128)S(1)}, u32[]{:S(2)}, u32[]{:S(2)}) collective-permute-start(f32[128,512]{1,0:T(8,128)S(1)} %slice_bitcast_fusion.4), channel_id=1, source_target_pairs={{0,1},{1,0},{2,3},{3,2},{4,5},{5,4},{6,7},{7,6},{8,9},{9,8},{10,11... | collective-permute-start | bytes 786440 | tf_op jit(solution)/shard_map/ppermute | solution.py:38
  108.2 12.9 %collective-permute-start.27 = (f32[128,512]{1,0:T(8,128)S(1)}, f32[128,512]{1,0:T(8,128)S(1)}, u32[]{:S(2)}, u32[]{:S(2)}) collective-permute-start(f32[128,512]{1,0:T(8,128)S(1)} %slice_bitcast_fusion.3), channel_id=1, source_target_pairs={{0,1},{1,0},{2,3},{3,2},{4,5},{5,4},{6,7},{7,6},{8,9},{9,8},{10,11... | collective-permute-start | bytes 786440 | tf_op jit(solution)/shard_map/ppermute | solution.py:38
  118.6 30.1 %collective-permute-start.20 = (f16[64,2176]{1,0:T(8,128)(2,1)S(1)}, f16[64,2176]{1,0:T(8,128)(2,1)S(1)}, u32[]{:S(2)}, u32[]{:S(2)}) collective-permute-start(f16[64,2176]{1,0:T(8,128)(2,1)S(1)} %get-tuple-element.133), channel_id=1, source_target_pairs={{0,24},{1,25},{2,26},{3,27},{4,28},{5,29},{6,30},{7,31},{8,16},{9,... | collective-permute-start | bytes 835592 | tf_op jit(solution)/shard_map/ppermute | solution.py:38
  119.6 30.3 %collective-permute-start.19 = (f16[64,2176]{1,0:T(8,128)(2,1)S(1)}, f16[64,2176]{1,0:T(8,128)(2,1)S(1)}, u32[]{:S(2)}, u32[]{:S(2)}) collective-permute-start(f16[64,2176]{1,0:T(8,128)(2,1)S(1)} %get-tuple-element.134), channel_id=1, source_target_pairs={{0,16},{1,17},{2,18},{3,19},{4,20},{5,21},{6,22},{7,23},{8,24},{9,... | collective-permute-start | bytes 835592 | tf_op jit(solution)/shard_map/ppermute | solution.py:38
  121.1 6.4 %collective-permute-start.22 = (f32[64,512]{1,0:T(8,128)S(1)}, f32[64,512]{1,0:T(8,128)S(1)}, u32[]{:S(2)}, u32[]{:S(2)}) collective-permute-start(f32[64,512]{1,0:T(8,128)S(1)} %pad_maximum_fusion.6), channel_id=1, source_target_pairs={{0,2},{1,3},{2,0},{3,1},{4,6},{5,7},{6,4},{7,5},{8,10},{9,11},{10,... | collective-permute-start | bytes 393224 | tf_op jit(solution)/shard_map/ppermute | solution.py:38
  121.4 8.9 %collective-permute-start.28 = (f32[64,512]{1,0:T(8,128)S(1)}, f32[64,512]{1,0:T(8,128)S(1)}, u32[]{:S(2)}, u32[]{:S(2)}) collective-permute-start(f32[64,512]{1,0:T(8,128)S(1)} %pad_maximum_fusion.7), channel_id=1, source_target_pairs={{0,2},{1,3},{2,0},{3,1},{4,6},{5,7},{6,4},{7,5},{8,10},{9,11},{10,... | collective-permute-start | bytes 393224 | tf_op jit(solution)/shard_map/ppermute | solution.py:38
  123.4 10.4 %collective-permute-start.31 = (f32[64,512]{1,0:T(8,128)S(1)}, f32[64,512]{1,0:T(8,128)S(1)}, u32[]{:S(2)}, u32[]{:S(2)}) collective-permute-start(f32[64,512]{1,0:T(8,128)S(1)} %pad_maximum_fusion.8), channel_id=1, source_target_pairs={{0,2},{1,3},{2,0},{3,1},{4,6},{5,7},{6,4},{7,5},{8,10},{9,11},{10,... | collective-permute-start | bytes 393224 | tf_op jit(solution)/shard_map/ppermute | solution.py:38
  127.5 9.5 %collective-permute-start.25 = (f32[72,512]{1,0:T(8,128)S(1)}, f32[72,512]{1,0:T(8,128)S(1)}, u32[]{:S(2)}, u32[]{:S(2)}) collective-permute-start(f32[72,512]{1,0:T(8,128)S(1)} %pad_maximum_fusion.5), channel_id=1, source_target_pairs={{0,2},{1,3},{2,0},{3,1},{4,6},{5,7},{6,4},{7,5},{8,10},{9,11},{10,... | collective-permute-start | bytes 442376 | tf_op jit(solution)/shard_map/ppermute | solution.py:38
  130.3 8.9 %collective-permute-start.23 = (f32[32,512]{1,0:T(8,128)S(1)}, f32[32,512]{1,0:T(8,128)S(1)}, u32[]{:S(2)}, u32[]{:S(2)}) collective-permute-start(f32[32,512]{1,0:T(8,128)S(1)} %get-tuple-element.78), channel_id=1, source_target_pairs={{0,4},{1,5},{2,6},{3,7},{4,0},{5,1},{6,2},{7,3},{8,12},{9,13},{10,... | collective-permute-start | bytes 196616 | tf_op jit(solution)/shard_map/ppermute | solution.py:38
  133.8 6.7 %collective-permute-start.29 = (f32[32,512]{1,0:T(8,128)S(1)}, f32[32,512]{1,0:T(8,128)S(1)}, u32[]{:S(2)}, u32[]{:S(2)}) collective-permute-start(f32[32,512]{1,0:T(8,128)S(1)} %get-tuple-element.87), channel_id=1, source_target_pairs={{0,4},{1,5},{2,6},{3,7},{4,0},{5,1},{6,2},{7,3},{8,12},{9,13},{10,... | collective-permute-start | bytes 196616 | tf_op jit(solution)/shard_map/ppermute | solution.py:38
  139.2 10.7 %collective-permute-start.18 = (f16[64,2176]{1,0:T(8,128)(2,1)S(1)}, f16[64,2176]{1,0:T(8,128)(2,1)S(1)}, u32[]{:S(2)}, u32[]{:S(2)}) collective-permute-start(f16[64,2176]{1,0:T(8,128)(2,1)S(1)} %get-tuple-element.135), channel_id=1, source_target_pairs={{0,8},{1,9},{2,10},{3,11},{4,12},{5,13},{6,14},{7,15},{8,0},{9,1},... | collective-permute-start | bytes 835592 | tf_op jit(solution)/shard_map/ppermute | solution.py:38
  (19 other events, 128.8 us)
